TPU v7x, 32 devices: a whole 2x2x4 slice. The times are simulated.
32 devices in a mesh: dp: 2 (over y), fsdp: 16 (over z, x, core).
Axes of the slice: x: 2, y: 2, z: 4, core: 2. Of those that a mesh axis runs over, the one named last changes fastest.
Arguments:
- block_input: bfloat16 [64, 512, 768], P(('dp', 'fsdp')), may hold values from -6 to 6
- segment_ids: int32 [64, 512], P(('dp', 'fsdp')), may hold values from 0 to 7, never falling along the last dimension, each value on 1 to 192 neighbouring positions
- cotangent: bfloat16 [64, 512, 768], P(('dp', 'fsdp')), may hold values from -12 to 12
- w_query: bfloat16 [768, 768], P(('dp', 'fsdp')), may hold values from -0.3125 to 0.3125
- b_query: bfloat16 [768], P(('dp', 'fsdp')), may hold values from -3 to 3
- w_key: bfloat16 [768, 768], P(('dp', 'fsdp')), may hold values from -0.3125 to 0.3125
- w_value: bfloat16 [768, 768], P(('dp', 'fsdp')), may hold values from -0.21875 to 0.21875
- b_value: bfloat16 [768], P(('dp', 'fsdp')), may hold values from -3 to 3
- w_out: bfloat16 [768, 768], P(('dp', 'fsdp')), may hold values from -1.25 to 1.25
- b_out: bfloat16 [768], P(('dp', 'fsdp')), may hold values from -3 to 3
- gain_one: bfloat16 [768], P(('dp', 'fsdp')), may hold values from 0.25 to 1.75
- shift_one: bfloat16 [768], P(('dp', 'fsdp')), may hold values from -3 to 3
- w_inner: bfloat16 [768, 3072], P(('dp', 'fsdp')), may hold values from -0.21875 to 0.21875
- b_inner: bfloat16 [3072], P(('dp', 'fsdp')), may hold values from -3 to 3
- w_outer: bfloat16 [3072, 768], P(('dp', 'fsdp')), may hold values from -0.15625 to 0.15625
- b_outer: bfloat16 [768], P(('dp', 'fsdp')), may hold values from -3 to 3
- gain_two: bfloat16 [768], P(('dp', 'fsdp')), may hold values from 0.25 to 1.75
- shift_two: bfloat16 [768], P(('dp', 'fsdp')), may hold values from -3 to 3
Outputs:
- layer_out: bfloat16 [64, 512, 768], P(('dp', 'fsdp'))
- grad_input: bfloat16 [64, 512, 768], P(('dp', 'fsdp'))
- grad_w_query: float32 [768, 768], P(('dp', 'fsdp'))
- grad_b_query: float32 [768], P(('dp', 'fsdp'))
- grad_w_key: float32 [768, 768], P(('dp', 'fsdp'))
- grad_w_value: float32 [768, 768], P(('dp', 'fsdp'))
- grad_b_value: float32 [768], P(('dp', 'fsdp'))
- grad_w_out: float32 [768, 768], P(('dp', 'fsdp'))
- grad_b_out: float32 [768], P(('dp', 'fsdp'))
- grad_gain_one: float32 [768], P(('dp', 'fsdp'))
- grad_shift_one: float32 [768], P(('dp', 'fsdp'))
- grad_w_inner: float32 [768, 3072], P(('dp', 'fsdp'))
- grad_b_inner: float32 [3072], P(('dp', 'fsdp'))
- grad_w_outer: float32 [3072, 768], P(('dp', 'fsdp'))
- grad_b_outer: float32 [768], P(('dp', 'fsdp'))
- grad_gain_two: float32 [768], P(('dp', 'fsdp'))
- grad_shift_two: float32 [768], P(('dp', 'fsdp'))
Inputs may be any that keep to these rules, and one draw needn't show every extreme that they name: `segment_ids`: along each row the numbers never fall; one document has 1 to 192 tokens, and some document has exactly 192.
All inputs are finite; a program needn't handle non-finite values.
Results may differ from a plain program's by a relative error of at most 0.015.
The roundings to bfloat16 on the way count: a program that leaves them out, or rounds other values in their place, can miss the bound.
Values may be sent and summed in bfloat16 or wider, within the bound.
No kernel may reach another device: no remote copies, remote signals or barrier semaphores. Data moves between devices by JAX's collectives and lax.ppermute only.
A program may use at most 192 MiB of HBM per device.

v0:
```python
import jax
import jax.numpy as jnp
import numpy as np
from jax import lax
from jax.experimental import pallas as pl
from jax.experimental.pallas import tpu as pltpu
from jax.sharding import Mesh, PartitionSpec as P

D = 768
FF = 3072
HEADS = 12
HEAD_DIM = 64
SEQ = 512
GROUP = 256
GROUPS = D // GROUP
TRIO = 3 * GROUP
PAIR = 128
SET = 4 * D + PAIR
KT = 256
CHUNK = 768
CHUNKS = FF // CHUNK
ROWS = 256
EPS = 1e-05
SHARE = 1.0
ROOT = 0.7978845608028654
CUBE = 0.044715
LOW = jnp.bfloat16
F32 = jnp.float32
MIB = 1 << 20
VMEM = 63 * MIB
MATRICES = (0, 2, 3, 5, 9, 11)
VECTORS = (1, 4, 6, 7, 8, 12, 13, 14, 10)
AXES = ("dp", "line", "side", "core")


def mm(a, b):
    return lax.dot_general(a, b, (((1,), (0,)), ((), ())), preferred_element_type=F32)


def mm_t(a, b):
    return lax.dot_general(a, b, (((1,), (1,)), ((), ())), preferred_element_type=F32)


def t_mm(a, b):
    return lax.dot_general(a, b, (((0,), (0,)), ((), ())), preferred_element_type=F32)


def cost(flops, moved, transcendentals):
    return pl.CostEstimate(
        flops=int(SHARE * flops),
        bytes_accessed=int(SHARE * moved),
        transcendentals=int(SHARE * transcendentals),
    )


def like(shape, kind):
    return jax.ShapeDtypeStruct(shape, kind)


def attention_forward_kernel(
    x_ref, w_ref, wout_ref, vec_ref, seg_ref,
    qkv_ref, ctx_ref, probs_ref, xt_ref, h1_ref, n1_ref, n1low_ref, n1t_ref, mask_ref,
):
    group = pl.program_id(1)
    x = x_ref[...]
    column = pl.ds(pl.multiple_of(group * GROUP, GROUP), GROUP)
    qkv_ref[:, :GROUP] = (mm(x, w_ref[:, :GROUP]) + vec_ref[0:1, column]).astype(LOW)
    qkv_ref[:, GROUP : 2 * GROUP] = mm(x, w_ref[:, GROUP : 2 * GROUP]).astype(LOW)
    qkv_ref[:, 2 * GROUP :] = (mm(x, w_ref[:, 2 * GROUP :]) + vec_ref[1:2, column]).astype(LOW)

    @pl.when(group == 0)
    def _():
        number = seg_ref[pl.ds(pl.program_id(0), 1), :].astype(F32)
        column = jnp.transpose(jnp.broadcast_to(number, (PAIR, SEQ)))[:, :1]
        mask_ref[...] = jnp.where(column == number, 0.0, -1e30)
        xt_ref[0] = jnp.transpose(x)
        h1_ref[...] = x.astype(F32) + vec_ref[2:3, :]

    lane = lax.broadcasted_iota(jnp.int32, (1, PAIR), 1)
    scale = jnp.asarray(HEAD_DIM**-0.5, LOW)
    for pair in range(GROUP // PAIR):
        q_lanes, k_lanes, v_lanes = (
            slice(part * GROUP + pair * PAIR, part * GROUP + (pair + 1) * PAIR) for part in range(3)
        )
        q_pair = qkv_ref[:, q_lanes] * scale
        v_pair = qkv_ref[:, v_lanes]
        halves = []
        for half in range(2):
            mine = (lane // HEAD_DIM) == half
            scores = mm_t(jnp.where(mine, qkv_ref[:, k_lanes], 0), q_pair) + mask_ref[...]
            weight = jnp.exp(scores - jnp.max(scores, axis=0, keepdims=True))
            total = jnp.sum(weight, axis=0, keepdims=True)
            probs = (weight * (1.0 / total)).astype(LOW)
            probs_ref[0, 0, 2 * pair + half] = probs
            halves.append(t_mm(probs, v_pair))
        ctx_ref[:, q_lanes] = jnp.where(lane < HEAD_DIM, halves[0], halves[1]).astype(LOW)
    h1_ref[...] += mm(ctx_ref[...], wout_ref[...])

    @pl.when(group == GROUPS - 1)
    def _():
        @pl.loop(0, SEQ // ROWS)
        def _(i):
            rows = pl.ds(pl.multiple_of(i * ROWS, ROWS), ROWS)
            n, _ = norm_parts(h1_ref[rows, :])
            n1 = n * vec_ref[3:4, :] + vec_ref[4:5, :]
            n1_ref[rows, :] = n1
            n1low_ref[rows, :] = n1.astype(LOW)

        n1t_ref[...] = jnp.transpose(n1low_ref[...])


def attention_forward(x, seg, weights, table):
    rows = x.shape[0]
    seqs = rows // SEQ
    row = pl.BlockSpec((SEQ, D), lambda b, g: (b, 0))
    return pl.pallas_call(
        attention_forward_kernel,
        grid=(seqs, GROUPS),
        in_specs=[
            row,
            pl.BlockSpec((D, TRIO), lambda b, g: (0, 1 + g)),
            pl.BlockSpec((GROUP, D), lambda b, g: (g, 0)),
            pl.BlockSpec((8, D), lambda b, g: (0, 0)),
            pl.BlockSpec((seqs, SEQ), lambda b, g: (0, 0)),
        ],
        out_specs=[
            pl.BlockSpec((SEQ, TRIO), lambda b, g: (b, g)),
            pl.BlockSpec((SEQ, GROUP), lambda b, g: (b, g)),
            pl.BlockSpec((1, 1, GROUP // HEAD_DIM, SEQ, SEQ), lambda b, g: (b, g, 0, 0, 0)),
            pl.BlockSpec((1, D, SEQ), lambda b, g: (b, 0, 0)),
            row,
            row,
            row,
            pl.BlockSpec((D, SEQ), lambda b, g: (0, b)),
        ],
        out_shape=[
            like((rows, 3 * D), LOW),
            like((rows, D), LOW),
            like((seqs, GROUPS, GROUP // HEAD_DIM, SEQ, SEQ), LOW),
            like((seqs, D, SEQ), LOW),
            like((rows, D), F32),
            like((rows, D), F32),
            like((rows, D), LOW),
            like((D, rows), LOW),
        ],
        scratch_shapes=[pltpu.VMEM((SEQ, SEQ), F32)],
        compiler_params=pltpu.CompilerParams(vmem_limit_bytes=VMEM),
        cost_estimate=cost(rows * (8 * D * D + 4 * D * SEQ), 36 * MIB, rows * SEQ * HEADS),
        name="attention_forward",
    )(x, weights, weights, table, seg)


def attention_backward_kernel(
    xt_ref, qkv_ref, ctx_ref, dctx_ref, probs_ref, vec_in_ref, gw_in_ref,
    gw_ref, dqkv_ref, vec_ref,
    ds_ref, acc_ref,
):
    row, seqs = pl.program_id(1), pl.num_programs(1)
    head_of = lax.broadcasted_iota(jnp.int32, (8, GROUP), 1) // HEAD_DIM
    picks = (head_of == lax.broadcasted_iota(jnp.int32, (8, GROUP), 0)).astype(F32)
    product = ctx_ref[...].astype(F32) * dctx_ref[...].astype(F32)
    inner = lax.dot_general(
        picks, product, (((1,), (1,)), ((), ())),
        preferred_element_type=F32, precision=lax.Precision.HIGHEST,
    )
    lane = lax.broadcasted_iota(jnp.int32, (1, PAIR), 1)
    first = lane < HEAD_DIM
    scale = jnp.asarray(HEAD_DIM**-0.5, LOW)
    tiles = [slice(i, i + KT) for i in range(0, SEQ, KT)]
    for pair in range(GROUP // PAIR):
        q_lanes, k_lanes, v_lanes = (
            slice(part * GROUP + pair * PAIR, part * GROUP + (pair + 1) * PAIR) for part in range(3)
        )
        q_pair = qkv_ref[:, q_lanes] * scale
        k_pair = qkv_ref[:, k_lanes] * scale
        dctx_pair = dctx_ref[:, q_lanes]
        dq, dk, dv = [], [], []
        for half in range(2):
            mine = (lane // HEAD_DIM) == half
            head = 2 * pair + half
            dk_tiles, dv_tiles = [], []
            for keys in tiles:
                probs = probs_ref[0, 0, head, keys, :]
                d_probs = mm_t(jnp.where(mine, qkv_ref[keys, v_lanes], 0), dctx_pair)
                d_scores = (probs.astype(F32) * (d_probs - inner[head : head + 1, :])).astype(LOW)
                ds_ref[half, keys, :] = d_scores
                dv_tiles.append(mm(probs, dctx_pair))
                dk_tiles.append(mm(d_scores, q_pair))
            dk.append(dk_tiles)
            dv.append(dv_tiles)
            dq.append([t_mm(ds_ref[half, :, rows], k_pair) for rows in tiles])
        for i, rows in enumerate(tiles):
            dqkv_ref[rows, q_lanes] = jnp.where(first, dq[0][i], dq[1][i]).astype(LOW)
            dqkv_ref[rows, k_lanes] = jnp.where(first, dk[0][i], dk[1][i]).astype(LOW)
            dqkv_ref[rows, v_lanes] = jnp.where(first, dv[0][i], dv[1][i]).astype(LOW)
    dqkv = dqkv_ref[...]
    product = mm(xt_ref[0], dqkv)
    bias_q = column_sum(dqkv[:, :GROUP].astype(F32))
    bias_v = column_sum(dqkv[:, 2 * GROUP :].astype(F32))

    @pl.when(row == 0)
    def _():
        acc_ref[...] = product
        vec_ref[...] = vec_in_ref[...]
        vec_ref[0:1, :] = bias_q
        vec_ref[1:2, :] = bias_v

    @pl.when(row > 0)
    def _():
        acc_ref[...] += product
        vec_ref[0:1, :] += bias_q
        vec_ref[1:2, :] += bias_v

    @pl.when(row == seqs - 1)
    def _():
        gw_ref[...] = acc_ref[...].astype(LOW)


def attention_backward(xt, qkv, ctx, probs, dctx, table, gw):
    rows = ctx.shape[0]
    seqs = rows // SEQ
    mine = lambda g, b: (b, g)
    return pl.pallas_call(
        attention_backward_kernel,
        grid=(GROUPS, seqs),
        in_specs=[
            pl.BlockSpec((1, D, SEQ), lambda g, b: (b, 0, 0)),
            pl.BlockSpec((SEQ, TRIO), mine),
            pl.BlockSpec((SEQ, GROUP), mine),
            pl.BlockSpec((SEQ, GROUP), mine),
            pl.BlockSpec((1, 1, GROUP // HEAD_DIM, SEQ, SEQ), lambda g, b: (b, g, 0, 0, 0)),
            pl.BlockSpec((8, GROUP), lambda g, b: (0, g)),
            pl.BlockSpec(memory_space=pl.ANY),
        ],
        out_specs=[
            pl.BlockSpec((D, TRIO), lambda g, b: (0, 1 + g)),
            pl.BlockSpec((SEQ, TRIO), mine),
            pl.BlockSpec((8, GROUP), lambda g, b: (0, g)),
        ],
        out_shape=[like((D, SET), LOW), like((rows, 3 * D), LOW), like((8, D), F32)],
        input_output_aliases={5: 2, 6: 0},
        scratch_shapes=[pltpu.VMEM((2, SEQ, SEQ), LOW), pltpu.VMEM((D, TRIO), F32)],
        compiler_params=pltpu.CompilerParams(vmem_limit_bytes=VMEM),
        cost_estimate=cost(rows * (6 * D * D + 8 * D * SEQ), 36 * MIB, 0),
        name="attention_backward",
    )(xt, qkv, ctx, dctx, probs, table, gw)


def input_grad_kernel(dh1_ref, dqkv_ref, *refs):
    total = dh1_ref[...]
    for g in range(GROUPS):
        total += mm_t(dqkv_ref[:, g * TRIO : (g + 1) * TRIO], refs[g][...])
    refs[GROUPS][...] = total.astype(LOW)


def input_grad(dh1, dqkv, weights):
    rows = dh1.shape[0]
    return pl.pallas_call(
        input_grad_kernel,
        grid=(rows // ROWS,),
        in_specs=[
            pl.BlockSpec((ROWS, D), lambda i: (i, 0)),
            pl.BlockSpec((ROWS, 3 * D), lambda i: (i, 0)),
            *(pl.BlockSpec((D, TRIO), lambda i, g=g: (0, 1 + g)) for g in range(GROUPS)),
        ],
        out_specs=pl.BlockSpec((ROWS, D), lambda i: (i, 0)),
        out_shape=like((rows, D), LOW),
        compiler_params=pltpu.CompilerParams(vmem_limit_bytes=VMEM),
        cost_estimate=cost(6 * rows * D * D, 13 * MIB, 0),
        name="input_grad",
    )(dh1, dqkv, *[weights] * GROUPS)


def norm_parts(hidden):
    mean = jnp.mean(hidden, axis=1, keepdims=True)
    centred = hidden - mean
    inverse = lax.rsqrt(jnp.mean(centred * centred, axis=1, keepdims=True) + EPS)
    return centred * inverse, inverse


def norm_back(grad, gain, normed, inverse):
    scaled = grad * gain
    mean = jnp.mean(scaled, axis=1, keepdims=True)
    along = jnp.mean(scaled * normed, axis=1, keepdims=True)
    return inverse * (scaled - mean - normed * along)


def column_sum(array):
    return jnp.sum(array, axis=0, keepdims=True)


def gelu_and_slope(v):
    square = v * v
    bent = jnp.tanh(v * (ROOT + ROOT * CUBE * square))
    half = 0.5 + 0.5 * bent
    act = v * half
    slope = half + act * (1.0 - half) * (2.0 * ROOT + 6.0 * ROOT * CUBE * square)
    return act, slope


def order_outer(block_ref, out_ref, unit):
    for o in range(block_ref.shape[0] // unit):
        for j in range(CHUNKS):
            to = (o * CHUNKS + j) * unit
            out_ref[to : to + unit, :] = block_ref[o * unit : (o + 1) * unit, j * D : (j + 1) * D]


def ffn_forward_kernel(
    unit, n1low_ref, outer_ref, wi_ref, bi_ref, vec_ref, n1_hbm, cot_hbm,
    slope_ref, gwo_ref, sums_ref, out_hbm, db_hbm, dh2_hbm,
    n1_ref, cot_ref, h2_ref, wo_ref, act_ref, out_ref, db_ref, dh2_ref, sem,
):
    step = pl.program_id(0)
    tiles = [slice(i, i + ROWS) for i in range(0, h2_ref.shape[0], ROWS)]
    loads = [
        pltpu.make_async_copy(n1_hbm, n1_ref, sem.at[0]),
        pltpu.make_async_copy(cot_hbm, cot_ref, sem.at[1]),
    ]
    stores = [
        pltpu.make_async_copy(out_ref, out_hbm, sem.at[2]),
        pltpu.make_async_copy(db_ref, db_hbm, sem.at[3]),
        pltpu.make_async_copy(dh2_ref, dh2_hbm, sem.at[4]),
    ]

    @pl.when(step == 0)
    def _():
        for copy in loads:
            copy.start()
        h2_ref[...] = jnp.zeros_like(h2_ref)

    @pl.when(step < CHUNKS)
    def _():
        order_outer(outer_ref, wo_ref, unit)
        for rows in tiles:
            pre = mm(n1low_ref[rows, :], wi_ref[...]) + bi_ref[...]
            act, slope = gelu_and_slope(pre)
            act = act.astype(LOW)
            act_ref[step, rows, :] = act
            slope_ref[rows, :] = slope.astype(LOW)
            h2_ref[rows, :] += mm(act, wo_ref[...])

    @pl.when(step == CHUNKS - 1)
    def _():
        for copy in loads:
            copy.wait()
        gain, shift = vec_ref[6:7, :], vec_ref[7:8, :]
        sums_ref[...] = jnp.zeros_like(sums_ref)

        @pl.loop(0, h2_ref.shape[0] // ROWS, unroll=2)
        def _(i):
            rows = pl.ds(pl.multiple_of(i * ROWS, ROWS), ROWS)
            n, inverse = norm_parts(h2_ref[rows, :] + (n1_ref[rows, :] + vec_ref[5:6, :]))
            out_ref[rows, :] = (n * gain + shift).astype(LOW)
            cot = cot_ref[rows, :].astype(F32)
            dh2 = norm_back(cot, gain, n, inverse)
            dh2_ref[rows, :] = dh2
            db = dh2.astype(LOW)
            db_ref[rows, :] = db
            for j, new in enumerate((column_sum(db.astype(F32)), column_sum(cot * n), column_sum(cot))):
                sums_ref[5 + j : 6 + j, :] += new

        for copy in stores:
            copy.start()

    @pl.when(step >= CHUNKS)
    def _():
        grad = t_mm(act_ref[step - CHUNKS], db_ref[...]).astype(LOW)
        if len(gwo_ref.shape) == 2:
            gwo_ref[...] = grad
        else:
            _, _, sides, lines, deep, _ = gwo_ref.shape
            for i in range(CHUNK // deep):
                core, side, line = i % 2, i // 2 % sides, i // 2 // sides
                gwo_ref[core, 0, side, line] = grad[i * deep : (i + 1) * deep, :]

    @pl.when(step == 2 * CHUNKS - 1)
    def _():
        for copy in stores:
            copy.wait()


def ffn_forward(unit, n1, n1low, cot, rest, b_inner, table, sizes=None):
    rows = n1.shape[0]
    last = CHUNKS - 1
    now = lambda c: jnp.minimum(c, last)
    then = lambda c: jnp.maximum(c - CHUNKS, 0)
    eight = pl.BlockSpec((8, D), lambda c: (0, 0))
    if sizes is None:
        outer_shape = (FF, D)
        outer_block = pl.BlockSpec((CHUNK, D), lambda c: (then(c), 0))
    else:
        dps, lines, sides, cores = sizes
        deep = CHUNKS * unit
        held = CHUNK // (deep * sides * cores)
        outer_shape = (cores, dps, sides, lines, deep, D)
        outer_block = pl.BlockSpec(
            (cores, 1, sides, held, deep, D),
            lambda c: (0, then(c) * held // lines, 0, then(c) % (lines // held), 0, 0),
        )
    anywhere = pl.BlockSpec(memory_space=pl.ANY)
    return pl.pallas_call(
        lambda *refs: ffn_forward_kernel(unit, *refs),
        grid=(2 * CHUNKS,),
        in_specs=[
            pl.BlockSpec((rows, D), lambda c: (0, 0), pipeline_mode=pl.Buffered(1)),
            pl.BlockSpec((D // CHUNKS, FF), lambda c: (now(c), 0)),
            pl.BlockSpec((D, CHUNK), lambda c: (0, CHUNKS + now(c))),
            pl.BlockSpec((1, CHUNK), lambda c: (0, now(c))),
            eight,
            anywhere,
            anywhere,
        ],
        out_specs=[
            pl.BlockSpec((rows, CHUNK), lambda c: (0, now(c))),
            outer_block,
            eight,
            anywhere,
            anywhere,
            anywhere,
        ],
        out_shape=[
            like((rows, FF), LOW),
            like(outer_shape, LOW),
            like((8, D), F32),
            like((rows, D), LOW),
            like((rows, D), LOW),
            like((rows, D), F32),
        ],
        scratch_shapes=[
            pltpu.VMEM((rows, D), F32),
            pltpu.VMEM((rows, D), LOW),
            pltpu.VMEM((rows, D), F32),
            pltpu.VMEM((CHUNK, D), LOW),
            pltpu.VMEM((CHUNKS, rows, CHUNK), LOW),
            pltpu.VMEM((rows, D), LOW),
            pltpu.VMEM((rows, D), LOW),
            pltpu.VMEM((rows, D), F32),
            pltpu.SemaphoreType.DMA((5,)),
        ],
        compiler_params=pltpu.CompilerParams(vmem_limit_bytes=VMEM),
        cost_estimate=cost(6 * rows * D * FF, 34 * MIB, rows * FF),
        name="ffn_forward",
    )(n1low, rest, rest, b_inner, table, n1, cot)


def ffn_backward_kernel(
    unit, n1t_ref, slope_ref, db_ref, outer_ref, wi_ref,
    gwi_ref, gbi_ref, dn1_ref,
    dpre_ref, wo_ref,
):
    step = pl.program_id(0)
    tiles = [slice(i, i + ROWS) for i in range(0, db_ref.shape[0], ROWS)]
    order_outer(outer_ref, wo_ref, unit)

    @pl.when(step == 0)
    def _():
        dn1_ref[...] = jnp.zeros_like(dn1_ref)

    bias = jnp.zeros((1, CHUNK), F32)
    for rows in tiles:
        dpre = (mm_t(db_ref[rows, :], wo_ref[...]) * slope_ref[rows, :].astype(F32)).astype(LOW)
        dpre_ref[rows, :] = dpre
        bias += column_sum(dpre.astype(F32))
        dn1_ref[rows, :] += mm_t(dpre, wi_ref[...])
    gbi_ref[...] = bias
    gwi_ref[...] = mm(n1t_ref[...], dpre_ref[...]).astype(LOW)


def ffn_backward(unit, n1t, slope, db, rest):
    rows = db.shape[0]
    once = pl.BlockSpec((rows, D), lambda c: (0, 0), pipeline_mode=pl.Buffered(1))
    return pl.pallas_call(
        lambda *refs: ffn_backward_kernel(unit, *refs),
        grid=(CHUNKS,),
        in_specs=[
            pl.BlockSpec((D, rows), lambda c: (0, 0), pipeline_mode=pl.Buffered(1)),
            pl.BlockSpec((rows, CHUNK), lambda c: (0, c)),
            once,
            pl.BlockSpec((D // CHUNKS, FF), lambda c: (c, 0)),
            pl.BlockSpec((D, CHUNK), lambda c: (0, CHUNKS + c)),
        ],
        out_specs=[
            pl.BlockSpec((D, CHUNK), lambda c: (0, c)),
            pl.BlockSpec((1, CHUNK), lambda c: (0, c)),
            pl.BlockSpec((rows, D), lambda c: (0, 0)),
        ],
        out_shape=[like((D, FF), LOW), like((1, FF), F32), like((rows, D), F32)],
        scratch_shapes=[pltpu.VMEM((rows, CHUNK), LOW), pltpu.VMEM((CHUNK, D), LOW)],
        compiler_params=pltpu.CompilerParams(vmem_limit_bytes=VMEM),
        cost_estimate=cost(6 * rows * D * FF, 30 * MIB, 0),
        name="ffn_backward",
    )(n1t, slope, db, rest, rest)


def norm_backward_kernel(
    wout_ref, vec_ref, sums_in_ref, h1_hbm, dn1_hbm, dh2_hbm, ctx_hbm,
    gw_ref, sums_ref, dctx_hbm, dh1_hbm,
    h1_ref, dn1_ref, dh2_ref, ctx_ref, da_ref, dctx_ref, dh1_ref, load_sem, store_sem,
):
    tiles = [slice(i, i + ROWS) for i in range(0, h1_ref.shape[0], ROWS)]
    pairs = ((h1_hbm, h1_ref), (dn1_hbm, dn1_ref), (dh2_hbm, dh2_ref), (ctx_hbm, ctx_ref))
    loads = [
        [pltpu.make_async_copy(a.at[rows, :], b.at[rows, :], load_sem.at[i, j]) for j, (a, b) in enumerate(pairs)]
        for i, rows in enumerate(tiles)
    ]
    stores = [
        [
            pltpu.make_async_copy(dh1_ref.at[rows, :], dh1_hbm.at[rows, :], store_sem.at[i, 0]),
            pltpu.make_async_copy(dctx_ref.at[rows, :], dctx_hbm.at[rows, :], store_sem.at[i, 1]),
        ]
        for i, rows in enumerate(tiles)
    ]
    for group in loads:
        for copy in group:
            copy.start()
    sums = [jnp.zeros((1, D), F32)] * 3
    for i, rows in enumerate([*tiles, None]):
        if rows is not None:
            for copy in loads[i]:
                copy.wait()
        if i > 0:
            dctx_ref[tiles[i - 1], :] = mm_t(da_ref[tiles[i - 1], :], wout_ref[...]).astype(LOW)
        if rows is not None:
            n, inverse = norm_parts(h1_ref[rows, :])
            dn1 = dn1_ref[rows, :] + dh2_ref[rows, :]
            dh1 = norm_back(dn1, vec_ref[3:4, :], n, inverse)
            dh1_ref[rows, :] = dh1
            da = dh1.astype(LOW)
            da_ref[rows, :] = da
            new = (column_sum(da.astype(F32)), column_sum(dn1 * n), column_sum(dn1))
            sums = [a + b for a, b in zip(sums, new)]
            stores[i][0].start()
        if i > 0:
            stores[i - 1][1].start()
    gw_ref[...] = t_mm(ctx_ref[...], da_ref[...]).astype(LOW)
    sums_ref[...] = sums_in_ref[...]
    for i in range(3):
        sums_ref[2 + i : 3 + i, :] = sums[i]
    for group in stores:
        for copy in group:
            copy.wait()


def norm_backward(h1, dn1, dh2, ctx, weights, table, sums):
    rows = h1.shape[0]
    eight = pl.BlockSpec((8, D), lambda i: (0, 0))
    square = pl.BlockSpec((D, D), lambda i: (0, 0))
    anywhere = pl.BlockSpec(memory_space=pl.ANY)
    return pl.pallas_call(
        norm_backward_kernel,
        grid=(1,),
        in_specs=[square, eight, eight] + [anywhere] * 4,
        out_specs=[square, eight, anywhere, anywhere],
        out_shape=[like((D, SET), LOW), like((8, D), F32), like((rows, D), LOW), like((rows, D), F32)],
        scratch_shapes=[
            pltpu.VMEM((rows, D), F32),
            pltpu.VMEM((rows, D), F32),
            pltpu.VMEM((rows, D), F32),
            pltpu.VMEM((rows, D), LOW),
            pltpu.VMEM((rows, D), LOW),
            pltpu.VMEM((rows, D), LOW),
            pltpu.VMEM((rows, D), F32),
            pltpu.SemaphoreType.DMA((rows // ROWS, 4)),
            pltpu.SemaphoreType.DMA((rows // ROWS, 2)),
        ],
        compiler_params=pltpu.CompilerParams(vmem_limit_bytes=VMEM),
        cost_estimate=cost(4 * rows * D * D, 17 * MIB, 0),
        name="norm_backward",
    )(weights, table, sums, h1, dn1, dh2, ctx)


def after(values, *others):
    return lax.optimization_barrier((values, others))[0]


def whole(array):
    return pl.BlockSpec(array.shape, lambda *_: (0,) * len(array.shape))


def pack_kernel(wq_ref, wk_ref, wv_ref, wout_ref, wi_ref, wo_ref, *refs):
    vectors, (set_ref, rest_ref) = refs[:9], refs[9:]
    unit = wq_ref.shape[0]
    set_ref[:, :D] = wout_ref[...]
    for g in range(GROUPS):
        for part, ref in enumerate((wq_ref, wk_ref, wv_ref)):
            to = D + g * TRIO + part * GROUP
            set_ref[:, to : to + GROUP] = ref[:, g * GROUP : (g + 1) * GROUP]
    table = jnp.zeros((unit, PAIR), F32)
    row = lax.broadcasted_iota(jnp.int32, (unit, PAIR), 0)
    for i, ref in enumerate(vectors):
        size = ref.shape[1]
        line = jnp.concatenate([ref[...].astype(F32), jnp.zeros((1, PAIR - size), F32)], axis=1)
        table = jnp.where(row == i, line, table)
    set_ref[:, 4 * D :] = table.astype(LOW)
    for j in range(CHUNKS):
        rest_ref[:, j * D : (j + 1) * D] = wo_ref[j * unit : (j + 1) * unit, :]
    rest_ref[:, FF:] = wi_ref[...]


def pack(wq, wk, wv, wout, wi, wo, vectors):
    unit = wq.shape[0]
    args = (wq, wk, wv, wout, wi, wo, *(v.reshape(1, -1) for v in vectors))
    shapes = [like((unit, SET), LOW), like((unit, 2 * FF), LOW)]
    return pl.pallas_call(
        pack_kernel,
        in_specs=[whole(a) for a in args],
        out_specs=[whole(a) for a in shapes],
        out_shape=shapes,
        name="pack",
    )(*args)


def stack_kernel(*refs):
    for i, ref in enumerate(refs[:-1]):
        refs[-1][i] = ref[...]


def stack(pieces):
    shape = like((len(pieces), *pieces[0].shape), pieces[0].dtype)
    return pl.pallas_call(
        stack_kernel,
        in_specs=[whole(a) for a in pieces],
        out_specs=whole(shape),
        out_shape=shape,
        name="stack",
    )(*pieces)


class Slice:
    def __init__(self):
        self.sizes = tuple(lax.axis_size(name) for name in AXES)
        self.dp, self.line, self.side, self.core = (lax.axis_index(name) for name in AXES)
        self.offsets = [(a, b) for a in range(self.sizes[0]) for b in range(self.sizes[2])]

    def to_core(self, array):
        return lax.ppermute(array, "core", [(0, 1), (1, 0)])

    def to_plane(self, array, offset):
        dps, _, sides, _ = self.sizes
        pairs = [
            (i * sides + j, (i + offset[0]) % dps * sides + (j + offset[1]) % sides)
            for i in range(dps)
            for j in range(sides)
        ]
        return lax.ppermute(array, ("dp", "side"), pairs)

    def to_line(self, array, shift):
        count = self.sizes[1]
        return lax.ppermute(array, "line", [(i, (i + shift) % count) for i in range(count)])

    def gather(self, mine):
        dps, lines, sides, _ = self.sizes
        unit, columns = mine.shape
        line = stack([mine] + [self.to_line(mine, s) for s in range(1, lines)])
        here = [line if o == (0, 0) else self.to_plane(line, o) for o in self.offsets]
        there = [self.to_core(a) for a in here]
        place = jnp.stack([self.dp, self.line, self.side, self.core]).astype(jnp.int32)
        pieces = here + there

        def kernel(place_ref, *refs):
            out_ref = refs[-1]
            for i in range(len(pieces)):
                a, b = self.offsets[i % len(here)]
                dp = lax.rem(place_ref[0] + dps - a, dps)
                side = lax.rem(place_ref[2] + sides - b, sides)
                core = place_ref[3] if i < len(here) else 1 - place_ref[3]
                for s in range(lines):
                    along = lax.rem(place_ref[1] + lines - s, lines)
                    out_ref[((dp * lines + along) * sides + side) * 2 + core] = refs[i][s]

        wide = 5 * PAIR
        count = dps * lines * sides * 2
        return pl.pallas_call(
            kernel,
            grid=(columns // wide,),
            in_specs=[pl.BlockSpec(memory_space=pltpu.SMEM)]
            + [pl.BlockSpec((lines, unit, wide), lambda i: (0, 0, i))] * len(pieces),
            out_specs=pl.BlockSpec((count, unit, wide), lambda i: (0, 0, i)),
            out_shape=like((count, unit, columns), mine.dtype),
            compiler_params=pltpu.CompilerParams(vmem_limit_bytes=VMEM),
            name="place",
        )(place, *pieces).reshape(-1, columns)


    def core_sum(self, grad):
        return lax.psum_scatter(grad, "core", scatter_dimension=0)

    def plane_sum(self, grad):
        return lax.psum_scatter(grad.reshape(-1, *grad.shape[2:]), ("dp", "side"), scatter_dimension=0)

    def line_sum(self, grad):
        return lax.psum_scatter(grad, "line", scatter_dimension=0)


    def plane_messages(self, grad, got):
        dps, _, sides, _ = self.sizes
        return [
            self.block(
                grad, got, lax.rem(self.dp + a, dps), lax.rem(self.side + b, sides), (0, grad.shape[1])
            )[0, :, 0].astype(LOW)
            for a, b in self.offsets
        ]

    def plane_exchange(self, messages):
        return messages[:1] + [self.to_plane(m, o) for m, o in zip(messages[1:], self.offsets[1:])]

    def plane_done(self, parts):
        return self.along_line(sum(p.astype(F32) for p in parts).astype(LOW))

    def block(self, grad, got, dp, side, columns):
        dps, lines, sides, _ = self.sizes
        parts = grad.reshape(*self.sizes, -1, grad.shape[1])
        unit, (first, last) = parts.shape[4], columns
        start = (0 if dp is None else dp, 0, 0 if side is None else side)
        size = (dps if dp is None else 1, lines, sides if side is None else 1)
        mine = lax.dynamic_slice(parts, (*start, self.core, 0, first), (*size, 1, unit, last - first))
        other = lax.dynamic_slice(got, (*start, 0, first), (*size, unit, last - first))
        return mine[:, :, :, 0].astype(F32) + other.astype(F32)

    def halves(self, grad):
        columns = grad.shape[1]
        middle = -(-columns // (2 * PAIR)) * PAIR
        return (0, middle), (middle, columns)

    def core_message(self, grad):
        parts = grad.reshape(*self.sizes, -1, grad.shape[1])
        return lax.dynamic_index_in_dim(parts, 1 - self.core, 3, keepdims=False)

    def first_messages(self, grad, got):
        one, two = self.halves(grad)
        return (
            self.block(grad, got, None, 1 - self.side, one).astype(LOW),
            self.block(grad, got, 1 - self.dp, None, two).astype(LOW),
        )

    def first_exchange(self, messages):
        return self.to_plane(messages[0], (0, 1)), self.to_plane(messages[1], (1, 0))

    def second_messages(self, grad, got, more):
        one, two = self.halves(grad)
        a = self.block(grad, got, 1 - self.dp, self.side, one)
        b = self.block(grad, got, self.dp, 1 - self.side, two)
        a += lax.dynamic_slice_in_dim(more[0], 1 - self.dp, 1, 0).astype(F32)
        b += lax.dynamic_slice_in_dim(more[1], 1 - self.side, 1, 2).astype(F32)
        return a.astype(LOW), b.astype(LOW)

    def second_exchange(self, messages):
        return self.to_plane(messages[0], (1, 0)), self.to_plane(messages[1], (0, 1))

    def line_messages(self, grad, got, more, most):
        one, two = self.halves(grad)
        a = self.block(grad, got, self.dp, self.side, one) + most[0].astype(F32)
        b = self.block(grad, got, self.dp, self.side, two) + most[1].astype(F32)
        a += lax.dynamic_slice_in_dim(more[0], self.dp, 1, 0).astype(F32)
        b += lax.dynamic_slice_in_dim(more[1], self.side, 1, 2).astype(F32)
        total = jnp.concatenate([a[0, :, 0], b[0, :, 0]], axis=2).astype(LOW)
        return self.along_line(total)

    def along_line(self, total):
        lines = self.sizes[1]
        at = [lax.rem(self.line + s, lines) for s in range(lines)]
        return [lax.dynamic_index_in_dim(total, i, 0, keepdims=False) for i in at]

    def line_exchange(self, messages):
        return messages[:1] + [self.to_line(m, s) for s, m in enumerate(messages) if s]


def finish_kernel(count, *refs):
    parts, (wout_ref, wq_ref, wk_ref, wv_ref), vectors = refs[:count], refs[count : count + 4], refs[count + 4 :]
    total = sum(ref[...].astype(F32) for ref in parts)
    wout_ref[...] = total[:, :D]
    for g in range(GROUPS):
        for part, ref in enumerate((wq_ref, wk_ref, wv_ref)):
            at = D + g * TRIO + part * GROUP
            ref[:, g * GROUP : (g + 1) * GROUP] = total[:, at : at + GROUP]
    for i, ref in enumerate(vectors):
        ref[...] = total[i : i + 1, 4 * D : 4 * D + ref.shape[1]]


def finish(parts):
    unit = parts[0].shape[0]
    shapes = [like((unit, D), F32)] * 4 + [like((1, unit), F32)] * 8 + [like((1, CHUNKS * unit), F32)]
    outs = pl.pallas_call(
        lambda *refs: finish_kernel(len(parts), *refs),
        in_specs=[whole(a) for a in parts],
        out_specs=[whole(a) for a in shapes],
        out_shape=shapes,
        name="finish",
    )(*parts)
    return outs[:4], [v.reshape(-1) for v in outs[4:]]


def vector_rows(table, b_inner, count):
    unit = D // count
    eight = table.reshape(8, count, unit).transpose(1, 0, 2)
    inner = b_inner.reshape(count, 1, CHUNKS * unit)
    eight = jnp.pad(eight, ((0, 0), (0, 0), (0, PAIR - unit)))
    inner = jnp.pad(inner, ((0, 0), (0, unit - 9), (0, PAIR - CHUNKS * unit)))
    return jnp.concatenate([eight, inner], axis=1).reshape(D, PAIR).astype(LOW)


def on_device(block_input, segment_ids, cotangent, *params):
    w_query, w_key, w_value, w_out, w_inner, w_outer = (params[i] for i in MATRICES)
    vectors = [params[i] for i in VECTORS]
    unit = w_query.shape[0]
    count = D // unit
    mesh = Slice()
    quick = mesh.sizes == (2, 4, 2, 2) and unit == 24
    x = block_input.reshape(-1, D)
    cot = cotangent.reshape(-1, D)

    if quick:
        mine, rest_mine = pack(w_query, w_key, w_value, w_out, w_inner, w_outer, vectors)
        rest = lax.all_gather(rest_mine, AXES, axis=0, tiled=True)
        weights = mesh.gather(mine)
        side = weights[:, 4 * D :].reshape(count, unit, PAIR)
        table = side[:, :8, :unit].transpose(1, 0, 2).reshape(8, D).astype(F32)
        b_inner = side[:, 8, : CHUNKS * unit].reshape(1, FF).astype(F32)
    else:
        trios = [w[:, g : g + GROUP] for g in range(0, D, GROUP) for w in (w_query, w_key, w_value)]
        full = lax.all_gather(jnp.concatenate([w_out, *trios, w_inner], axis=1), AXES, axis=0, tiled=True)
        outer = lax.all_gather(w_outer, AXES, axis=0, tiled=True)
        vector = lax.all_gather(jnp.concatenate(vectors), AXES, axis=0).astype(F32)
        weights = full[:, : 4 * D]
        table = jnp.concatenate([vector[:, i * unit : (i + 1) * unit].reshape(1, D) for i in range(8)])
        b_inner = vector[:, 8 * unit :].reshape(1, FF)
        unit = 24
        outer = outer.reshape(-1, CHUNKS, unit, D).transpose(0, 2, 1, 3).reshape(D, FF)
        rest = jnp.concatenate([outer, full[:, 4 * D :]], axis=1)

    qkv, ctx, probs, xt, h1, n1, n1low, n1t = attention_forward(x, segment_ids, weights, table)
    slope, g_outer, sums, result, db, dh2 = ffn_forward(
        unit, n1, n1low, cot, rest, b_inner, table, mesh.sizes if quick else None
    )
    if quick:
        db = after(db, g_outer)
        g_outer = mesh.core_sum(g_outer)
    g_inner, g_b_inner, dn1 = ffn_backward(unit, n1t, slope, db, rest)
    if not quick:
        late, sums, dctx, dh1 = norm_backward(h1, dn1, dh2, ctx, weights, table, sums)
        late, dqkv, sums = attention_backward(xt, qkv, ctx, probs, dctx, sums, late)
        dx = input_grad(dh1, dqkv, weights)
        wide = jnp.concatenate([late[:, : 4 * D], g_inner], axis=1)
        wide = lax.psum_scatter(wide, AXES, scatter_dimension=0, tiled=True).astype(F32)
        g_outer = lax.psum_scatter(g_outer, AXES, scatter_dimension=0, tiled=True).astype(F32)
        vector = jnp.concatenate([*sums.reshape(8, count, -1), g_b_inner.reshape(count, -1)], axis=1)
        vector = lax.psum_scatter(vector.reshape(-1), AXES, scatter_dimension=0, tiled=True)
        size = D // count
        vectors = [vector[i * size : (i + 1) * size] for i in range(8)] + [vector[8 * size :]]
        matrices = [wide[:, :D]] + [
            jnp.concatenate([wide[:, g + part : g + part + GROUP] for g in range(D, 4 * D, TRIO)], axis=1)
            for part in range(0, TRIO, GROUP)
        ]
        g_inner = wide[:, 4 * D :]
    else:
        message = mesh.core_message(g_inner)
        dn1, g_outer = after((dn1, g_outer), message)
        g_outer = mesh.plane_sum(g_outer)
        got = mesh.to_core(message)
        late, sums, dctx, dh1 = norm_backward(h1, dn1, dh2, ctx, weights, table, sums)
        got, sums = after((got, sums), dctx)
        message = mesh.plane_messages(g_inner, got)
        sums = after(sums, message)
        parts = mesh.plane_exchange(message)
        late, dqkv, sums = attention_backward(xt, qkv, ctx, probs, dctx, sums, late)
        late, parts, g_outer = after((late, parts, g_outer), dqkv)
        g_outer = mesh.line_sum(g_outer)
        late = lax.dynamic_update_slice(late, vector_rows(sums, g_b_inner, count), (0, 4 * D))
        message = mesh.core_message(late)
        dqkv, parts = after((dqkv, parts), message)
        lines = mesh.line_exchange(mesh.plane_done(parts))
        got = mesh.to_core(message)
        more = mesh.first_exchange(mesh.first_messages(late, got))
        dx = input_grad(dh1, dqkv, weights)
        more, g_inner = after((more, lines), dx)
        most = mesh.second_exchange(mesh.second_messages(late, got, more))
        most, g_outer = after((most, g_outer), dx)
        message = mesh.line_messages(late, got, more, most)
        g_outer, g_inner = after((g_outer, g_inner), message)
        matrices, vectors = finish(mesh.line_exchange(message))
        g_outer = g_outer.astype(F32)
        g_inner = sum(p.astype(F32) for p in g_inner)
    g_out, *matrices = matrices

    shards = [None] * len(params)
    for i, value in zip(MATRICES, (*matrices, g_out, g_inner, g_outer)):
        shards[i] = value
    for i, value in zip(VECTORS, vectors):
        shards[i] = value
    return (result.reshape(block_input.shape), dx.reshape(block_input.shape), *shards)


def solution(mesh):
    sizes = (mesh.shape["dp"], mesh.shape["fsdp"] // 4, 2, 2)
    parts = Mesh(np.asarray(mesh.devices).reshape(sizes), AXES)
    vector, matrix, rows = P(AXES), P(AXES, None), P(AXES, None, None)
    params = tuple(vector if i in VECTORS else matrix for i in range(15))
    return jax.shard_map(
        on_device,
        mesh=parts,
        in_specs=(rows, matrix, rows) + params,
        out_specs=(rows, rows) + params,
        check_vma=False,
    )
```

profile of v0, /device:TPU:0, one launch (start us, length us, event | category | flops | bytes accessed | tf_op | source)
XLA Modules:
  0.0 288.7 jit_solution(14132107018480948084)
XLA Ops:
  9.2 3.1 %collective-permute-start = (bf16[24,3200]{1,0:T(8,128)(2,1)}, bf16[24,3200]{1,0:T(8,128)(2,1)S(1)}, u32[]{:S(2)}, u32[]{:S(2)}) collective-permute-start(bf16[24,3200]{1,0:T(8,128)(2,1)} %get-tuple-element.87.refs_0_), channel_id=1, source_target_pairs={{0,4},{4,8},{8,12},{12,0},{1,5},{5,9},{9,13},{13,1},{2,6},{6,10},{... | collective-permute-start | bytes 460808 | tf_op jit(solution)/shard_map/ppermute | solution.py:649
  12.3 2.6 collective-permute-start.1
  16.2 3.2 %collective-permute-done.refs_1_ = bf16[24,3200]{1,0:T(8,128)(2,1)S(1)} collective-permute-done((bf16[24,3200]{1,0:T(8,128)(2,1)}, bf16[24,3200]{1,0:T(8,128)(2,1)S(1)}, u32[]{:S(2)}, u32[]{:S(2)}) %collective-permute-start) | collective-permute-done | bytes 153632 | tf_op jit(solution)/shard_map/ppermute | solution.py:649
  19.4 5.7 %collective-permute-done.1.refs_2_ = bf16[24,3200]{1,0:T(8,128)(2,1)S(1)} collective-permute-done((bf16[24,3200]{1,0:T(8,128)(2,1)}, bf16[24,3200]{1,0:T(8,128)(2,1)S(1)}, u32[]{:S(2)}, u32[]{:S(2)}) %collective-permute-start.1) | collective-permute-done | bytes 153632 | tf_op jit(solution)/shard_map/ppermute | solution.py:649
  32.0 15.1 %collective-permute-done.3.refs_1_ = bf16[4,24,3200]{2,1,0:T(8,128)(2,1)S(1)} collective-permute-done((bf16[4,24,3200]{2,1,0:T(8,128)(2,1)}, bf16[4,24,3200]{2,1,0:T(8,128)(2,1)S(1)}, u32[]{:S(2)}, u32[]{:S(2)}) %collective-permute-start.3) | collective-permute-done | bytes 614432 | tf_op jit(solution)/shard_map/ppermute | solution.py:645
  47.1 6.0 %collective-permute-done.4.refs_2_ = bf16[4,24,3200]{2,1,0:T(8,128)(2,1)S(1)} collective-permute-done((bf16[4,24,3200]{2,1,0:T(8,128)(2,1)}, bf16[4,24,3200]{2,1,0:T(8,128)(2,1)S(1)}, u32[]{:S(2)}, u32[]{:S(2)}) %collective-permute-start.4) | collective-permute-done | bytes 614432 | tf_op jit(solution)/shard_map/ppermute | solution.py:645
  53.1 13.8 %collective-permute-done.5.refs_3_ = bf16[4,24,3200]{2,1,0:T(8,128)(2,1)S(1)} collective-permute-done((bf16[4,24,3200]{2,1,0:T(8,128)(2,1)}, bf16[4,24,3200]{2,1,0:T(8,128)(2,1)S(1)}, u32[]{:S(2)}, u32[]{:S(2)}) %collective-permute-start.5) | collective-permute-done | bytes 614432 | tf_op jit(solution)/shard_map/ppermute | solution.py:645
  69.1 6.6 %place.1 = bf16[32,24,3200]{2,1,0:T(8,128)(2,1)} custom-call(s32[4]{0:T(128)} %pad_add_fusion.place_ref, bf16[4,24,3200]{2,1,0:T(8,128)(2,1)} %stack.21.refs_0_, bf16[4,24,3200]{2,1,0:T(8,128)(2,1)} %copy-done, bf16[4,24,3200]{2,1,0:T(8,128)(2,1)} %copy-done.1, bf16[4,24,3200]{2,1,0:T(8,128)(2,1)} %copy-done.2, bf16[4,24,3200]{2,1,0:T(8,128)(2,1)} %copy-done.3, ...), custom_call_target="tpu_custom_call" | custom-call | tf_op jit(solution)/shard_map/place/pallas_call | solution.py:673
  78.2 30.7 %attention_forward.1 = (bf16[1024,2304]{1,0:T(8,128)(2,1)}, bf16[1024,768]{1,0:T(8,128)(2,1)}, bf16[2,3,4,512,512]{4,3,2,1,0:T(8,128)(2,1)}, bf16[2,768,512]{2,1...) custom-call(bf16[1024,768]{1,0:T(8,128)(2,1)} %bitcast.152, ...), custom_call_target="tpu_custom_call" | custom-call | flops 6442450944 | bytes 37748736 | tf_op jit(solution)/shard_map/attention_forward/pallas_call | solution.py:116
  109.0 27.6 %ffn_forward.1 = (bf16[1024,3072]{1,0:T(8,128)(2,1)}, bf16[2,2,2,4,96,768]{5,4,3,2,1,0:T(8,128)(2,1)}, f32[8,768]{1,0:T(8,128)}, bf16[1024,768]{1,0:T(8,128)(2,1...) custom-call(bf16[1024,768]{1,0:T(8,128)(2,1)} %get-tuple-element.88.refs_0_, ...), custom_call_target="tpu_custom_call" | custom-call | flops 14495514624 | bytes 35651584 | tf_op jit(solution)/shard_map/ffn_forward/pallas_call | solution.py:401
  136.8 21.2 %ffn_backward.1 = (bf16[768,3072]{1,0:T(8,128)(2,1)}, f32[1,3072]{1,0:T(1,128)}, f32[1024,768]{1,0:T(8,128)}) custom-call(bf16[768,1024]{1,0:T(8,128)(2,1)} %get-tuple-element.94.refs_0_, bf16[1024,3072]{1,0:T(8,128)(2,1)} %get-tuple-element.95.refs_1_, bf16[1024,768]{1,0:T(8,128)(2,1)} %get-tuple-element.98.refs_2_, ...), custom_call_target="tpu_custom_call" | custom-call | flops 14495514624 | bytes 31457280 | tf_op jit(solution)/shard_map/ffn_backward/pallas_call | solution.py:472
  158.0 3.3 %copy_bitcast_fusion.1 = bf16[2,4,2,24,3072]{4,3,1,2,0:T(8,128)(2,1)} fusion(bf16[2,4,2,2,24,3072]{5,4,3,2,1,0:T(8,128)(2,1)} %bitcast.133, s32[]{:T(128)S(6)} %select_n.41), kind=kLoop, calls=%fused_computation.1 | loop fusion | bytes 4718596 | tf_op jit(solution)/shard_map/jit(dynamic_index_in_dim)/squeeze | solution.py:727
  162.1 9.8 %norm_backward.1 = (bf16[768,3200]{1,0:T(8,128)(2,1)}, f32[8,768]{1,0:T(8,128)}, bf16[1024,768]{1,0:T(8,128)(2,1)}, f32[1024,768]{1,0:T(8,128)}) custom-call(bf16[768,3200]{1,0:T(8,128)(2,1)} %bitcast.122, f32[8,768]{1,0:T(8,128)} %reshape.325.vec_ref.refs_4_, f32[8,768]{1,0:T(8,128)} %get-tuple-element.92.sums_in_ref, ...), custom_call_target="tpu_custom_call" | custom-call | flops 2415919104 | bytes 17825792 | tf_op jit(solution)/shard_map/norm_backward/pallas_call | solution.py:549
  171.9 4.2 %fusion.14 = (bf16[4,24,3072]{2,1,0:T(8,128)(2,1)}, bf16[4,24,3072]{2,1,0:T(8,128)(2,1)}, bf16[4,24,3072]{2,1,0:T(8,128)(2,1)}, bf16[4,24,3072]{2,1,0:T(8,128)(2,1)S(1)}) fusion(bf16[2,4,2,24,3072]{4,3,1,2,0:T(8,128)(2,1)} %collective-permute-done.10, s32[]{:T(128)S(6)} %select_n.46, s32[]{:T(128)S(6)} %select_n.45, ...), kind=kLoop, calls=%fused_computation.33 | loop fusion | flops 4718592 | bytes 7077908 | tf_op jit(solution)/shard_map/convert_element_type | solution.py:700
  179.6 27.8 %attention_backward.1 = (bf16[768,3200]{1,0:T(8,128)(2,1)}, bf16[1024,2304]{1,0:T(8,128)(2,1)}, f32[8,768]{1,0:T(8,128)}) custom-call(bf16[2,768,512]{2,1,0:T(8,128)(2,1)} %get-tuple-element.105.xt_ref, bf16[1024,2304]{1,0:T(8,128)(2,1)} %get-tuple-element.106.qkv_ref, ...), custom_call_target="tpu_custom_call", output_to_operand_aliasing={{2}: (5, {}), {0}: (6, {})} | custom-call | flops 6845104128 | bytes 37748736 | tf_op jit(solution)/shard_map/attention_backward/pallas_call | solution.py:223
  208.4 9.6 %collective-permute-done.13 = bf16[4,24,3072]{2,1,0:T(8,128)(2,1)} collective-permute-done((bf16[4,24,3072]{2,1,0:T(8,128)(2,1)}, bf16[4,24,3072]{2,1,0:T(8,128)(2,1)}, u32[]{:S(2)}, u32[]{:S(2)}) %collective-permute-start.13) | collective-permute-done | bytes 589856 | tf_op jit(solution)/shard_map/ppermute | solution.py:645
  222.5 3.0 %collective-permute-done.14 = bf16[2,4,2,24,3200]{4,3,1,2,0:T(8,128)(2,1)} collective-permute-done((bf16[2,4,2,24,3200]{4,3,1,2,0:T(8,128)(2,1)S(1)}, bf16[2,4,2,24,3200]{4,3,1,2,0:T(8,128)(2,1)}, u32[]{:S(2)}, u32[]{:S(2)}) %collective-permute-start.14) | collective-permute-done | bytes 2457632 | tf_op jit(solution)/shard_map/ppermute | solution.py:636
  228.2 2.3 fusion
  233.3 2.4 collective-permute-start.18
  237.1 8.5 %input_grad.1 = bf16[1024,768]{1,0:T(8,128)(2,1)} custom-call(f32[1024,768]{1,0:T(8,128)} %get-tuple-element.104.dh1_ref, bf16[1024,2304]{1,0:T(8,128)(2,1)} %get-tuple-element.124.dqkv_ref, bf16[768,3200]{1,0:T(8,128)(2,1)} %bitcast.123, bf16[768,3200]{1,0:T(8,128)(2,1)} %bitcast.124, bf16[768,3200]{1,0:T(8,128)(2,1)} %bitcast.125), custom_call_target="tpu_custom_call" | custom-call | flops 3623878656 | bytes 13631488 | tf_op jit(solution)/shard_map/input_grad/pallas_call | solution.py:258
  245.7 3.2 %collective-permute-done.18 = bf16[24,3072]{1,0:T(8,128)(2,1)} collective-permute-done((bf16[24,3072]{1,0:T(8,128)(2,1)}, bf16[24,3072]{1,0:T(8,128)(2,1)}, u32[]{:S(2)}, u32[]{:S(2)}) %collective-permute-start.18) | collective-permute-done | bytes 147488 | tf_op jit(solution)/shard_map/ppermute | solution.py:649
  254.4 6.9 %collective-permute-done.21 = bf16[1,4,1,24,1536]{4,3,1,2,0:T(8,128)(2,1)S(1)} collective-permute-done((bf16[1,4,1,24,1536]{4,3,1,2,0:T(8,128)(2,1)S(1)}, bf16[1,4,1,24,1536]{4,3,1,2,0:T(8,128)(2,1)S(1)}, u32[]{:S(2)}, u32[]{:S(2)}) %collective-permute-start.21) | collective-permute-done | bytes 294944 | tf_op jit(solution)/shard_map/ppermute | solution.py:645
  264.6 3.7 %collective-permute-start.22 = (bf16[24,3200]{1,0:T(8,128)(2,1)S(1)}, bf16[24,3200]{1,0:T(8,128)(2,1)S(1)}, u32[]{:S(2)}, u32[]{:S(2)}) collective-permute-start(bf16[24,3200]{1,0:T(8,128)(2,1)S(1)} %get-tuple-element.163), channel_id=1, source_target_pairs={{0,4},{4,8},{8,12},{12,0},{1,5},{5,9},{9,13},{13,1},{2,6},{6,10},{... | collective-permute-start | bytes 460808 | tf_op jit(solution)/shard_map/ppermute | solution.py:649
  274.7 4.3 %collective-permute-done.23.refs_2_ = bf16[24,3200]{1,0:T(8,128)(2,1)S(1)} collective-permute-done((bf16[24,3200]{1,0:T(8,128)(2,1)S(1)}, bf16[24,3200]{1,0:T(8,128)(2,1)S(1)}, u32[]{:S(2)}, u32[]{:S(2)}) %collective-permute-start.23) | collective-permute-done | bytes 153632 | tf_op jit(solution)/shard_map/ppermute | solution.py:649
  (102 shorter events, 50.0 us)
Async XLA Ops:
  7.2 101.8 %all-gather.2.cloned.1.call-start = ((), (), s32[]{:S(2)}) async-start(), calls=%async_computation.3 | async-start | bytes 9732096 | tf_op jit(solution)/shard_map/all_gather | solution.py:814
  9.2 152.1 %reduce-scatter.6.cloned.1.call-start = ((), (), s32[]{:S(2)}) async-start(), calls=%async_computation.4 | async-start | bytes 7077888 | tf_op jit(solution)/shard_map/reduce_scatter | solution.py:686
  9.2 10.2 %collective-permute-start = (bf16[24,3200]{1,0:T(8,128)(2,1)}, bf16[24,3200]{1,0:T(8,128)(2,1)S(1)}, u32[]{:S(2)}, u32[]{:S(2)}) collective-permute-start(bf16[24,3200]{1,0:T(8,128)(2,1)} %get-tuple-element.87.refs_0_), channel_id=1, source_target_pairs={{0,4},{4,8},{8,12},{12,0},{1,5},{5,9},{9,13},{13,1},{2,6},{6,10},{... | collective-permute-start | bytes 460808 | tf_op jit(solution)/shard_map/ppermute | solution.py:649
  12.3 12.9 %collective-permute-start.1 = (bf16[24,3200]{1,0:T(8,128)(2,1)}, bf16[24,3200]{1,0:T(8,128)(2,1)S(1)}, u32[]{:S(2)}, u32[]{:S(2)}) collective-permute-start(bf16[24,3200]{1,0:T(8,128)(2,1)} %get-tuple-element.87.refs_0_), channel_id=1, source_target_pairs={{0,8},{4,12},{8,0},{12,4},{1,9},{5,13},{9,1},{13,5},{2,10},{6,14},... | collective-permute-start | bytes 460808 | tf_op jit(solution)/shard_map/ppermute | solution.py:649
  14.9 10.3 %collective-permute-start.2 = (bf16[24,3200]{1,0:T(8,128)(2,1)}, bf16[24,3200]{1,0:T(8,128)(2,1)S(1)}, u32[]{:S(2)}, u32[]{:S(2)}) collective-permute-start(bf16[24,3200]{1,0:T(8,128)(2,1)} %get-tuple-element.87.refs_0_), channel_id=1, source_target_pairs={{0,12},{4,0},{8,4},{12,8},{1,13},{5,1},{9,5},{13,9},{2,14},{6,2},{... | collective-permute-start | bytes 460808 | tf_op jit(solution)/shard_map/ppermute | solution.py:649
  28.5 18.6 %collective-permute-start.3 = (bf16[4,24,3200]{2,1,0:T(8,128)(2,1)}, bf16[4,24,3200]{2,1,0:T(8,128)(2,1)S(1)}, u32[]{:S(2)}, u32[]{:S(2)}) collective-permute-start(bf16[4,24,3200]{2,1,0:T(8,128)(2,1)} %stack.21.refs_0_), channel_id=1, source_target_pairs={{0,2},{2,0},{16,18},{18,16},{1,3},{3,1},{17,19},{19,17},{4,6},{6,4... | collective-permute-start | bytes 1843208 | tf_op jit(solution)/shard_map/ppermute | solution.py:645
  30.0 23.1 %collective-permute-start.4 = (bf16[4,24,3200]{2,1,0:T(8,128)(2,1)}, bf16[4,24,3200]{2,1,0:T(8,128)(2,1)S(1)}, u32[]{:S(2)}, u32[]{:S(2)}) collective-permute-start(bf16[4,24,3200]{2,1,0:T(8,128)(2,1)} %stack.21.refs_0_), channel_id=1, source_target_pairs={{0,16},{2,18},{16,0},{18,2},{1,17},{3,19},{17,1},{19,3},{4,20},{6,... | collective-permute-start | bytes 1843208 | tf_op jit(solution)/shard_map/ppermute | solution.py:645
  31.5 35.4 %collective-permute-start.5 = (bf16[4,24,3200]{2,1,0:T(8,128)(2,1)}, bf16[4,24,3200]{2,1,0:T(8,128)(2,1)S(1)}, u32[]{:S(2)}, u32[]{:S(2)}) collective-permute-start(bf16[4,24,3200]{2,1,0:T(8,128)(2,1)} %stack.21.refs_0_), channel_id=1, source_target_pairs={{0,18},{2,16},{16,2},{18,0},{1,19},{3,17},{17,3},{19,1},{4,22},{6,... | collective-permute-start | bytes 1843208 | tf_op jit(solution)/shard_map/ppermute | solution.py:645
  32.0 35.6 %collective-permute-start.6 = (bf16[4,24,3200]{2,1,0:T(8,128)(2,1)}, bf16[4,24,3200]{2,1,0:T(8,128)(2,1)S(1)}, u32[]{:S(2)}, u32[]{:S(2)}) collective-permute-start(bf16[4,24,3200]{2,1,0:T(8,128)(2,1)} %stack.21.refs_0_), channel_id=1, source_target_pairs={{0,1},{1,0},{2,3},{3,2},{4,5},{5,4},{6,7},{7,6},{8,9},{9,8},{10,11... | collective-permute-start | bytes 1843208 | tf_op jit(solution)/shard_map/ppermute | solution.py:636
  47.1 20.5 %collective-permute-start.7 = (bf16[4,24,3200]{2,1,0:T(8,128)(2,1)S(1)}, bf16[4,24,3200]{2,1,0:T(8,128)(2,1)S(1)}, u32[]{:S(2)}, u32[]{:S(2)}) collective-permute-start(bf16[4,24,3200]{2,1,0:T(8,128)(2,1)S(1)} %collective-permute-done.3.refs_1_), channel_id=1, source_target_pairs={{0,1},{1,0},{2,3},{3,2},{4,5},{5,4},{6,7},{7,6},{8,9},{9,8},{10,11... | collective-permute-start | bytes 1843208 | tf_op jit(solution)/shard_map/ppermute | solution.py:636
  53.1 14.5 %collective-permute-start.8 = (bf16[4,24,3200]{2,1,0:T(8,128)(2,1)S(1)}, bf16[4,24,3200]{2,1,0:T(8,128)(2,1)}, u32[]{:S(2)}, u32[]{:S(2)}) collective-permute-start(bf16[4,24,3200]{2,1,0:T(8,128)(2,1)S(1)} %collective-permute-done.4.refs_2_), channel_id=1, source_target_pairs={{0,1},{1,0},{2,3},{3,2},{4,5},{5,4},{6,7},{7,6},{8,9},{9,8},{10,11... | collective-permute-start | bytes 1843208 | tf_op jit(solution)/shard_map/ppermute | solution.py:636
  136.5 81.5 %reduce-scatter.10.cloned.1.call-start = ((), (), s32[]{:S(2)}) async-start(), calls=%async_computation.6 | async-start | bytes 2949120
  161.3 93.1 %reduce-scatter.8.cloned.1.call-start = ((), (), s32[]{:S(2)}) async-start(), calls=%async_computation.5 | async-start | bytes 737280 | tf_op jit(solution)/shard_map/reduce_scatter | solution.py:692
  161.3 10.6 %collective-permute-start.10 = (bf16[2,4,2,24,3072]{4,3,1,2,0:T(8,128)(2,1)}, bf16[2,4,2,24,3072]{4,3,1,2,0:T(8,128)(2,1)}, u32[]{:S(2)}, u32[]{:S(2)}) collective-permute-start(bf16[2,4,2,24,3072]{4,3,1,2,0:T(8,128)(2,1)} %copy_bitcast_fusion.1), channel_id=1, source_target_pairs={{0,1},{1,0},{2,3},{3,2},{4,5},{5,4},{6,7},{7,6},{8,9},{9,8},{10,11... | collective-permute-start | bytes 7077896 | tf_op jit(solution)/shard_map/ppermute | solution.py:636
  176.1 32.2 %collective-permute-start.11 = (bf16[4,24,3072]{2,1,0:T(8,128)(2,1)}, bf16[4,24,3072]{2,1,0:T(8,128)(2,1)}, u32[]{:S(2)}, u32[]{:S(2)}) collective-permute-start(bf16[4,24,3072]{2,1,0:T(8,128)(2,1)} %get-tuple-element.159), channel_id=1, source_target_pairs={{0,2},{2,0},{16,18},{18,16},{1,3},{3,1},{17,19},{19,17},{4,6},{6,4... | collective-permute-start | bytes 1769480 | tf_op jit(solution)/shard_map/ppermute | solution.py:645
  177.6 30.7 %collective-permute-start.12 = (bf16[4,24,3072]{2,1,0:T(8,128)(2,1)}, bf16[4,24,3072]{2,1,0:T(8,128)(2,1)}, u32[]{:S(2)}, u32[]{:S(2)}) collective-permute-start(bf16[4,24,3072]{2,1,0:T(8,128)(2,1)} %get-tuple-element.158), channel_id=1, source_target_pairs={{0,16},{2,18},{16,0},{18,2},{1,17},{3,19},{17,1},{19,3},{4,20},{6,... | collective-permute-start | bytes 1769480 | tf_op jit(solution)/shard_map/ppermute | solution.py:645
  178.1 39.9 %collective-permute-start.13 = (bf16[4,24,3072]{2,1,0:T(8,128)(2,1)}, bf16[4,24,3072]{2,1,0:T(8,128)(2,1)}, u32[]{:S(2)}, u32[]{:S(2)}) collective-permute-start(bf16[4,24,3072]{2,1,0:T(8,128)(2,1)} %get-tuple-element.157), channel_id=1, source_target_pairs={{0,18},{2,16},{16,2},{18,0},{1,19},{3,17},{17,3},{19,1},{4,22},{6,... | collective-permute-start | bytes 1769480 | tf_op jit(solution)/shard_map/ppermute | solution.py:645
  227.7 21.2 %collective-permute-start.16 = (bf16[1,4,2,24,1536]{4,3,1,2,0:T(8,128)(2,1)}, bf16[1,4,2,24,1536]{4,3,1,2,0:T(8,128)(2,1)}, u32[]{:S(2)}, u32[]{:S(2)}) collective-permute-start(bf16[1,4,2,24,1536]{4,3,1,2,0:T(8,128)(2,1)} %fusion.1), channel_id=1, source_target_pairs={{0,16},{2,18},{16,0},{18,2},{1,17},{3,19},{17,1},{19,3},{4,20},{6,... | collective-permute-start | bytes 1769480 | tf_op jit(solution)/shard_map/ppermute | solution.py:645
  230.5 18.4 %collective-permute-start.15 = (bf16[2,4,1,24,1664]{4,3,1,2,0:T(8,128)(2,1)}, bf16[2,4,1,24,1664]{4,3,1,2,0:T(8,128)(2,1)S(1)}, u32[]{:S(2)}, u32[]{:S(2)}) collective-permute-start(bf16[2,4,1,24,1664]{4,3,1,2,0:T(8,128)(2,1)} %fusion), channel_id=1, source_target_pairs={{0,2},{2,0},{16,18},{18,16},{1,3},{3,1},{17,19},{19,17},{4,6},{6,4... | collective-permute-start | bytes 1916936 | tf_op jit(solution)/shard_map/ppermute | solution.py:645
  232.9 12.7 %collective-permute-start.17 = (bf16[24,3072]{1,0:T(8,128)(2,1)}, bf16[24,3072]{1,0:T(8,128)(2,1)}, u32[]{:S(2)}, u32[]{:S(2)}) collective-permute-start(bf16[24,3072]{1,0:T(8,128)(2,1)} %get-tuple-element.167), channel_id=1, source_target_pairs={{0,4},{4,8},{8,12},{12,0},{1,5},{5,9},{9,13},{13,1},{2,6},{6,10},{... | collective-permute-start | bytes 442376 | tf_op jit(solution)/shard_map/ppermute | solution.py:649
  233.3 15.6 %collective-permute-start.18 = (bf16[24,3072]{1,0:T(8,128)(2,1)}, bf16[24,3072]{1,0:T(8,128)(2,1)}, u32[]{:S(2)}, u32[]{:S(2)}) collective-permute-start(bf16[24,3072]{1,0:T(8,128)(2,1)} %get-tuple-element.166), channel_id=1, source_target_pairs={{0,8},{4,12},{8,0},{12,4},{1,9},{5,13},{9,1},{13,5},{2,10},{6,14},... | collective-permute-start | bytes 442376 | tf_op jit(solution)/shard_map/ppermute | solution.py:649
  235.7 13.2 %collective-permute-start.19 = (bf16[24,3072]{1,0:T(8,128)(2,1)S(1)}, bf16[24,3072]{1,0:T(8,128)(2,1)}, u32[]{:S(2)}, u32[]{:S(2)}) collective-permute-start(bf16[24,3072]{1,0:T(8,128)(2,1)S(1)} %get-tuple-element.165), channel_id=1, source_target_pairs={{0,12},{4,0},{8,4},{12,8},{1,13},{5,1},{9,5},{13,9},{2,14},{6,2},{... | collective-permute-start | bytes 442376 | tf_op jit(solution)/shard_map/ppermute | solution.py:649
  250.1 11.2 %collective-permute-start.20 = (bf16[1,4,1,24,1664]{4,3,1,2,0:T(8,128)(2,1)S(1)}, bf16[1,4,1,24,1664]{4,3,1,2,0:T(8,128)(2,1)S(1)}, u32[]{:S(2)}, u32[]{:S(2)}) collective-permute-start(bf16[1,4,1,24,1664]{4,3,1,2,0:T(8,128)(2,1)S(1)} %fusion.7), channel_id=1, source_target_pairs={{0,16},{2,18},{16,0},{18,2},{1,17},{3,19},{17,1},{19,3},{4,20},{6,... | collective-permute-start | bytes 958472 | tf_op jit(solution)/shard_map/ppermute | solution.py:645
  268.3 10.6 %collective-permute-start.23 = (bf16[24,3200]{1,0:T(8,128)(2,1)S(1)}, bf16[24,3200]{1,0:T(8,128)(2,1)S(1)}, u32[]{:S(2)}, u32[]{:S(2)}) collective-permute-start(bf16[24,3200]{1,0:T(8,128)(2,1)S(1)} %get-tuple-element.164), channel_id=1, source_target_pairs={{0,8},{4,12},{8,0},{12,4},{1,9},{5,13},{9,1},{13,5},{2,10},{6,14},... | collective-permute-start | bytes 460808 | tf_op jit(solution)/shard_map/ppermute | solution.py:649
  (18 other events, 98.2 us)
Sparse Core Ops, SparseCore 0:
  11.5 94.2 all-gather.1
  136.7 15.3 reduce-scatter.5
  161.4 51.6 reduce-scatter.9
  220.8 23.9 reduce-scatter.7
where the time goes:
time: 290 us; the launch traced here: 289 us
  Pallas kernels  138 us (48%)
  waiting for transfers between devices  72.9 us (25%)
  starting transfers between devices  30.1 us (10%)
  other arithmetic  20.3 us (7%)
  between operations  14 us (5%)
  local copies, waits for them, and re-layouts  13.3 us (5%)
    ppermute x10, waiting for transfers between devices, to_plane(): return lax.ppermute(array, ('dp', 'side'), pairs)  51.5 us
    pallas_call x1, Pallas kernels, attention_forward(): pl.pallas_call(attention_forward_kernel, grid=(seqs, GROUPS), in_specs=[r...  30.7 us
    pallas_call x1, Pallas kernels, attention_backward(): pl.pallas_call(attention_backward_kernel, grid=(GROUPS, seqs), in_specs=[...  27.8 us
    pallas_call x1, Pallas kernels, ffn_forward(): pl.pallas_call(lambda *refs: ffn_forward_kernel(unit, *refs), grid=(2 * C...  27.6 us
    pallas_call x1, Pallas kernels, ffn_backward(): pl.pallas_call(lambda *refs: ffn_backward_kernel(unit, *refs), grid=(CHUN...  21.2 us
    ppermute x9, waiting for transfers between devices, to_line(): lax.ppermute(array, 'line', [(i, (i + shift) % count) for i in range(coun...  17.9 us
    ppermute x9, starting transfers between devices, to_line(): lax.ppermute(array, 'line', [(i, (i + shift) % count) for i in range(coun...  17.3 us
    ppermute x10, starting transfers between devices, to_plane(): return lax.ppermute(array, ('dp', 'side'), pairs)  12.2 us
  transfers between devices with their start and end apart: 29, of which 12 were waited for; matrix products, arithmetic and copies ran while one was open for 8% of the time, Pallas kernels for 37%

commit v1 on v0

--- a/solution.py
+++ b/solution.py
@@ -59,7 +59,7 @@
 
 def attention_forward_kernel(
     x_ref, w_ref, wout_ref, vec_ref, seg_ref,
-    qkv_ref, ctx_ref, probs_ref, xt_ref, h1_ref, n1_ref, n1low_ref, n1t_ref, mask_ref,
+    qkv_ref, ctx_ref, probs_ref, xt_ref, n_ref, inverse_ref, n1low_ref, n1t_ref, mask_ref, h1_ref,
 ):
     group = pl.program_id(1)
     x = x_ref[...]
@@ -101,10 +101,10 @@
         @pl.loop(0, SEQ // ROWS)
         def _(i):
             rows = pl.ds(pl.multiple_of(i * ROWS, ROWS), ROWS)
-            n, _ = norm_parts(h1_ref[rows, :])
-            n1 = n * vec_ref[3:4, :] + vec_ref[4:5, :]
-            n1_ref[rows, :] = n1
-            n1low_ref[rows, :] = n1.astype(LOW)
+            n, inverse = norm_parts(h1_ref[rows, :])
+            n_ref[rows, :] = n
+            inverse_ref[rows, :] = jnp.broadcast_to(inverse, (ROWS, PAIR))
+            n1low_ref[rows, :] = (n * vec_ref[3:4, :] + vec_ref[4:5, :]).astype(LOW)
 
         n1t_ref[...] = jnp.transpose(n1low_ref[...])
 
@@ -129,7 +129,7 @@
             pl.BlockSpec((1, 1, GROUP // HEAD_DIM, SEQ, SEQ), lambda b, g: (b, g, 0, 0, 0)),
             pl.BlockSpec((1, D, SEQ), lambda b, g: (b, 0, 0)),
             row,
-            row,
+            pl.BlockSpec((SEQ, PAIR), lambda b, g: (b, 0)),
             row,
             pl.BlockSpec((D, SEQ), lambda b, g: (0, b)),
         ],
@@ -139,11 +139,11 @@
             like((seqs, GROUPS, GROUP // HEAD_DIM, SEQ, SEQ), LOW),
             like((seqs, D, SEQ), LOW),
             like((rows, D), F32),
-            like((rows, D), F32),
+            like((rows, PAIR), F32),
             like((rows, D), LOW),
             like((D, rows), LOW),
         ],
-        scratch_shapes=[pltpu.VMEM((SEQ, SEQ), F32)],
+        scratch_shapes=[pltpu.VMEM((SEQ, SEQ), F32), pltpu.VMEM((SEQ, D), F32)],
         compiler_params=pltpu.CompilerParams(vmem_limit_bytes=VMEM),
         cost_estimate=cost(rows * (8 * D * D + 4 * D * SEQ), 36 * MIB, rows * SEQ * HEADS),
         name="attention_forward",
@@ -151,8 +151,8 @@
 
 
 def attention_backward_kernel(
-    xt_ref, qkv_ref, ctx_ref, dctx_ref, probs_ref, vec_in_ref, gw_in_ref,
-    gw_ref, dqkv_ref, vec_ref,
+    unit, core_ref, xt_ref, qkv_ref, ctx_ref, dctx_ref, probs_ref, vec_in_ref, keep_in_ref, send_in_ref,
+    keep_ref, send_ref, dqkv_ref, vec_ref,
     ds_ref, acc_ref,
 ):
     row, seqs = pl.program_id(1), pl.num_programs(1)
@@ -213,17 +213,18 @@
 
     @pl.when(row == seqs - 1)
     def _():
-        gw_ref[...] = acc_ref[...].astype(LOW)
-
-
-def attention_backward(xt, qkv, ctx, probs, dctx, table, gw):
+        keep_ref[...], send_ref[...] = split_cores(acc_ref[...], core_ref[0], unit)
+
+
+def attention_backward(unit, core, xt, qkv, ctx, probs, dctx, table, keep, send):
     rows = ctx.shape[0]
     seqs = rows // SEQ
     mine = lambda g, b: (b, g)
     return pl.pallas_call(
-        attention_backward_kernel,
+        lambda *refs: attention_backward_kernel(unit, *refs),
         grid=(GROUPS, seqs),
         in_specs=[
+            pl.BlockSpec(memory_space=pltpu.SMEM),
             pl.BlockSpec((1, D, SEQ), lambda g, b: (b, 0, 0)),
             pl.BlockSpec((SEQ, TRIO), mine),
             pl.BlockSpec((SEQ, GROUP), mine),
@@ -231,30 +232,32 @@
             pl.BlockSpec((1, 1, GROUP // HEAD_DIM, SEQ, SEQ), lambda g, b: (b, g, 0, 0, 0)),
             pl.BlockSpec((8, GROUP), lambda g, b: (0, g)),
             pl.BlockSpec(memory_space=pl.ANY),
+            pl.BlockSpec(memory_space=pl.ANY),
         ],
         out_specs=[
-            pl.BlockSpec((D, TRIO), lambda g, b: (0, 1 + g)),
+            pl.BlockSpec((D // 2, TRIO), lambda g, b: (0, 1 + g)),
+            pl.BlockSpec((D // 2, TRIO), lambda g, b: (0, 1 + g)),
             pl.BlockSpec((SEQ, TRIO), mine),
             pl.BlockSpec((8, GROUP), lambda g, b: (0, g)),
         ],
-        out_shape=[like((D, SET), LOW), like((rows, 3 * D), LOW), like((8, D), F32)],
-        input_output_aliases={5: 2, 6: 0},
+        out_shape=[like((D // 2, SET), LOW)] * 2 + [like((rows, 3 * D), LOW), like((8, D), F32)],
+        input_output_aliases={6: 3, 7: 0, 8: 1},
         scratch_shapes=[pltpu.VMEM((2, SEQ, SEQ), LOW), pltpu.VMEM((D, TRIO), F32)],
         compiler_params=pltpu.CompilerParams(vmem_limit_bytes=VMEM),
         cost_estimate=cost(rows * (6 * D * D + 8 * D * SEQ), 36 * MIB, 0),
         name="attention_backward",
-    )(xt, qkv, ctx, dctx, probs, table, gw)
-
-
-def input_grad_kernel(dh1_ref, dqkv_ref, *refs):
-    total = dh1_ref[...]
+    )(core, xt, qkv, ctx, dctx, probs, table, keep, send)
+
+
+def input_grad_kernel(da_ref, dqkv_ref, *refs):
+    total = da_ref[...].astype(F32)
     for g in range(GROUPS):
         total += mm_t(dqkv_ref[:, g * TRIO : (g + 1) * TRIO], refs[g][...])
     refs[GROUPS][...] = total.astype(LOW)
 
 
-def input_grad(dh1, dqkv, weights):
-    rows = dh1.shape[0]
+def input_grad(da, dqkv, weights):
+    rows = da.shape[0]
     return pl.pallas_call(
         input_grad_kernel,
         grid=(rows // ROWS,),
@@ -268,7 +271,7 @@
         compiler_params=pltpu.CompilerParams(vmem_limit_bytes=VMEM),
         cost_estimate=cost(6 * rows * D * D, 13 * MIB, 0),
         name="input_grad",
-    )(dh1, dqkv, *[weights] * GROUPS)
+    )(da, dqkv, *[weights] * GROUPS)
 
 
 def norm_parts(hidden):
@@ -306,14 +309,14 @@
 
 
 def ffn_forward_kernel(
-    unit, n1low_ref, outer_ref, wi_ref, bi_ref, vec_ref, n1_hbm, cot_hbm,
+    unit, n1low_ref, outer_ref, wi_ref, bi_ref, vec_ref, n_hbm, cot_hbm,
     slope_ref, gwo_ref, sums_ref, out_hbm, db_hbm, dh2_hbm,
-    n1_ref, cot_ref, h2_ref, wo_ref, act_ref, out_ref, db_ref, dh2_ref, sem,
+    n_ref, cot_ref, h2_ref, wo_ref, act_ref, out_ref, db_ref, dh2_ref, sem,
 ):
     step = pl.program_id(0)
     tiles = [slice(i, i + ROWS) for i in range(0, h2_ref.shape[0], ROWS)]
     loads = [
-        pltpu.make_async_copy(n1_hbm, n1_ref, sem.at[0]),
+        pltpu.make_async_copy(n_hbm, n_ref, sem.at[0]),
         pltpu.make_async_copy(cot_hbm, cot_ref, sem.at[1]),
     ]
     stores = [
@@ -349,7 +352,9 @@
         @pl.loop(0, h2_ref.shape[0] // ROWS, unroll=2)
         def _(i):
             rows = pl.ds(pl.multiple_of(i * ROWS, ROWS), ROWS)
-            n, inverse = norm_parts(h2_ref[rows, :] + (n1_ref[rows, :] + vec_ref[5:6, :]))
+            n, inverse = norm_parts(
+                h2_ref[rows, :] + (n_ref[rows, :] * vec_ref[3:4, :] + vec_ref[4:5, :] + vec_ref[5:6, :])
+            )
             out_ref[rows, :] = (n * gain + shift).astype(LOW)
             cot = cot_ref[rows, :].astype(F32)
             dh2 = norm_back(cot, gain, n, inverse)
@@ -379,8 +384,8 @@
             copy.wait()
 
 
-def ffn_forward(unit, n1, n1low, cot, rest, b_inner, table, sizes=None):
-    rows = n1.shape[0]
+def ffn_forward(unit, normed, n1low, cot, rest, b_inner, table, sizes=None):
+    rows = normed.shape[0]
     last = CHUNKS - 1
     now = lambda c: jnp.minimum(c, last)
     then = lambda c: jnp.maximum(c - CHUNKS, 0)
@@ -440,21 +445,36 @@
         compiler_params=pltpu.CompilerParams(vmem_limit_bytes=VMEM),
         cost_estimate=cost(6 * rows * D * FF, 34 * MIB, rows * FF),
         name="ffn_forward",
-    )(n1low, rest, rest, b_inner, table, n1, cot)
+    )(n1low, rest, rest, b_inner, table, normed, cot)
+
+
+def split_cores(grad, core, unit):
+    rows = range(0, grad.shape[0], 2 * unit)
+    even = jnp.concatenate([grad[i : i + unit] for i in rows], axis=0)
+    odd = jnp.concatenate([grad[i + unit : i + 2 * unit] for i in rows], axis=0)
+    return jnp.where(core == 0, even, odd).astype(LOW), jnp.where(core == 0, odd, even).astype(LOW)
 
 
 def ffn_backward_kernel(
-    unit, n1t_ref, slope_ref, db_ref, outer_ref, wi_ref,
-    gwi_ref, gbi_ref, dn1_ref,
-    dpre_ref, wo_ref,
+    unit, core_ref, n1t_ref, slope_ref, db_ref, outer_ref, wi_ref, dh2_hbm,
+    keep_ref, send_ref, gbi_ref, dn1_ref,
+    dpre_ref, wo_ref, dh2_ref, sem,
 ):
     step = pl.program_id(0)
     tiles = [slice(i, i + ROWS) for i in range(0, db_ref.shape[0], ROWS)]
     order_outer(outer_ref, wo_ref, unit)
 
+    load = pltpu.make_async_copy(dh2_hbm, dh2_ref, sem)
+
     @pl.when(step == 0)
     def _():
+        load.start()
         dn1_ref[...] = jnp.zeros_like(dn1_ref)
+
+    @pl.when(step == CHUNKS - 1)
+    def _():
+        load.wait()
+        dn1_ref[...] += dh2_ref[...]
 
     bias = jnp.zeros((1, CHUNK), F32)
     for rows in tiles:
@@ -463,49 +483,57 @@
         bias += column_sum(dpre.astype(F32))
         dn1_ref[rows, :] += mm_t(dpre, wi_ref[...])
     gbi_ref[...] = bias
-    gwi_ref[...] = mm(n1t_ref[...], dpre_ref[...]).astype(LOW)
-
-
-def ffn_backward(unit, n1t, slope, db, rest):
+    keep_ref[...], send_ref[...] = split_cores(mm(n1t_ref[...], dpre_ref[...]), core_ref[0], unit)
+
+
+def ffn_backward(unit, core, n1t, slope, db, dh2, rest):
     rows = db.shape[0]
     once = pl.BlockSpec((rows, D), lambda c: (0, 0), pipeline_mode=pl.Buffered(1))
     return pl.pallas_call(
         lambda *refs: ffn_backward_kernel(unit, *refs),
         grid=(CHUNKS,),
         in_specs=[
+            pl.BlockSpec(memory_space=pltpu.SMEM),
             pl.BlockSpec((D, rows), lambda c: (0, 0), pipeline_mode=pl.Buffered(1)),
             pl.BlockSpec((rows, CHUNK), lambda c: (0, c)),
             once,
             pl.BlockSpec((D // CHUNKS, FF), lambda c: (c, 0)),
             pl.BlockSpec((D, CHUNK), lambda c: (0, CHUNKS + c)),
+            pl.BlockSpec(memory_space=pl.ANY),
         ],
         out_specs=[
-            pl.BlockSpec((D, CHUNK), lambda c: (0, c)),
+            pl.BlockSpec((D // 2, CHUNK), lambda c: (0, c)),
+            pl.BlockSpec((D // 2, CHUNK), lambda c: (0, c)),
             pl.BlockSpec((1, CHUNK), lambda c: (0, c)),
             pl.BlockSpec((rows, D), lambda c: (0, 0)),
         ],
-        out_shape=[like((D, FF), LOW), like((1, FF), F32), like((rows, D), F32)],
-        scratch_shapes=[pltpu.VMEM((rows, CHUNK), LOW), pltpu.VMEM((CHUNK, D), LOW)],
+        out_shape=[like((D // 2, FF), LOW)] * 2 + [like((1, FF), F32), like((rows, D), F32)],
+        scratch_shapes=[
+            pltpu.VMEM((rows, CHUNK), LOW),
+            pltpu.VMEM((CHUNK, D), LOW),
+            pltpu.VMEM((rows, D), F32),
+            pltpu.SemaphoreType.DMA,
+        ],
         compiler_params=pltpu.CompilerParams(vmem_limit_bytes=VMEM),
         cost_estimate=cost(6 * rows * D * FF, 30 * MIB, 0),
         name="ffn_backward",
-    )(n1t, slope, db, rest, rest)
+    )(core, n1t, slope, db, rest, rest, dh2)
 
 
 def norm_backward_kernel(
-    wout_ref, vec_ref, sums_in_ref, h1_hbm, dn1_hbm, dh2_hbm, ctx_hbm,
-    gw_ref, sums_ref, dctx_hbm, dh1_hbm,
-    h1_ref, dn1_ref, dh2_ref, ctx_ref, da_ref, dctx_ref, dh1_ref, load_sem, store_sem,
+    unit, core_ref, wout_ref, vec_ref, sums_in_ref, n_hbm, inverse_hbm, dn1_hbm, ctx_hbm,
+    keep_ref, send_ref, sums_ref, dctx_hbm, da_hbm,
+    n_ref, inverse_ref, dn1_ref, ctx_ref, da_ref, dctx_ref, load_sem, store_sem,
 ):
-    tiles = [slice(i, i + ROWS) for i in range(0, h1_ref.shape[0], ROWS)]
-    pairs = ((h1_hbm, h1_ref), (dn1_hbm, dn1_ref), (dh2_hbm, dh2_ref), (ctx_hbm, ctx_ref))
+    tiles = [slice(i, i + ROWS) for i in range(0, n_ref.shape[0], ROWS)]
+    pairs = ((n_hbm, n_ref), (inverse_hbm, inverse_ref), (dn1_hbm, dn1_ref), (ctx_hbm, ctx_ref))
     loads = [
         [pltpu.make_async_copy(a.at[rows, :], b.at[rows, :], load_sem.at[i, j]) for j, (a, b) in enumerate(pairs)]
         for i, rows in enumerate(tiles)
     ]
     stores = [
         [
-            pltpu.make_async_copy(dh1_ref.at[rows, :], dh1_hbm.at[rows, :], store_sem.at[i, 0]),
+            pltpu.make_async_copy(da_ref.at[rows, :], da_hbm.at[rows, :], store_sem.at[i, 0]),
             pltpu.make_async_copy(dctx_ref.at[rows, :], dctx_hbm.at[rows, :], store_sem.at[i, 1]),
         ]
         for i, rows in enumerate(tiles)
@@ -521,18 +549,16 @@
         if i > 0:
             dctx_ref[tiles[i - 1], :] = mm_t(da_ref[tiles[i - 1], :], wout_ref[...]).astype(LOW)
         if rows is not None:
-            n, inverse = norm_parts(h1_ref[rows, :])
-            dn1 = dn1_ref[rows, :] + dh2_ref[rows, :]
-            dh1 = norm_back(dn1, vec_ref[3:4, :], n, inverse)
-            dh1_ref[rows, :] = dh1
-            da = dh1.astype(LOW)
+            n = n_ref[rows, :]
+            dn1 = dn1_ref[rows, :]
+            da = norm_back(dn1, vec_ref[3:4, :], n, inverse_ref[rows, 0:1]).astype(LOW)
             da_ref[rows, :] = da
             new = (column_sum(da.astype(F32)), column_sum(dn1 * n), column_sum(dn1))
             sums = [a + b for a, b in zip(sums, new)]
             stores[i][0].start()
         if i > 0:
             stores[i - 1][1].start()
-    gw_ref[...] = t_mm(ctx_ref[...], da_ref[...]).astype(LOW)
+    keep_ref[...], send_ref[...] = split_cores(t_mm(ctx_ref[...], da_ref[...]), core_ref[0], unit)
     sums_ref[...] = sums_in_ref[...]
     for i in range(3):
         sums_ref[2 + i : 3 + i, :] = sums[i]
@@ -541,32 +567,38 @@
             copy.wait()
 
 
-def norm_backward(h1, dn1, dh2, ctx, weights, table, sums):
-    rows = h1.shape[0]
+def norm_backward(unit, core, normed, inverse, dn1, ctx, weights, table, sums):
+    rows = normed.shape[0]
     eight = pl.BlockSpec((8, D), lambda i: (0, 0))
-    square = pl.BlockSpec((D, D), lambda i: (0, 0))
+    half = pl.BlockSpec((D // 2, D), lambda i: (0, 0))
     anywhere = pl.BlockSpec(memory_space=pl.ANY)
     return pl.pallas_call(
-        norm_backward_kernel,
+        lambda *refs: norm_backward_kernel(unit, *refs),
         grid=(1,),
-        in_specs=[square, eight, eight] + [anywhere] * 4,
-        out_specs=[square, eight, anywhere, anywhere],
-        out_shape=[like((D, SET), LOW), like((8, D), F32), like((rows, D), LOW), like((rows, D), F32)],
+        in_specs=[
+            pl.BlockSpec(memory_space=pltpu.SMEM),
+            pl.BlockSpec((D, D), lambda i: (0, 0)),
+            eight,
+            eight,
+        ]
+        + [anywhere] * 4,
+        out_specs=[half, half, eight, anywhere, anywhere],
+        out_shape=[like((D // 2, SET), LOW)] * 2
+        + [like((8, D), F32), like((rows, D), LOW), like((rows, D), LOW)],
         scratch_shapes=[
             pltpu.VMEM((rows, D), F32),
-            pltpu.VMEM((rows, D), F32),
+            pltpu.VMEM((rows, PAIR), F32),
             pltpu.VMEM((rows, D), F32),
             pltpu.VMEM((rows, D), LOW),
             pltpu.VMEM((rows, D), LOW),
             pltpu.VMEM((rows, D), LOW),
-            pltpu.VMEM((rows, D), F32),
             pltpu.SemaphoreType.DMA((rows // ROWS, 4)),
             pltpu.SemaphoreType.DMA((rows // ROWS, 2)),
         ],
         compiler_params=pltpu.CompilerParams(vmem_limit_bytes=VMEM),
         cost_estimate=cost(4 * rows * D * D, 17 * MIB, 0),
         name="norm_backward",
-    )(weights, table, sums, h1, dn1, dh2, ctx)
+    )(core, weights, table, sums, normed, inverse, dn1, ctx)
 
 
 def after(values, *others):
@@ -603,9 +635,11 @@
     shapes = [like((unit, SET), LOW), like((unit, 2 * FF), LOW)]
     return pl.pallas_call(
         pack_kernel,
+        grid=(1,),
         in_specs=[whole(a) for a in args],
         out_specs=[whole(a) for a in shapes],
         out_shape=shapes,
+        compiler_params=pltpu.CompilerParams(vmem_limit_bytes=VMEM),
         name="pack",
     )(*args)
 
@@ -619,9 +653,11 @@
     shape = like((len(pieces), *pieces[0].shape), pieces[0].dtype)
     return pl.pallas_call(
         stack_kernel,
-        in_specs=[whole(a) for a in pieces],
+        grid=(1,),
+        in_specs=[pl.BlockSpec(memory_space=pltpu.VMEM)] * len(pieces),
         out_specs=whole(shape),
         out_shape=shape,
+        compiler_params=pltpu.CompilerParams(vmem_limit_bytes=8 * MIB),
         name="stack",
     )(*pieces)
 
@@ -656,6 +692,8 @@
         there = [self.to_core(a) for a in here]
         place = jnp.stack([self.dp, self.line, self.side, self.core]).astype(jnp.int32)
         pieces = here + there
+
+        wide = 5 * PAIR
 
         def kernel(place_ref, *refs):
             out_ref = refs[-1]
@@ -668,7 +706,6 @@
                     along = lax.rem(place_ref[1] + lines - s, lines)
                     out_ref[((dp * lines + along) * sides + side) * 2 + core] = refs[i][s]
 
-        wide = 5 * PAIR
         count = dps * lines * sides * 2
         return pl.pallas_call(
             kernel,
@@ -682,79 +719,41 @@
         )(place, *pieces).reshape(-1, columns)
 
 
-    def core_sum(self, grad):
-        return lax.psum_scatter(grad, "core", scatter_dimension=0)
-
-    def plane_sum(self, grad):
-        return lax.psum_scatter(grad.reshape(-1, *grad.shape[2:]), ("dp", "side"), scatter_dimension=0)
+    def chips_sum(self, grad):
+        return lax.psum_scatter(grad.reshape(-1, *grad.shape[3:]), ("core", "dp", "side"), scatter_dimension=0)
 
     def line_sum(self, grad):
         return lax.psum_scatter(grad, "line", scatter_dimension=0)
+
+    def join_cores(self, keep, send, unit):
+        keep, send = (part.reshape(-1, 1, unit, part.shape[1]) for part in (keep, send))
+        mine = self.core == 0
+        pair = [jnp.where(mine, keep, send), jnp.where(mine, send, keep)]
+        return jnp.concatenate(pair, axis=1).reshape(-1, keep.shape[3])
 
 
     def plane_messages(self, grad, got):
         dps, _, sides, _ = self.sizes
         return [
-            self.block(
-                grad, got, lax.rem(self.dp + a, dps), lax.rem(self.side + b, sides), (0, grad.shape[1])
-            )[0, :, 0].astype(LOW)
-            for a, b in self.offsets
+            self.block(grad, got, lax.rem(self.dp + a, dps), lax.rem(self.side + b, sides)).astype(LOW)
+            for a, b in self.offsets[1:]
         ]
 
     def plane_exchange(self, messages):
-        return messages[:1] + [self.to_plane(m, o) for m, o in zip(messages[1:], self.offsets[1:])]
-
-    def plane_done(self, parts):
-        return self.along_line(sum(p.astype(F32) for p in parts).astype(LOW))
-
-    def block(self, grad, got, dp, side, columns):
+        return [self.to_plane(m, o) for m, o in zip(messages, self.offsets[1:])]
+
+    def plane_done(self, grad, got, parts):
+        total = self.block(grad, got, self.dp, self.side)
+        return self.along_line((total + sum(p.astype(F32) for p in parts)).astype(LOW))
+
+    def block(self, grad, got, dp, side):
         dps, lines, sides, _ = self.sizes
-        parts = grad.reshape(*self.sizes, -1, grad.shape[1])
-        unit, (first, last) = parts.shape[4], columns
-        start = (0 if dp is None else dp, 0, 0 if side is None else side)
-        size = (dps if dp is None else 1, lines, sides if side is None else 1)
-        mine = lax.dynamic_slice(parts, (*start, self.core, 0, first), (*size, 1, unit, last - first))
-        other = lax.dynamic_slice(got, (*start, 0, first), (*size, unit, last - first))
-        return mine[:, :, :, 0].astype(F32) + other.astype(F32)
-
-    def halves(self, grad):
-        columns = grad.shape[1]
-        middle = -(-columns // (2 * PAIR)) * PAIR
-        return (0, middle), (middle, columns)
-
-    def core_message(self, grad):
-        parts = grad.reshape(*self.sizes, -1, grad.shape[1])
-        return lax.dynamic_index_in_dim(parts, 1 - self.core, 3, keepdims=False)
-
-    def first_messages(self, grad, got):
-        one, two = self.halves(grad)
-        return (
-            self.block(grad, got, None, 1 - self.side, one).astype(LOW),
-            self.block(grad, got, 1 - self.dp, None, two).astype(LOW),
-        )
-
-    def first_exchange(self, messages):
-        return self.to_plane(messages[0], (0, 1)), self.to_plane(messages[1], (1, 0))
-
-    def second_messages(self, grad, got, more):
-        one, two = self.halves(grad)
-        a = self.block(grad, got, 1 - self.dp, self.side, one)
-        b = self.block(grad, got, self.dp, 1 - self.side, two)
-        a += lax.dynamic_slice_in_dim(more[0], 1 - self.dp, 1, 0).astype(F32)
-        b += lax.dynamic_slice_in_dim(more[1], 1 - self.side, 1, 2).astype(F32)
-        return a.astype(LOW), b.astype(LOW)
-
-    def second_exchange(self, messages):
-        return self.to_plane(messages[0], (1, 0)), self.to_plane(messages[1], (0, 1))
-
-    def line_messages(self, grad, got, more, most):
-        one, two = self.halves(grad)
-        a = self.block(grad, got, self.dp, self.side, one) + most[0].astype(F32)
-        b = self.block(grad, got, self.dp, self.side, two) + most[1].astype(F32)
-        a += lax.dynamic_slice_in_dim(more[0], self.dp, 1, 0).astype(F32)
-        b += lax.dynamic_slice_in_dim(more[1], self.side, 1, 2).astype(F32)
-        total = jnp.concatenate([a[0, :, 0], b[0, :, 0]], axis=2).astype(LOW)
-        return self.along_line(total)
+        total = 0.0
+        for part in (grad, got):
+            part = part.reshape(dps, lines, sides, -1, grad.shape[1])
+            size = (1, lines, 1, *part.shape[3:])
+            total += lax.dynamic_slice(part, (dp, 0, side, 0, 0), size)[0, :, 0].astype(F32)
+        return total
 
     def along_line(self, total):
         lines = self.sizes[1]
@@ -782,9 +781,11 @@
     shapes = [like((unit, D), F32)] * 4 + [like((1, unit), F32)] * 8 + [like((1, CHUNKS * unit), F32)]
     outs = pl.pallas_call(
         lambda *refs: finish_kernel(len(parts), *refs),
-        in_specs=[whole(a) for a in parts],
+        grid=(1,),
+        in_specs=[pl.BlockSpec(memory_space=pltpu.VMEM)] * len(parts),
         out_specs=[whole(a) for a in shapes],
         out_shape=shapes,
+        compiler_params=pltpu.CompilerParams(vmem_limit_bytes=8 * MIB),
         name="finish",
     )(*parts)
     return outs[:4], [v.reshape(-1) for v in outs[4:]]
@@ -796,7 +797,7 @@
     inner = b_inner.reshape(count, 1, CHUNKS * unit)
     eight = jnp.pad(eight, ((0, 0), (0, 0), (0, PAIR - unit)))
     inner = jnp.pad(inner, ((0, 0), (0, unit - 9), (0, PAIR - CHUNKS * unit)))
-    return jnp.concatenate([eight, inner], axis=1).reshape(D, PAIR).astype(LOW)
+    return jnp.concatenate([eight, inner], axis=1).astype(LOW)
 
 
 def on_device(block_input, segment_ids, cotangent, *params):
@@ -828,18 +829,21 @@
         outer = outer.reshape(-1, CHUNKS, unit, D).transpose(0, 2, 1, 3).reshape(D, FF)
         rest = jnp.concatenate([outer, full[:, 4 * D :]], axis=1)
 
-    qkv, ctx, probs, xt, h1, n1, n1low, n1t = attention_forward(x, segment_ids, weights, table)
+    core = mesh.core[None].astype(jnp.int32)
+    qkv, ctx, probs, xt, normed, inverse, n1low, n1t = attention_forward(x, segment_ids, weights, table)
     slope, g_outer, sums, result, db, dh2 = ffn_forward(
-        unit, n1, n1low, cot, rest, b_inner, table, mesh.sizes if quick else None
+        unit, normed, n1low, cot, rest, b_inner, table, mesh.sizes if quick else None
     )
     if quick:
         db = after(db, g_outer)
-        g_outer = mesh.core_sum(g_outer)
-    g_inner, g_b_inner, dn1 = ffn_backward(unit, n1t, slope, db, rest)
+        g_outer = mesh.chips_sum(g_outer)
+    keep, send, g_b_inner, dn1 = ffn_backward(unit, core, n1t, slope, db, dh2, rest)
     if not quick:
-        late, sums, dctx, dh1 = norm_backward(h1, dn1, dh2, ctx, weights, table, sums)
-        late, dqkv, sums = attention_backward(xt, qkv, ctx, probs, dctx, sums, late)
-        dx = input_grad(dh1, dqkv, weights)
+        g_inner = mesh.join_cores(keep, send, unit)
+        keep, send, sums, dctx, da = norm_backward(unit, core, normed, inverse, dn1, ctx, weights, table, sums)
+        keep, send, dqkv, sums = attention_backward(unit, core, xt, qkv, ctx, probs, dctx, sums, keep, send)
+        late = mesh.join_cores(keep, send, unit)
+        dx = input_grad(da, dqkv, weights)
         wide = jnp.concatenate([late[:, : 4 * D], g_inner], axis=1)
         wide = lax.psum_scatter(wide, AXES, scatter_dimension=0, tiled=True).astype(F32)
         g_outer = lax.psum_scatter(g_outer, AXES, scatter_dimension=0, tiled=True).astype(F32)
@@ -853,29 +857,29 @@
         ]
         g_inner = wide[:, 4 * D :]
     else:
-        message = mesh.core_message(g_inner)
-        dn1, g_outer = after((dn1, g_outer), message)
-        g_outer = mesh.plane_sum(g_outer)
-        got = mesh.to_core(message)
-        late, sums, dctx, dh1 = norm_backward(h1, dn1, dh2, ctx, weights, table, sums)
-        got, sums = after((got, sums), dctx)
-        message = mesh.plane_messages(g_inner, got)
+        g_inner = keep
+        dn1 = after(dn1, send)
+        got = mesh.to_core(send)
+        keep, send, sums, dctx, da = norm_backward(unit, core, normed, inverse, dn1, ctx, weights, table, sums)
+        inner_got, sums = after((got, sums), dctx)
+        message = mesh.plane_messages(g_inner, inner_got)
         sums = after(sums, message)
         parts = mesh.plane_exchange(message)
-        late, dqkv, sums = attention_backward(xt, qkv, ctx, probs, dctx, sums, late)
-        late, parts, g_outer = after((late, parts, g_outer), dqkv)
+        late, send, dqkv, sums = attention_backward(unit, core, xt, qkv, ctx, probs, dctx, sums, keep, send)
+        late, send, parts, g_outer = after((late, send, parts, g_outer), dqkv)
         g_outer = mesh.line_sum(g_outer)
-        late = lax.dynamic_update_slice(late, vector_rows(sums, g_b_inner, count), (0, 4 * D))
-        message = mesh.core_message(late)
-        dqkv, parts = after((dqkv, parts), message)
-        lines = mesh.line_exchange(mesh.plane_done(parts))
-        got = mesh.to_core(message)
-        more = mesh.first_exchange(mesh.first_messages(late, got))
-        dx = input_grad(dh1, dqkv, weights)
-        more, g_inner = after((more, lines), dx)
-        most = mesh.second_exchange(mesh.second_messages(late, got, more))
-        most, g_outer = after((most, g_outer), dx)
-        message = mesh.line_messages(late, got, more, most)
+        vector = vector_rows(sums, g_b_inner, count).reshape(-1, 2, unit, PAIR)
+        at = (mesh.core, 1 - mesh.core)
+        vector = [lax.dynamic_index_in_dim(vector, i, 1, keepdims=False).reshape(-1, PAIR) for i in at]
+        late = lax.dynamic_update_slice(late, vector[0], (0, 4 * D))
+        send = lax.dynamic_update_slice(send, vector[1], (0, 4 * D))
+        dqkv, parts = after((dqkv, parts), (late, send))
+        lines = mesh.line_exchange(mesh.plane_done(g_inner, inner_got, parts))
+        got = mesh.to_core(send)
+        parts = mesh.plane_exchange(mesh.plane_messages(late, got))
+        dx = input_grad(da, dqkv, weights)
+        parts, g_inner, g_outer = after((parts, lines, g_outer), dx)
+        message = mesh.plane_done(late, got, parts)
         g_outer, g_inner = after((g_outer, g_inner), message)
         matrices, vectors = finish(mesh.line_exchange(message))
         g_outer = g_outer.astype(F32)

time: 290 us -> 271 us (0.934)
  waiting for transfers between devices: 72.9 us -> 65.3 us
  local copies, waits for them, and re-layouts: 13.3 us -> 6.8 us
  other arithmetic: 20.3 us -> 14.9 us
  Pallas kernels: 138 us -> 134 us
  starting transfers between devices: 30.1 us -> 34 us
    ppermute x10 -> x9, waiting for transfers between devices: 51.5 us -> 41.2 us  [to_plane(): return lax.ppermute(array, ('dp', 'side'), pairs)]
    ppermute x9, starting transfers between devices: 17.3 us -> 22.9 us  [to_line(): lax.ppermute(array, 'line', [(i, (i + shift) % count) for i in range(coun...]
    squeeze x2 -> x0, local copies, waits for them, and re-layouts: 5.13 us -> none  [core_message(): return lax.dynamic_index_in_dim(parts, 1 - self.core, 3, keepdims=False)]
    ppermute x9, waiting for transfers between devices: 17.9 us -> 21.5 us  [to_line(): lax.ppermute(array, 'line', [(i, (i + shift) % count) for i in range(coun...]
    pallas_call x5, Pallas kernels: 43.4 us -> 39.9 us  [the longest x1 27.9 us: attention_backward(): pl.pallas_call(lambda *refs: attention_backward_kernel(unit, *refs), grid...]
    squeeze x3 -> x0, other arithmetic: 3.29 us -> none  [the longest x2 2.57 us: line_messages(): total = jnp.concatenate([a[0, :, 0], b[0, :, 0]], axis=2).astype(LOW)]
    convert_element_type x6 -> x4, other arithmetic: 12.9 us -> 10.1 us  [the longest x2 5.66 us: plane_messages(): self.block(grad, got, lax.rem(self.dp + a, dps), lax.rem(self.side + b, s...]
    ppermute x10 -> x9, starting transfers between devices: 12.2 us -> 10.5 us  [to_plane(): return lax.ppermute(array, ('dp', 'side'), pairs)]
  transfers between devices with their start and end apart: 29 -> 27, of which waited for: 12 -> 11; matrix products, arithmetic and copies ran while one was open for 8% -> 6% of each run, Pallas kernels for 37% -> 39%
where the time goes in v1:
time: 271 us; the launch traced here: 269 us
  Pallas kernels  134 us (49%)
  waiting for transfers between devices  65.3 us (24%)
  starting transfers between devices  34 us (13%)
  other arithmetic  14.9 us (5%)
  between operations  14 us (5%)
  local copies, waits for them, and re-layouts  6.8 us (3%)
    ppermute x9, waiting for transfers between devices, to_plane(): return lax.ppermute(array, ('dp', 'side'), pairs)  41.2 us
    pallas_call x1, Pallas kernels, attention_forward(): pl.pallas_call(attention_forward_kernel, grid=(seqs, GROUPS), in_specs=[r...  30.2 us
    pallas_call x1, Pallas kernels, attention_backward(): pl.pallas_call(lambda *refs: attention_backward_kernel(unit, *refs), grid...  27.9 us
    pallas_call x1, Pallas kernels, ffn_forward(): pl.pallas_call(lambda *refs: ffn_forward_kernel(unit, *refs), grid=(2 * C...  27.9 us
    ppermute x9, starting transfers between devices, to_line(): lax.ppermute(array, 'line', [(i, (i + shift) % count) for i in range(coun...  22.9 us
    pallas_call x1, Pallas kernels, ffn_backward(): pl.pallas_call(lambda *refs: ffn_backward_kernel(unit, *refs), grid=(CHUN...  21.5 us
    ppermute x9, waiting for transfers between devices, to_line(): lax.ppermute(array, 'line', [(i, (i + shift) % count) for i in range(coun...  21.5 us
    ppermute x9, starting transfers between devices, to_plane(): return lax.ppermute(array, ('dp', 'side'), pairs)  10.5 us
  transfers between devices with their start and end apart: 27, of which 11 were waited for; matrix products, arithmetic and copies ran while one was open for 6% of the time, Pallas kernels for 39%

profile of v1, /device:TPU:0, one launch (start us, length us, event | category | flops | bytes accessed | tf_op | source)
XLA Modules:
  0.0 269.3 jit_solution(14356079952837055309)
XLA Ops:
  9.2 3.1 %collective-permute-start = (bf16[24,3200]{1,0:T(8,128)(2,1)}, bf16[24,3200]{1,0:T(8,128)(2,1)S(1)}, u32[]{:S(2)}, u32[]{:S(2)}) collective-permute-start(bf16[24,3200]{1,0:T(8,128)(2,1)} %get-tuple-element.87.refs_0_), channel_id=1, source_target_pairs={{0,4},{4,8},{8,12},{12,0},{1,5},{5,9},{9,13},{13,1},{2,6},{6,10},{... | collective-permute-start | bytes 460808 | tf_op jit(solution)/shard_map/ppermute | solution.py:685
  12.3 2.6 collective-permute-start.1
  16.2 3.2 %collective-permute-done.refs_1_ = bf16[24,3200]{1,0:T(8,128)(2,1)S(1)} collective-permute-done((bf16[24,3200]{1,0:T(8,128)(2,1)}, bf16[24,3200]{1,0:T(8,128)(2,1)S(1)}, u32[]{:S(2)}, u32[]{:S(2)}) %collective-permute-start) | collective-permute-done | bytes 153632 | tf_op jit(solution)/shard_map/ppermute | solution.py:685
  19.4 5.7 %collective-permute-done.1.refs_2_ = bf16[24,3200]{1,0:T(8,128)(2,1)S(1)} collective-permute-done((bf16[24,3200]{1,0:T(8,128)(2,1)}, bf16[24,3200]{1,0:T(8,128)(2,1)S(1)}, u32[]{:S(2)}, u32[]{:S(2)}) %collective-permute-start.1) | collective-permute-done | bytes 153632 | tf_op jit(solution)/shard_map/ppermute | solution.py:685
  29.7 13.2 %collective-permute-done.3.refs_1_ = bf16[4,24,3200]{2,1,0:T(8,128)(2,1)S(1)} collective-permute-done((bf16[4,24,3200]{2,1,0:T(8,128)(2,1)S(1)}, bf16[4,24,3200]{2,1,0:T(8,128)(2,1)S(1)}, u32[]{:S(2)}, u32[]{:S(2)}) %collective-permute-start.3) | collective-permute-done | bytes 614432 | tf_op jit(solution)/shard_map/ppermute | solution.py:681
  43.0 6.9 %collective-permute-done.4.refs_2_ = bf16[4,24,3200]{2,1,0:T(8,128)(2,1)S(1)} collective-permute-done((bf16[4,24,3200]{2,1,0:T(8,128)(2,1)S(1)}, bf16[4,24,3200]{2,1,0:T(8,128)(2,1)S(1)}, u32[]{:S(2)}, u32[]{:S(2)}) %collective-permute-start.4) | collective-permute-done | bytes 614432 | tf_op jit(solution)/shard_map/ppermute | solution.py:681
  49.9 14.6 %collective-permute-done.5.refs_3_ = bf16[4,24,3200]{2,1,0:T(8,128)(2,1)S(1)} collective-permute-done((bf16[4,24,3200]{2,1,0:T(8,128)(2,1)S(1)}, bf16[4,24,3200]{2,1,0:T(8,128)(2,1)S(1)}, u32[]{:S(2)}, u32[]{:S(2)}) %collective-permute-start.5) | collective-permute-done | bytes 614432 | tf_op jit(solution)/shard_map/ppermute | solution.py:681
  66.7 6.5 %place.1 = bf16[32,24,3200]{2,1,0:T(8,128)(2,1)} custom-call(s32[4]{0:T(128)} %pad_add_fusion.place_ref, bf16[4,24,3200]{2,1,0:T(8,128)(2,1)} %copy-done, bf16[4,24,3200]{2,1,0:T(8,128)(2,1)} %copy-done.4, bf16[4,24,3200]{2,1,0:T(8,128)(2,1)} %copy-done.5, bf16[4,24,3200]{2,1,0:T(8,128)(2,1)} %copy-done.6, bf16[4,24,3200]{2,1,0:T(8,128)(2,1)} %copy-done.7, ...), custom_call_target="tpu_custom_call" | custom-call | tf_op jit(solution)/shard_map/place/pallas_call | solution.py:710
  75.8 30.2 %attention_forward.1 = (bf16[1024,2304]{1,0:T(8,128)(2,1)}, bf16[1024,768]{1,0:T(8,128)(2,1)}, bf16[2,3,4,512,512]{4,3,2,1,0:T(8,128)(2,1)}, bf16[2,768,512]{2,1...) custom-call(bf16[1024,768]{1,0:T(8,128)(2,1)} %bitcast.139, ...), custom_call_target="tpu_custom_call" | custom-call | flops 6442450944 | bytes 37748736 | tf_op jit(solution)/shard_map/attention_forward/pallas_call | solution.py:116
  106.0 27.9 %ffn_forward.1 = (bf16[1024,3072]{1,0:T(8,128)(2,1)}, bf16[2,2,2,4,96,768]{5,4,3,2,1,0:T(8,128)(2,1)}, f32[8,768]{1,0:T(8,128)}, bf16[1024,768]{1,0:T(8,128)(2,1...) custom-call(bf16[1024,768]{1,0:T(8,128)(2,1)} %get-tuple-element.88.refs_0_, ...), custom_call_target="tpu_custom_call" | custom-call | flops 14495514624 | bytes 35651584 | tf_op jit(solution)/shard_map/ffn_forward/pallas_call | solution.py:406
  134.2 21.5 %ffn_backward.1 = (bf16[384,3072]{1,0:T(8,128)(2,1)}, bf16[384,3072]{1,0:T(8,128)(2,1)}, f32[1,3072]{1,0:T(1,128)}, f32[1024,768]{1,0:T(8,128)}) custom-call(s32[1]{0:T(128)} %bitcast.4.refs_0_, bf16[768,1024]{1,0:T(8,128)(2,1)} %get-tuple-element.94.refs_1_, bf16[1024,3072]{1,0:T(8,128)(2,1)} %get-tuple-element.95.refs_2_, ...), custom_call_target="tpu_custom_call" | custom-call | flops 14495514624 | bytes 31457280 | tf_op jit(solution)/shard_map/ffn_backward/pallas_call | solution.py:492
  156.8 9.3 %norm_backward.1 = (bf16[384,3200]{1,0:T(8,128)(2,1)}, bf16[384,3200]{1,0:T(8,128)(2,1)}, f32[8,768]{1,0:T(8,128)}, bf16[1024,768]{1,0:T(8,128)(2,1)}, bf16[1024,768]{1,0:T(8,128)(2,1)}) custom-call(s32[1]{0:T(128)} %bitcast.4.refs_0_, bf16[768,3200]{1,0:T(8,128)(2,1)} %bitcast.109, f32[8,768]{1,0:T(8,128)} %reshape.234.vec_ref.refs_4_.refs_2_, ...), custom_call_target="tpu_custom_call" | custom-call | flops 2415919104 | bytes 17825792 | tf_op jit(solution)/shard_map/norm_backward/pallas_call | solution.py:575
  166.1 3.7 %fusion.7 = (bf16[4,24,3072]{2,1,0:T(8,128)(2,1)S(1)}, bf16[4,24,3072]{2,1,0:T(8,128)(2,1)}, bf16[4,24,3072]{2,1,0:T(8,128)(2,1)}) fusion(bf16[2,4,2,24,3072]{4,3,2,1,0:T(8,128)(2,1)} %bitcast.20, s32[]{:T(128)S(6)} %select_n.71, s32[]{:T(128)S(6)} %select_n.70, bf16[2,4,2,24,3072]{4,3,2,1,0:T(8,128)(2,1)} %bitcast.118, s32[]{:T(128)S(6)} %select_n.72, ...), kind=kLoop, calls=%fused_computation.15 | loop fusion | flops 3538944 | bytes 5308432 | tf_op jit(solution)/shard_map/convert_element_type | solution.py:738
  171.4 2.0 collective-permute-start.13
  173.3 27.9 %attention_backward.1 = (bf16[384,3200]{1,0:T(8,128)(2,1)}, bf16[384,3200]{1,0:T(8,128)(2,1)}, bf16[1024,2304]{1,0:T(8,128)(2,1)}, f32[8,768]{1,0:T(8,128)}) custom-call(s32[1]{0:T(128)} %bitcast.4.refs_0_, bf16[2,768,512]{2,1,0:T(8,128)(2,1)} %get-tuple-element.105.refs_1_, ...), custom_call_target="tpu_custom_call", output_to_operand_aliasing={{3}: (6, {}), {0}: (7, {}), {1}: (8, {})} | custom-call | flops 6845104128 | bytes 37748736 | tf_op jit(solution)/shard_map/attention_backward/pallas_call | solution.py:223
  202.3 5.0 %collective-permute-done.13 = bf16[4,24,3072]{2,1,0:T(8,128)(2,1)} collective-permute-done((bf16[4,24,3072]{2,1,0:T(8,128)(2,1)S(1)}, bf16[4,24,3072]{2,1,0:T(8,128)(2,1)}, u32[]{:S(2)}, u32[]{:S(2)}) %collective-permute-start.13) | collective-permute-done | bytes 589856 | tf_op jit(solution)/shard_map/ppermute | solution.py:681
  208.7 2.4 fusion.1
  219.2 4.7 %collective-permute-start.18 = (bf16[24,3072]{1,0:T(8,128)(2,1)S(1)}, bf16[24,3072]{1,0:T(8,128)(2,1)S(1)}, u32[]{:S(2)}, u32[]{:S(2)}) collective-permute-start(bf16[24,3072]{1,0:T(8,128)(2,1)S(1)} %get-tuple-element.169), channel_id=1, source_target_pairs={{0,4},{4,8},{8,12},{12,0},{1,5},{5,9},{9,13},{13,1},{2,6},{6,10},{... | collective-permute-start | bytes 442376 | tf_op jit(solution)/shard_map/ppermute | solution.py:685
  224.8 7.4 %collective-permute-done.18 = bf16[24,3072]{1,0:T(8,128)(2,1)S(1)} collective-permute-done((bf16[24,3072]{1,0:T(8,128)(2,1)S(1)}, bf16[24,3072]{1,0:T(8,128)(2,1)S(1)}, u32[]{:S(2)}, u32[]{:S(2)}) %collective-permute-start.18) | collective-permute-done | bytes 147488 | tf_op jit(solution)/shard_map/ppermute | solution.py:685
  232.3 2.7 collective-permute-start.20
  234.9 8.3 %input_grad.1 = bf16[1024,768]{1,0:T(8,128)(2,1)} custom-call(bf16[1024,768]{1,0:T(8,128)(2,1)} %get-tuple-element.104.da_ref, bf16[1024,2304]{1,0:T(8,128)(2,1)} %get-tuple-element.126.dqkv_ref, bf16[768,3200]{1,0:T(8,128)(2,1)} %bitcast.110, bf16[768,3200]{1,0:T(8,128)(2,1)} %bitcast.111, bf16[768,3200]{1,0:T(8,128)(2,1)} %bitcast.112), custom_call_target="tpu_custom_call" | custom-call | flops 3623878656 | bytes 13631488 | tf_op jit(solution)/shard_map/input_grad/pallas_call | solution.py:261
  244.7 2.0 fusion
  246.8 5.1 %collective-permute-start.21 = (bf16[24,3200]{1,0:T(8,128)(2,1)S(1)}, bf16[24,3200]{1,0:T(8,128)(2,1)S(1)}, u32[]{:S(2)}, u32[]{:S(2)}) collective-permute-start(bf16[24,3200]{1,0:T(8,128)(2,1)S(1)} %get-tuple-element.165), channel_id=1, source_target_pairs={{0,4},{4,8},{8,12},{12,0},{1,5},{5,9},{9,13},{13,1},{2,6},{6,10},{... | collective-permute-start | bytes 460808 | tf_op jit(solution)/shard_map/ppermute | solution.py:685
  256.9 5.1 %collective-permute-done.22.refs_2_ = bf16[24,3200]{1,0:T(8,128)(2,1)S(1)} collective-permute-done((bf16[24,3200]{1,0:T(8,128)(2,1)S(1)}, bf16[24,3200]{1,0:T(8,128)(2,1)S(1)}, u32[]{:S(2)}, u32[]{:S(2)}) %collective-permute-start.22) | collective-permute-done | bytes 153632 | tf_op jit(solution)/shard_map/ppermute | solution.py:685
  (90 shorter events, 34.1 us)
Async XLA Ops:
  7.2 98.8 %all-gather.2.cloned.1.call-start = ((), (), s32[]{:S(2)}) async-start(), calls=%async_computation.2 | async-start | bytes 9732096 | tf_op jit(solution)/shard_map/all_gather | solution.py:815
  9.2 198.1 %reduce-scatter.3.cloned.1.call-start = ((), (), s32[]{:S(2)}) async-start(), calls=%async_computation.3 | async-start | bytes 5308416 | tf_op jit(solution)/shard_map/reduce_scatter | solution.py:723
  9.2 10.2 %collective-permute-start = (bf16[24,3200]{1,0:T(8,128)(2,1)}, bf16[24,3200]{1,0:T(8,128)(2,1)S(1)}, u32[]{:S(2)}, u32[]{:S(2)}) collective-permute-start(bf16[24,3200]{1,0:T(8,128)(2,1)} %get-tuple-element.87.refs_0_), channel_id=1, source_target_pairs={{0,4},{4,8},{8,12},{12,0},{1,5},{5,9},{9,13},{13,1},{2,6},{6,10},{... | collective-permute-start | bytes 460808 | tf_op jit(solution)/shard_map/ppermute | solution.py:685
  12.3 12.9 %collective-permute-start.1 = (bf16[24,3200]{1,0:T(8,128)(2,1)}, bf16[24,3200]{1,0:T(8,128)(2,1)S(1)}, u32[]{:S(2)}, u32[]{:S(2)}) collective-permute-start(bf16[24,3200]{1,0:T(8,128)(2,1)} %get-tuple-element.87.refs_0_), channel_id=1, source_target_pairs={{0,8},{4,12},{8,0},{12,4},{1,9},{5,13},{9,1},{13,5},{2,10},{6,14},... | collective-permute-start | bytes 460808 | tf_op jit(solution)/shard_map/ppermute | solution.py:685
  14.9 10.3 %collective-permute-start.2 = (bf16[24,3200]{1,0:T(8,128)(2,1)}, bf16[24,3200]{1,0:T(8,128)(2,1)S(1)}, u32[]{:S(2)}, u32[]{:S(2)}) collective-permute-start(bf16[24,3200]{1,0:T(8,128)(2,1)} %get-tuple-element.87.refs_0_), channel_id=1, source_target_pairs={{0,12},{4,0},{8,4},{12,8},{1,13},{5,1},{9,5},{13,9},{2,14},{6,2},{... | collective-permute-start | bytes 460808 | tf_op jit(solution)/shard_map/ppermute | solution.py:685
  26.2 16.8 %collective-permute-start.3 = (bf16[4,24,3200]{2,1,0:T(8,128)(2,1)S(1)}, bf16[4,24,3200]{2,1,0:T(8,128)(2,1)S(1)}, u32[]{:S(2)}, u32[]{:S(2)}) collective-permute-start(bf16[4,24,3200]{2,1,0:T(8,128)(2,1)S(1)} %stack.21.refs_0_), channel_id=1, source_target_pairs={{0,2},{2,0},{16,18},{18,16},{1,3},{3,1},{17,19},{19,17},{4,6},{6,4... | collective-permute-start | bytes 1843208 | tf_op jit(solution)/shard_map/ppermute | solution.py:681
  27.7 22.1 %collective-permute-start.4 = (bf16[4,24,3200]{2,1,0:T(8,128)(2,1)S(1)}, bf16[4,24,3200]{2,1,0:T(8,128)(2,1)S(1)}, u32[]{:S(2)}, u32[]{:S(2)}) collective-permute-start(bf16[4,24,3200]{2,1,0:T(8,128)(2,1)S(1)} %stack.21.refs_0_), channel_id=1, source_target_pairs={{0,16},{2,18},{16,0},{18,2},{1,17},{3,19},{17,1},{19,3},{4,20},{6,... | collective-permute-start | bytes 1843208 | tf_op jit(solution)/shard_map/ppermute | solution.py:681
  29.2 35.3 %collective-permute-start.5 = (bf16[4,24,3200]{2,1,0:T(8,128)(2,1)S(1)}, bf16[4,24,3200]{2,1,0:T(8,128)(2,1)S(1)}, u32[]{:S(2)}, u32[]{:S(2)}) collective-permute-start(bf16[4,24,3200]{2,1,0:T(8,128)(2,1)S(1)} %stack.21.refs_0_), channel_id=1, source_target_pairs={{0,18},{2,16},{16,2},{18,0},{1,19},{3,17},{17,3},{19,1},{4,22},{6,... | collective-permute-start | bytes 1843208 | tf_op jit(solution)/shard_map/ppermute | solution.py:681
  29.7 35.5 %collective-permute-start.6 = (bf16[4,24,3200]{2,1,0:T(8,128)(2,1)S(1)}, bf16[4,24,3200]{2,1,0:T(8,128)(2,1)S(1)}, u32[]{:S(2)}, u32[]{:S(2)}) collective-permute-start(bf16[4,24,3200]{2,1,0:T(8,128)(2,1)S(1)} %stack.21.refs_0_), channel_id=1, source_target_pairs={{0,1},{1,0},{2,3},{3,2},{4,5},{5,4},{6,7},{7,6},{8,9},{9,8},{10,11... | collective-permute-start | bytes 1843208 | tf_op jit(solution)/shard_map/ppermute | solution.py:672
  43.0 22.2 %collective-permute-start.7 = (bf16[4,24,3200]{2,1,0:T(8,128)(2,1)S(1)}, bf16[4,24,3200]{2,1,0:T(8,128)(2,1)}, u32[]{:S(2)}, u32[]{:S(2)}) collective-permute-start(bf16[4,24,3200]{2,1,0:T(8,128)(2,1)S(1)} %collective-permute-done.3.refs_1_), channel_id=1, source_target_pairs={{0,1},{1,0},{2,3},{3,2},{4,5},{5,4},{6,7},{7,6},{8,9},{9,8},{10,11... | collective-permute-start | bytes 1843208 | tf_op jit(solution)/shard_map/ppermute | solution.py:672
  49.9 15.4 %collective-permute-start.8 = (bf16[4,24,3200]{2,1,0:T(8,128)(2,1)S(1)}, bf16[4,24,3200]{2,1,0:T(8,128)(2,1)}, u32[]{:S(2)}, u32[]{:S(2)}) collective-permute-start(bf16[4,24,3200]{2,1,0:T(8,128)(2,1)S(1)} %collective-permute-done.4.refs_2_), channel_id=1, source_target_pairs={{0,1},{1,0},{2,3},{3,2},{4,5},{5,4},{6,7},{7,6},{8,9},{9,8},{10,11... | collective-permute-start | bytes 1843208 | tf_op jit(solution)/shard_map/ppermute | solution.py:672
  133.9 109.3 %reduce-scatter.5.cloned.1.call-start = ((), (), s32[]{:S(2)}) async-start(), calls=%async_computation.4 | async-start | bytes 737280 | tf_op jit(solution)/shard_map/reduce_scatter | solution.py:726
  155.7 10.4 %collective-permute-start.10 = (bf16[384,3072]{1,0:T(8,128)(2,1)}, bf16[384,3072]{1,0:T(8,128)(2,1)}, u32[]{:S(2)}, u32[]{:S(2)}) collective-permute-start(bf16[384,3072]{1,0:T(8,128)(2,1)} %get-tuple-element.101), channel_id=1, source_target_pairs={{0,1},{1,0},{2,3},{3,2},{4,5},{5,4},{6,7},{7,6},{8,9},{9,8},{10,11... | collective-permute-start | bytes 7077896 | tf_op jit(solution)/shard_map/ppermute | solution.py:672
  169.8 32.4 %collective-permute-start.11 = (bf16[4,24,3072]{2,1,0:T(8,128)(2,1)}, bf16[4,24,3072]{2,1,0:T(8,128)(2,1)}, u32[]{:S(2)}, u32[]{:S(2)}) collective-permute-start(bf16[4,24,3072]{2,1,0:T(8,128)(2,1)} %get-tuple-element.162), channel_id=1, source_target_pairs={{0,2},{2,0},{16,18},{18,16},{1,3},{3,1},{17,19},{19,17},{4,6},{6,4... | collective-permute-start | bytes 1769480 | tf_op jit(solution)/shard_map/ppermute | solution.py:681
  171.4 30.9 %collective-permute-start.12 = (bf16[4,24,3072]{2,1,0:T(8,128)(2,1)}, bf16[4,24,3072]{2,1,0:T(8,128)(2,1)}, u32[]{:S(2)}, u32[]{:S(2)}) collective-permute-start(bf16[4,24,3072]{2,1,0:T(8,128)(2,1)} %get-tuple-element.161), channel_id=1, source_target_pairs={{0,16},{2,18},{16,0},{18,2},{1,17},{3,19},{17,1},{19,3},{4,20},{6,... | collective-permute-start | bytes 1769480 | tf_op jit(solution)/shard_map/ppermute | solution.py:681
  171.4 35.9 %collective-permute-start.13 = (bf16[4,24,3072]{2,1,0:T(8,128)(2,1)S(1)}, bf16[4,24,3072]{2,1,0:T(8,128)(2,1)}, u32[]{:S(2)}, u32[]{:S(2)}) collective-permute-start(bf16[4,24,3072]{2,1,0:T(8,128)(2,1)S(1)} %get-tuple-element.160), channel_id=1, source_target_pairs={{0,18},{2,16},{16,2},{18,0},{1,19},{3,17},{17,3},{19,1},{4,22},{6,... | collective-permute-start | bytes 1769480 | tf_op jit(solution)/shard_map/ppermute | solution.py:681
  215.0 28.2 %collective-permute-start.15 = (bf16[4,24,3200]{2,1,0:T(8,128)(2,1)}, bf16[4,24,3200]{2,1,0:T(8,128)(2,1)S(1)}, u32[]{:S(2)}, u32[]{:S(2)}) collective-permute-start(bf16[4,24,3200]{2,1,0:T(8,128)(2,1)} %get-tuple-element.159), channel_id=1, source_target_pairs={{0,2},{2,0},{16,18},{18,16},{1,3},{3,1},{17,19},{19,17},{4,6},{6,4... | collective-permute-start | bytes 1843208 | tf_op jit(solution)/shard_map/ppermute | solution.py:681
  215.6 29.1 %collective-permute-start.16 = (bf16[4,24,3200]{2,1,0:T(8,128)(2,1)}, bf16[4,24,3200]{2,1,0:T(8,128)(2,1)}, u32[]{:S(2)}, u32[]{:S(2)}) collective-permute-start(bf16[4,24,3200]{2,1,0:T(8,128)(2,1)} %get-tuple-element.158), channel_id=1, source_target_pairs={{0,16},{2,18},{16,0},{18,2},{1,17},{3,19},{17,1},{19,3},{4,20},{6,... | collective-permute-start | bytes 1843208 | tf_op jit(solution)/shard_map/ppermute | solution.py:681
  217.2 27.4 %collective-permute-start.17 = (bf16[4,24,3200]{2,1,0:T(8,128)(2,1)}, bf16[4,24,3200]{2,1,0:T(8,128)(2,1)}, u32[]{:S(2)}, u32[]{:S(2)}) collective-permute-start(bf16[4,24,3200]{2,1,0:T(8,128)(2,1)} %get-tuple-element.157), channel_id=1, source_target_pairs={{0,18},{2,16},{16,2},{18,0},{1,19},{3,17},{17,3},{19,1},{4,22},{6,... | collective-permute-start | bytes 1843208 | tf_op jit(solution)/shard_map/ppermute | solution.py:681
  219.2 13.1 %collective-permute-start.18 = (bf16[24,3072]{1,0:T(8,128)(2,1)S(1)}, bf16[24,3072]{1,0:T(8,128)(2,1)S(1)}, u32[]{:S(2)}, u32[]{:S(2)}) collective-permute-start(bf16[24,3072]{1,0:T(8,128)(2,1)S(1)} %get-tuple-element.169), channel_id=1, source_target_pairs={{0,4},{4,8},{8,12},{12,0},{1,5},{5,9},{9,13},{13,1},{2,6},{6,10},{... | collective-permute-start | bytes 442376 | tf_op jit(solution)/shard_map/ppermute | solution.py:685
  223.9 19.3 %collective-permute-start.19 = (bf16[24,3072]{1,0:T(8,128)(2,1)}, bf16[24,3072]{1,0:T(8,128)(2,1)}, u32[]{:S(2)}, u32[]{:S(2)}) collective-permute-start(bf16[24,3072]{1,0:T(8,128)(2,1)} %get-tuple-element.168), channel_id=1, source_target_pairs={{0,8},{4,12},{8,0},{12,4},{1,9},{5,13},{9,1},{13,5},{2,10},{6,14},... | collective-permute-start | bytes 442376 | tf_op jit(solution)/shard_map/ppermute | solution.py:685
  232.3 10.9 %collective-permute-start.20 = (bf16[24,3072]{1,0:T(8,128)(2,1)S(1)}, bf16[24,3072]{1,0:T(8,128)(2,1)}, u32[]{:S(2)}, u32[]{:S(2)}) collective-permute-start(bf16[24,3072]{1,0:T(8,128)(2,1)S(1)} %get-tuple-element.167), channel_id=1, source_target_pairs={{0,12},{4,0},{8,4},{12,8},{1,13},{5,1},{9,5},{13,9},{2,14},{6,2},{... | collective-permute-start | bytes 442376 | tf_op jit(solution)/shard_map/ppermute | solution.py:685
  246.8 10.1 %collective-permute-start.21 = (bf16[24,3200]{1,0:T(8,128)(2,1)S(1)}, bf16[24,3200]{1,0:T(8,128)(2,1)S(1)}, u32[]{:S(2)}, u32[]{:S(2)}) collective-permute-start(bf16[24,3200]{1,0:T(8,128)(2,1)S(1)} %get-tuple-element.165), channel_id=1, source_target_pairs={{0,4},{4,8},{8,12},{12,0},{1,5},{5,9},{9,13},{13,1},{2,6},{6,10},{... | collective-permute-start | bytes 460808 | tf_op jit(solution)/shard_map/ppermute | solution.py:685
  251.9 10.1 %collective-permute-start.22 = (bf16[24,3200]{1,0:T(8,128)(2,1)S(1)}, bf16[24,3200]{1,0:T(8,128)(2,1)S(1)}, u32[]{:S(2)}, u32[]{:S(2)}) collective-permute-start(bf16[24,3200]{1,0:T(8,128)(2,1)S(1)} %get-tuple-element.164), channel_id=1, source_target_pairs={{0,8},{4,12},{8,0},{12,4},{1,9},{5,13},{9,1},{13,5},{2,10},{6,14},... | collective-permute-start | bytes 460808 | tf_op jit(solution)/shard_map/ppermute | solution.py:685
  (14 other events, 125.4 us)
Sparse Core Ops, SparseCore 0:
  11.5 94.1 all-gather.1
  134.1 63.7 reduce-scatter.2
  208.8 26.8 reduce-scatter.4

commit v2 on v1

--- a/solution.py
+++ b/solution.py
@@ -157,12 +157,10 @@
 ):
     row, seqs = pl.program_id(1), pl.num_programs(1)
     head_of = lax.broadcasted_iota(jnp.int32, (8, GROUP), 1) // HEAD_DIM
-    picks = (head_of == lax.broadcasted_iota(jnp.int32, (8, GROUP), 0)).astype(F32)
+    picks = (head_of == lax.broadcasted_iota(jnp.int32, (8, GROUP), 0)).astype(LOW)
     product = ctx_ref[...].astype(F32) * dctx_ref[...].astype(F32)
-    inner = lax.dot_general(
-        picks, product, (((1,), (1,)), ((), ())),
-        preferred_element_type=F32, precision=lax.Precision.HIGHEST,
-    )
+    high = product.astype(LOW)
+    inner = mm_t(picks, high) + mm_t(picks, (product - high.astype(F32)).astype(LOW))
     lane = lax.broadcasted_iota(jnp.int32, (1, PAIR), 1)
     first = lane < HEAD_DIM
     scale = jnp.asarray(HEAD_DIM**-0.5, LOW)
@@ -732,10 +730,22 @@
         return jnp.concatenate(pair, axis=1).reshape(-1, keep.shape[3])
 
 
+    def block(self, grad, got, dp, side, columns=None):
+        dps, lines, sides, _ = self.sizes
+        first, last = columns or (0, grad.shape[1])
+        start = (0 if dp is None else dp, 0, 0 if side is None else side, 0, first)
+        size = (dps if dp is None else 1, lines, sides if side is None else 1)
+        total = 0.0
+        for part in (grad, got):
+            part = part.reshape(dps, lines, sides, -1, grad.shape[1])
+            total += lax.dynamic_slice(part, start, (*size, part.shape[3], last - first)).astype(F32)
+        return total
+
+
     def plane_messages(self, grad, got):
         dps, _, sides, _ = self.sizes
         return [
-            self.block(grad, got, lax.rem(self.dp + a, dps), lax.rem(self.side + b, sides)).astype(LOW)
+            self.block(grad, got, lax.rem(self.dp + a, dps), lax.rem(self.side + b, sides))[0, :, 0].astype(LOW)
             for a, b in self.offsets[1:]
         ]
 
@@ -743,17 +753,42 @@
         return [self.to_plane(m, o) for m, o in zip(messages, self.offsets[1:])]
 
     def plane_done(self, grad, got, parts):
-        total = self.block(grad, got, self.dp, self.side)
+        total = self.block(grad, got, self.dp, self.side)[0, :, 0]
         return self.along_line((total + sum(p.astype(F32) for p in parts)).astype(LOW))
 
-    def block(self, grad, got, dp, side):
-        dps, lines, sides, _ = self.sizes
-        total = 0.0
-        for part in (grad, got):
-            part = part.reshape(dps, lines, sides, -1, grad.shape[1])
-            size = (1, lines, 1, *part.shape[3:])
-            total += lax.dynamic_slice(part, (dp, 0, side, 0, 0), size)[0, :, 0].astype(F32)
-        return total
+
+    def halves(self, grad):
+        columns = grad.shape[1]
+        return (0, columns // 2), (columns // 2, columns)
+
+    def first_messages(self, grad, got):
+        one, two = self.halves(grad)
+        return (
+            self.block(grad, got, None, 1 - self.side, one).astype(LOW),
+            self.block(grad, got, 1 - self.dp, None, two).astype(LOW),
+        )
+
+    def first_exchange(self, messages):
+        return self.to_plane(messages[0], (0, 1)), self.to_plane(messages[1], (1, 0))
+
+    def second_messages(self, grad, got, more):
+        one, two = self.halves(grad)
+        a = self.block(grad, got, 1 - self.dp, self.side, one)
+        b = self.block(grad, got, self.dp, 1 - self.side, two)
+        a += lax.dynamic_slice_in_dim(more[0], 1 - self.dp, 1, 0).astype(F32)
+        b += lax.dynamic_slice_in_dim(more[1], 1 - self.side, 1, 2).astype(F32)
+        return a.astype(LOW), b.astype(LOW)
+
+    def second_exchange(self, messages):
+        return self.to_plane(messages[0], (1, 0)), self.to_plane(messages[1], (0, 1))
+
+    def second_done(self, grad, got, more, most):
+        one, two = self.halves(grad)
+        a = self.block(grad, got, self.dp, self.side, one) + most[0].astype(F32)
+        b = self.block(grad, got, self.dp, self.side, two) + most[1].astype(F32)
+        a += lax.dynamic_slice_in_dim(more[0], self.dp, 1, 0).astype(F32)
+        b += lax.dynamic_slice_in_dim(more[1], self.side, 1, 2).astype(F32)
+        return self.along_line(jnp.concatenate([a[0, :, 0], b[0, :, 0]], axis=2).astype(LOW))
 
     def along_line(self, total):
         lines = self.sizes[1]
@@ -862,21 +897,26 @@
         got = mesh.to_core(send)
         keep, send, sums, dctx, da = norm_backward(unit, core, normed, inverse, dn1, ctx, weights, table, sums)
         inner_got, sums = after((got, sums), dctx)
-        message = mesh.plane_messages(g_inner, inner_got)
+        message = mesh.first_messages(g_inner, inner_got)
         sums = after(sums, message)
-        parts = mesh.plane_exchange(message)
+        more = mesh.first_exchange(message)
         late, send, dqkv, sums = attention_backward(unit, core, xt, qkv, ctx, probs, dctx, sums, keep, send)
-        late, send, parts, g_outer = after((late, send, parts, g_outer), dqkv)
+        late, send, more, g_outer = after((late, send, more, g_outer), dqkv)
         g_outer = mesh.line_sum(g_outer)
+        g_b_inner = after(g_b_inner, dqkv)
         vector = vector_rows(sums, g_b_inner, count).reshape(-1, 2, unit, PAIR)
         at = (mesh.core, 1 - mesh.core)
         vector = [lax.dynamic_index_in_dim(vector, i, 1, keepdims=False).reshape(-1, PAIR) for i in at]
         late = lax.dynamic_update_slice(late, vector[0], (0, 4 * D))
         send = lax.dynamic_update_slice(send, vector[1], (0, 4 * D))
-        dqkv, parts = after((dqkv, parts), (late, send))
-        lines = mesh.line_exchange(mesh.plane_done(g_inner, inner_got, parts))
         got = mesh.to_core(send)
-        parts = mesh.plane_exchange(mesh.plane_messages(late, got))
+        message = mesh.second_messages(g_inner, inner_got, more)
+        got, dqkv = after((got, dqkv), message)
+        most = mesh.second_exchange(message)
+        message = mesh.plane_messages(late, got)
+        most, dqkv = after((most, dqkv), message)
+        parts = mesh.plane_exchange(message)
+        lines = mesh.line_exchange(mesh.second_done(g_inner, inner_got, more, most))
         dx = input_grad(da, dqkv, weights)
         parts, g_inner, g_outer = after((parts, lines, g_outer), dx)
         message = mesh.plane_done(late, got, parts)

time: 271 us -> 268 us (0.989)
  waiting for transfers between devices: 65.3 us -> 57 us
  other arithmetic: 14.9 us -> 21.7 us
    convert_element_type x0 -> x4, other arithmetic: none -> 8.24 us  [the longest x2 3.84 us: second_messages(): return (a.astype(LOW), b.astype(LOW))]
    ppermute x9 -> x10, waiting for transfers between devices: 41.2 us -> 35.9 us  [to_plane(): return lax.ppermute(array, ('dp', 'side'), pairs)]
    squeeze x0 -> x3, other arithmetic: none -> 3.44 us  [the longest x1 1.39 us: second_done(): b[0, :, 0]]
    convert_element_type x2 -> x1, other arithmetic: 5.66 us -> 3.9 us  [plane_messages(): self.block(grad, got, lax.rem(self.dp + a, dps), lax.rem(self.side + b, s...]
    ppermute x9 -> x10, starting transfers between devices: 10.5 us -> 11 us  [to_plane(): return lax.ppermute(array, ('dp', 'side'), pairs)]
  transfers between devices with their start and end apart: 27 -> 28, of which waited for: 11 -> 9; matrix products, arithmetic and copies ran while one was open for 6% -> 9% of each run, Pallas kernels for 39% -> 38%
where the time goes in v2:
time: 268 us; the launch traced here: 267 us
  Pallas kernels  133 us (50%)
  waiting for transfers between devices  57 us (21%)
  starting transfers between devices  35 us (13%)
  other arithmetic  21.7 us (8%)
  between operations  14 us (5%)
  local copies, waits for them, and re-layouts  5.96 us (2%)
    ppermute x10, waiting for transfers between devices, to_plane(): return lax.ppermute(array, ('dp', 'side'), pairs)  35.9 us
    pallas_call x1, Pallas kernels, attention_forward(): pl.pallas_call(attention_forward_kernel, grid=(seqs, GROUPS), in_specs=[r...  30.3 us
    pallas_call x1, Pallas kernels, ffn_forward(): pl.pallas_call(lambda *refs: ffn_forward_kernel(unit, *refs), grid=(2 * C...  27.8 us
    pallas_call x1, Pallas kernels, attention_backward(): pl.pallas_call(lambda *refs: attention_backward_kernel(unit, *refs), grid...  26.6 us
    ppermute x9, starting transfers between devices, to_line(): lax.ppermute(array, 'line', [(i, (i + shift) % count) for i in range(coun...  23.3 us
    pallas_call x1, Pallas kernels, ffn_backward(): pl.pallas_call(lambda *refs: ffn_backward_kernel(unit, *refs), grid=(CHUN...  21.6 us
    ppermute x9, waiting for transfers between devices, to_line(): lax.ppermute(array, 'line', [(i, (i + shift) % count) for i in range(coun...  20.3 us
    ppermute x10, starting transfers between devices, to_plane(): return lax.ppermute(array, ('dp', 'side'), pairs)  11 us
  transfers between devices with their start and end apart: 28, of which 9 were waited for; matrix products, arithmetic and copies ran while one was open for 9% of the time, Pallas kernels for 38%

profile of v2, /device:TPU:0, one launch (start us, length us, event | category | flops | bytes accessed | tf_op | source)
XLA Modules:
  0.0 266.5 jit_solution(3491500706328979018)
XLA Ops:
  9.2 3.1 %collective-permute-start = (bf16[24,3200]{1,0:T(8,128)(2,1)}, bf16[24,3200]{1,0:T(8,128)(2,1)S(1)}, u32[]{:S(2)}, u32[]{:S(2)}) collective-permute-start(bf16[24,3200]{1,0:T(8,128)(2,1)} %get-tuple-element.88.refs_0_), channel_id=1, source_target_pairs={{0,4},{4,8},{8,12},{12,0},{1,5},{5,9},{9,13},{13,1},{2,6},{6,10},{... | collective-permute-start | bytes 460808 | tf_op jit(solution)/shard_map/ppermute | solution.py:683
  12.3 2.6 collective-permute-start.1
  16.2 3.2 %collective-permute-done.refs_1_ = bf16[24,3200]{1,0:T(8,128)(2,1)S(1)} collective-permute-done((bf16[24,3200]{1,0:T(8,128)(2,1)}, bf16[24,3200]{1,0:T(8,128)(2,1)S(1)}, u32[]{:S(2)}, u32[]{:S(2)}) %collective-permute-start) | collective-permute-done | bytes 153632 | tf_op jit(solution)/shard_map/ppermute | solution.py:683
  19.4 5.7 %collective-permute-done.1.refs_2_ = bf16[24,3200]{1,0:T(8,128)(2,1)S(1)} collective-permute-done((bf16[24,3200]{1,0:T(8,128)(2,1)}, bf16[24,3200]{1,0:T(8,128)(2,1)S(1)}, u32[]{:S(2)}, u32[]{:S(2)}) %collective-permute-start.1) | collective-permute-done | bytes 153632 | tf_op jit(solution)/shard_map/ppermute | solution.py:683
  29.7 13.2 %collective-permute-done.3.refs_1_ = bf16[4,24,3200]{2,1,0:T(8,128)(2,1)S(1)} collective-permute-done((bf16[4,24,3200]{2,1,0:T(8,128)(2,1)S(1)}, bf16[4,24,3200]{2,1,0:T(8,128)(2,1)S(1)}, u32[]{:S(2)}, u32[]{:S(2)}) %collective-permute-start.3) | collective-permute-done | bytes 614432 | tf_op jit(solution)/shard_map/ppermute | solution.py:679
  43.0 6.9 %collective-permute-done.4.refs_2_ = bf16[4,24,3200]{2,1,0:T(8,128)(2,1)S(1)} collective-permute-done((bf16[4,24,3200]{2,1,0:T(8,128)(2,1)S(1)}, bf16[4,24,3200]{2,1,0:T(8,128)(2,1)S(1)}, u32[]{:S(2)}, u32[]{:S(2)}) %collective-permute-start.4) | collective-permute-done | bytes 614432 | tf_op jit(solution)/shard_map/ppermute | solution.py:679
  49.9 14.6 %collective-permute-done.5.refs_3_ = bf16[4,24,3200]{2,1,0:T(8,128)(2,1)S(1)} collective-permute-done((bf16[4,24,3200]{2,1,0:T(8,128)(2,1)S(1)}, bf16[4,24,3200]{2,1,0:T(8,128)(2,1)S(1)}, u32[]{:S(2)}, u32[]{:S(2)}) %collective-permute-start.5) | collective-permute-done | bytes 614432 | tf_op jit(solution)/shard_map/ppermute | solution.py:679
  66.7 6.5 %place.1 = bf16[32,24,3200]{2,1,0:T(8,128)(2,1)} custom-call(s32[4]{0:T(128)} %pad_add_fusion.place_ref, bf16[4,24,3200]{2,1,0:T(8,128)(2,1)} %copy-done, bf16[4,24,3200]{2,1,0:T(8,128)(2,1)} %copy-done.3, bf16[4,24,3200]{2,1,0:T(8,128)(2,1)} %copy-done.4, bf16[4,24,3200]{2,1,0:T(8,128)(2,1)} %copy-done.5, bf16[4,24,3200]{2,1,0:T(8,128)(2,1)} %copy-done.6, ...), custom_call_target="tpu_custom_call" | custom-call | tf_op jit(solution)/shard_map/place/pallas_call | solution.py:708
  75.8 30.3 %attention_forward.1 = (bf16[1024,2304]{1,0:T(8,128)(2,1)}, bf16[1024,768]{1,0:T(8,128)(2,1)}, bf16[2,3,4,512,512]{4,3,2,1,0:T(8,128)(2,1)}, bf16[2,768,512]{2,1...) custom-call(bf16[1024,768]{1,0:T(8,128)(2,1)} %bitcast.137, ...), custom_call_target="tpu_custom_call" | custom-call | flops 6442450944 | bytes 37748736 | tf_op jit(solution)/shard_map/attention_forward/pallas_call | solution.py:116
  106.1 27.8 %ffn_forward.1 = (bf16[1024,3072]{1,0:T(8,128)(2,1)}, bf16[2,2,2,4,96,768]{5,4,3,2,1,0:T(8,128)(2,1)}, f32[8,768]{1,0:T(8,128)}, bf16[1024,768]{1,0:T(8,128)(2,1...) custom-call(bf16[1024,768]{1,0:T(8,128)(2,1)} %get-tuple-element.89.refs_0_, ...), custom_call_target="tpu_custom_call" | custom-call | flops 14495514624 | bytes 35651584 | tf_op jit(solution)/shard_map/ffn_forward/pallas_call | solution.py:404
  134.1 21.6 %ffn_backward.1 = (bf16[384,3072]{1,0:T(8,128)(2,1)}, bf16[384,3072]{1,0:T(8,128)(2,1)}, f32[1,3072]{1,0:T(1,128)}, f32[1024,768]{1,0:T(8,128)}) custom-call(s32[1]{0:T(128)} %bitcast.4.refs_0_, bf16[768,1024]{1,0:T(8,128)(2,1)} %get-tuple-element.95.refs_1_, bf16[1024,3072]{1,0:T(8,128)(2,1)} %get-tuple-element.96.refs_2_, ...), custom_call_target="tpu_custom_call" | custom-call | flops 14495514624 | bytes 31457280 | tf_op jit(solution)/shard_map/ffn_backward/pallas_call | solution.py:490
  155.9 9.1 %norm_backward.1 = (bf16[384,3200]{1,0:T(8,128)(2,1)}, bf16[384,3200]{1,0:T(8,128)(2,1)}, f32[8,768]{1,0:T(8,128)}, bf16[1024,768]{1,0:T(8,128)(2,1)}, bf16[1024,768]{1,0:T(8,128)(2,1)}) custom-call(s32[1]{0:T(128)} %bitcast.4.refs_0_, bf16[768,3200]{1,0:T(8,128)(2,1)} %bitcast.103, f32[8,768]{1,0:T(8,128)} %reshape.211.vec_ref.refs_4_.refs_2_, ...), custom_call_target="tpu_custom_call" | custom-call | flops 2415919104 | bytes 17825792 | tf_op jit(solution)/shard_map/norm_backward/pallas_call | solution.py:573
  165.1 2.2 add_convert_fusion.4
  168.4 2.2 add_convert_fusion.3
  170.8 26.6 %attention_backward.1 = (bf16[384,3200]{1,0:T(8,128)(2,1)}, bf16[384,3200]{1,0:T(8,128)(2,1)}, bf16[1024,2304]{1,0:T(8,128)(2,1)}, f32[8,768]{1,0:T(8,128)}) custom-call(s32[1]{0:T(128)} %bitcast.4.refs_0_, bf16[2,768,512]{2,1,0:T(8,128)(2,1)} %get-tuple-element.110.refs_1_, ...), custom_call_target="tpu_custom_call", output_to_operand_aliasing={{3}: (6, {}), {0}: (7, {}), {1}: (8, {})} | custom-call | flops 6845104128 | bytes 37748736 | tf_op jit(solution)/shard_map/attention_backward/pallas_call | solution.py:221
  206.6 3.9 %fusion.3 = (bf16[4,24,3200]{2,1,0:T(8,128)(2,1)}, bf16[4,24,3200]{2,1,0:T(8,128)(2,1)}, bf16[4,24,3200]{2,1,0:T(8,128)(2,1)}) fusion(bf16[2,4,2,24,3200]{4,3,2,1,0:T(8,128)(2,1)S(1)} %bitcast.110, s32[]{:T(128)S(6)} %select_n.89, s32[]{:T(128)S(6)} %select_n.88, bf16[2,4,2,24,3200]{4,3,2,1,0:T(8,128)(2,1)} %bitcast.107, s32[]{:T(128)S(6)} %select_n.90, ...), kind=kLoop, calls=%fused_computation.17 | loop fusion | flops 3686400 | bytes 5529616 | tf_op jit(solution)/shard_map/convert_element_type | solution.py:748
  211.9 2.1 collective-permute-start.18
  218.6 6.4 %collective-permute-start.19 = (bf16[24,3072]{1,0:T(8,128)(2,1)S(1)}, bf16[24,3072]{1,0:T(8,128)(2,1)S(1)}, u32[]{:S(2)}, u32[]{:S(2)}) collective-permute-start(bf16[24,3072]{1,0:T(8,128)(2,1)S(1)} %get-tuple-element.168), channel_id=1, source_target_pairs={{0,4},{4,8},{8,12},{12,0},{1,5},{5,9},{9,13},{13,1},{2,6},{6,10},{... | collective-permute-start | bytes 442376 | tf_op jit(solution)/shard_map/ppermute | solution.py:683
  225.4 6.6 %collective-permute-done.19 = bf16[24,3072]{1,0:T(8,128)(2,1)S(1)} collective-permute-done((bf16[24,3072]{1,0:T(8,128)(2,1)S(1)}, bf16[24,3072]{1,0:T(8,128)(2,1)S(1)}, u32[]{:S(2)}, u32[]{:S(2)}) %collective-permute-start.19) | collective-permute-done | bytes 147488 | tf_op jit(solution)/shard_map/ppermute | solution.py:683
  233.2 8.2 %input_grad.1 = bf16[1024,768]{1,0:T(8,128)(2,1)} custom-call(bf16[1024,768]{1,0:T(8,128)(2,1)} %get-tuple-element.105.da_ref, bf16[1024,2304]{1,0:T(8,128)(2,1)} %get-tuple-element.129.dqkv_ref, bf16[768,3200]{1,0:T(8,128)(2,1)} %bitcast.104, bf16[768,3200]{1,0:T(8,128)(2,1)} %bitcast.105, bf16[768,3200]{1,0:T(8,128)(2,1)} %bitcast.106), custom_call_target="tpu_custom_call" | custom-call | flops 3623878656 | bytes 13631488 | tf_op jit(solution)/shard_map/input_grad/pallas_call | solution.py:259
  241.5 2.1 fusion
  243.6 5.9 %collective-permute-start.22 = (bf16[24,3200]{1,0:T(8,128)(2,1)S(1)}, bf16[24,3200]{1,0:T(8,128)(2,1)S(1)}, u32[]{:S(2)}, u32[]{:S(2)}) collective-permute-start(bf16[24,3200]{1,0:T(8,128)(2,1)S(1)} %get-tuple-element.164), channel_id=1, source_target_pairs={{0,4},{4,8},{8,12},{12,0},{1,5},{5,9},{9,13},{13,1},{2,6},{6,10},{... | collective-permute-start | bytes 460808 | tf_op jit(solution)/shard_map/ppermute | solution.py:683
  249.5 2.4 collective-permute-start.24
  254.5 4.8 %collective-permute-done.23.refs_2_ = bf16[24,3200]{1,0:T(8,128)(2,1)S(1)} collective-permute-done((bf16[24,3200]{1,0:T(8,128)(2,1)S(1)}, bf16[24,3200]{1,0:T(8,128)(2,1)S(1)}, u32[]{:S(2)}, u32[]{:S(2)}) %collective-permute-start.23) | collective-permute-done | bytes 153632 | tf_op jit(solution)/shard_map/ppermute | solution.py:683
  (98 shorter events, 34.4 us)
Async XLA Ops:
  7.2 98.9 %all-gather.2.cloned.1.call-start = ((), (), s32[]{:S(2)}) async-start(), calls=%async_computation.2 | async-start | bytes 9732096 | tf_op jit(solution)/shard_map/all_gather | solution.py:850
  9.2 189.4 %reduce-scatter.3.cloned.1.call-start = ((), (), s32[]{:S(2)}) async-start(), calls=%async_computation.3 | async-start | bytes 5308416 | tf_op jit(solution)/shard_map/reduce_scatter | solution.py:721
  9.2 10.2 %collective-permute-start = (bf16[24,3200]{1,0:T(8,128)(2,1)}, bf16[24,3200]{1,0:T(8,128)(2,1)S(1)}, u32[]{:S(2)}, u32[]{:S(2)}) collective-permute-start(bf16[24,3200]{1,0:T(8,128)(2,1)} %get-tuple-element.88.refs_0_), channel_id=1, source_target_pairs={{0,4},{4,8},{8,12},{12,0},{1,5},{5,9},{9,13},{13,1},{2,6},{6,10},{... | collective-permute-start | bytes 460808 | tf_op jit(solution)/shard_map/ppermute | solution.py:683
  12.3 12.9 %collective-permute-start.1 = (bf16[24,3200]{1,0:T(8,128)(2,1)}, bf16[24,3200]{1,0:T(8,128)(2,1)S(1)}, u32[]{:S(2)}, u32[]{:S(2)}) collective-permute-start(bf16[24,3200]{1,0:T(8,128)(2,1)} %get-tuple-element.88.refs_0_), channel_id=1, source_target_pairs={{0,8},{4,12},{8,0},{12,4},{1,9},{5,13},{9,1},{13,5},{2,10},{6,14},... | collective-permute-start | bytes 460808 | tf_op jit(solution)/shard_map/ppermute | solution.py:683
  14.9 10.3 %collective-permute-start.2 = (bf16[24,3200]{1,0:T(8,128)(2,1)}, bf16[24,3200]{1,0:T(8,128)(2,1)S(1)}, u32[]{:S(2)}, u32[]{:S(2)}) collective-permute-start(bf16[24,3200]{1,0:T(8,128)(2,1)} %get-tuple-element.88.refs_0_), channel_id=1, source_target_pairs={{0,12},{4,0},{8,4},{12,8},{1,13},{5,1},{9,5},{13,9},{2,14},{6,2},{... | collective-permute-start | bytes 460808 | tf_op jit(solution)/shard_map/ppermute | solution.py:683
  26.2 16.8 %collective-permute-start.3 = (bf16[4,24,3200]{2,1,0:T(8,128)(2,1)S(1)}, bf16[4,24,3200]{2,1,0:T(8,128)(2,1)S(1)}, u32[]{:S(2)}, u32[]{:S(2)}) collective-permute-start(bf16[4,24,3200]{2,1,0:T(8,128)(2,1)S(1)} %stack.21.refs_0_), channel_id=1, source_target_pairs={{0,2},{2,0},{16,18},{18,16},{1,3},{3,1},{17,19},{19,17},{4,6},{6,4... | collective-permute-start | bytes 1843208 | tf_op jit(solution)/shard_map/ppermute | solution.py:679
  27.7 22.1 %collective-permute-start.4 = (bf16[4,24,3200]{2,1,0:T(8,128)(2,1)S(1)}, bf16[4,24,3200]{2,1,0:T(8,128)(2,1)S(1)}, u32[]{:S(2)}, u32[]{:S(2)}) collective-permute-start(bf16[4,24,3200]{2,1,0:T(8,128)(2,1)S(1)} %stack.21.refs_0_), channel_id=1, source_target_pairs={{0,16},{2,18},{16,0},{18,2},{1,17},{3,19},{17,1},{19,3},{4,20},{6,... | collective-permute-start | bytes 1843208 | tf_op jit(solution)/shard_map/ppermute | solution.py:679
  29.2 35.3 %collective-permute-start.5 = (bf16[4,24,3200]{2,1,0:T(8,128)(2,1)S(1)}, bf16[4,24,3200]{2,1,0:T(8,128)(2,1)S(1)}, u32[]{:S(2)}, u32[]{:S(2)}) collective-permute-start(bf16[4,24,3200]{2,1,0:T(8,128)(2,1)S(1)} %stack.21.refs_0_), channel_id=1, source_target_pairs={{0,18},{2,16},{16,2},{18,0},{1,19},{3,17},{17,3},{19,1},{4,22},{6,... | collective-permute-start | bytes 1843208 | tf_op jit(solution)/shard_map/ppermute | solution.py:679
  29.7 35.5 %collective-permute-start.6 = (bf16[4,24,3200]{2,1,0:T(8,128)(2,1)S(1)}, bf16[4,24,3200]{2,1,0:T(8,128)(2,1)S(1)}, u32[]{:S(2)}, u32[]{:S(2)}) collective-permute-start(bf16[4,24,3200]{2,1,0:T(8,128)(2,1)S(1)} %stack.21.refs_0_), channel_id=1, source_target_pairs={{0,1},{1,0},{2,3},{3,2},{4,5},{5,4},{6,7},{7,6},{8,9},{9,8},{10,11... | collective-permute-start | bytes 1843208 | tf_op jit(solution)/shard_map/ppermute | solution.py:670
  43.0 22.2 %collective-permute-start.7 = (bf16[4,24,3200]{2,1,0:T(8,128)(2,1)S(1)}, bf16[4,24,3200]{2,1,0:T(8,128)(2,1)}, u32[]{:S(2)}, u32[]{:S(2)}) collective-permute-start(bf16[4,24,3200]{2,1,0:T(8,128)(2,1)S(1)} %collective-permute-done.3.refs_1_), channel_id=1, source_target_pairs={{0,1},{1,0},{2,3},{3,2},{4,5},{5,4},{6,7},{7,6},{8,9},{9,8},{10,11... | collective-permute-start | bytes 1843208 | tf_op jit(solution)/shard_map/ppermute | solution.py:670
  49.9 15.4 %collective-permute-start.8 = (bf16[4,24,3200]{2,1,0:T(8,128)(2,1)S(1)}, bf16[4,24,3200]{2,1,0:T(8,128)(2,1)}, u32[]{:S(2)}, u32[]{:S(2)}) collective-permute-start(bf16[4,24,3200]{2,1,0:T(8,128)(2,1)S(1)} %collective-permute-done.4.refs_2_), channel_id=1, source_target_pairs={{0,1},{1,0},{2,3},{3,2},{4,5},{5,4},{6,7},{7,6},{8,9},{9,8},{10,11... | collective-permute-start | bytes 1843208 | tf_op jit(solution)/shard_map/ppermute | solution.py:670
  133.9 107.5 %reduce-scatter.5.cloned.1.call-start = ((), (), s32[]{:S(2)}) async-start(), calls=%async_computation.4 | async-start | bytes 737280 | tf_op jit(solution)/shard_map/reduce_scatter | solution.py:724
  167.3 31.2 %collective-permute-start.11 = (bf16[2,4,1,24,1536]{4,3,1,2,0:T(8,128)(2,1)}, bf16[2,4,1,24,1536]{4,3,1,2,0:T(8,128)(2,1)S(1)}, u32[]{:S(2)}, u32[]{:S(2)}) collective-permute-start(bf16[2,4,1,24,1536]{4,3,1,2,0:T(8,128)(2,1)} %add_convert_fusion.4), channel_id=1, source_target_pairs={{0,2},{2,0},{16,18},{18,16},{1,3},{3,1},{17,19},{19,17},{4,6},{6,4... | collective-permute-start | bytes 1769480 | tf_op jit(solution)/shard_map/ppermute | solution.py:679
  170.6 27.9 %collective-permute-start.12 = (bf16[1,4,2,24,1536]{4,3,2,1,0:T(8,128)(2,1)}, bf16[1,4,2,24,1536]{4,3,2,1,0:T(8,128)(2,1)}, u32[]{:S(2)}, u32[]{:S(2)}) collective-permute-start(bf16[1,4,2,24,1536]{4,3,2,1,0:T(8,128)(2,1)} %add_convert_fusion.3), channel_id=1, source_target_pairs={{0,16},{2,18},{16,0},{18,2},{1,17},{3,19},{17,1},{19,3},{4,20},{6,... | collective-permute-start | bytes 1769480 | tf_op jit(solution)/shard_map/ppermute | solution.py:679
  201.3 12.7 %collective-permute-start.13 = (bf16[1,4,1,24,1536]{4,3,1,2,0:T(8,128)(2,1)}, bf16[1,4,1,24,1536]{4,3,1,2,0:T(8,128)(2,1)S(1)}, u32[]{:S(2)}, u32[]{:S(2)}) collective-permute-start(bf16[1,4,1,24,1536]{4,3,1,2,0:T(8,128)(2,1)} %add_convert_fusion.8), channel_id=1, source_target_pairs={{0,16},{2,18},{16,0},{18,2},{1,17},{3,19},{17,1},{19,3},{4,20},{6,... | collective-permute-start | bytes 884744 | tf_op jit(solution)/shard_map/ppermute | solution.py:679
  205.0 10.2 %collective-permute-start.14 = (bf16[1,4,1,24,1536]{4,3,2,1,0:T(8,128)(2,1)}, bf16[1,4,1,24,1536]{4,3,2,1,0:T(8,128)(2,1)}, u32[]{:S(2)}, u32[]{:S(2)}) collective-permute-start(bf16[1,4,1,24,1536]{4,3,2,1,0:T(8,128)(2,1)} %add_convert_fusion.7), channel_id=1, source_target_pairs={{0,2},{2,0},{16,18},{18,16},{1,3},{3,1},{17,19},{19,17},{4,6},{6,4... | collective-permute-start | bytes 884744 | tf_op jit(solution)/shard_map/ppermute | solution.py:679
  210.5 30.9 %collective-permute-start.16 = (bf16[4,24,3200]{2,1,0:T(8,128)(2,1)}, bf16[4,24,3200]{2,1,0:T(8,128)(2,1)S(1)}, u32[]{:S(2)}, u32[]{:S(2)}) collective-permute-start(bf16[4,24,3200]{2,1,0:T(8,128)(2,1)} %get-tuple-element.161), channel_id=1, source_target_pairs={{0,2},{2,0},{16,18},{18,16},{1,3},{3,1},{17,19},{19,17},{4,6},{6,4... | collective-permute-start | bytes 1843208 | tf_op jit(solution)/shard_map/ppermute | solution.py:679
  211.6 29.8 %collective-permute-start.17 = (bf16[4,24,3200]{2,1,0:T(8,128)(2,1)}, bf16[4,24,3200]{2,1,0:T(8,128)(2,1)}, u32[]{:S(2)}, u32[]{:S(2)}) collective-permute-start(bf16[4,24,3200]{2,1,0:T(8,128)(2,1)} %get-tuple-element.160), channel_id=1, source_target_pairs={{0,16},{2,18},{16,0},{18,2},{1,17},{3,19},{17,1},{19,3},{4,20},{6,... | collective-permute-start | bytes 1843208 | tf_op jit(solution)/shard_map/ppermute | solution.py:679
  211.9 29.5 %collective-permute-start.18 = (bf16[4,24,3200]{2,1,0:T(8,128)(2,1)}, bf16[4,24,3200]{2,1,0:T(8,128)(2,1)}, u32[]{:S(2)}, u32[]{:S(2)}) collective-permute-start(bf16[4,24,3200]{2,1,0:T(8,128)(2,1)} %get-tuple-element.159), channel_id=1, source_target_pairs={{0,18},{2,16},{16,2},{18,0},{1,19},{3,17},{17,3},{19,1},{4,22},{6,... | collective-permute-start | bytes 1843208 | tf_op jit(solution)/shard_map/ppermute | solution.py:679
  218.6 13.3 %collective-permute-start.19 = (bf16[24,3072]{1,0:T(8,128)(2,1)S(1)}, bf16[24,3072]{1,0:T(8,128)(2,1)S(1)}, u32[]{:S(2)}, u32[]{:S(2)}) collective-permute-start(bf16[24,3072]{1,0:T(8,128)(2,1)S(1)} %get-tuple-element.168), channel_id=1, source_target_pairs={{0,4},{4,8},{8,12},{12,0},{1,5},{5,9},{9,13},{13,1},{2,6},{6,10},{... | collective-permute-start | bytes 442376 | tf_op jit(solution)/shard_map/ppermute | solution.py:683
  225.0 16.4 %collective-permute-start.20 = (bf16[24,3072]{1,0:T(8,128)(2,1)}, bf16[24,3072]{1,0:T(8,128)(2,1)}, u32[]{:S(2)}, u32[]{:S(2)}) collective-permute-start(bf16[24,3072]{1,0:T(8,128)(2,1)} %get-tuple-element.169), channel_id=1, source_target_pairs={{0,8},{4,12},{8,0},{12,4},{1,9},{5,13},{9,1},{13,5},{2,10},{6,14},... | collective-permute-start | bytes 442376 | tf_op jit(solution)/shard_map/ppermute | solution.py:683
  243.6 10.9 %collective-permute-start.22 = (bf16[24,3200]{1,0:T(8,128)(2,1)S(1)}, bf16[24,3200]{1,0:T(8,128)(2,1)S(1)}, u32[]{:S(2)}, u32[]{:S(2)}) collective-permute-start(bf16[24,3200]{1,0:T(8,128)(2,1)S(1)} %get-tuple-element.164), channel_id=1, source_target_pairs={{0,4},{4,8},{8,12},{12,0},{1,5},{5,9},{9,13},{13,1},{2,6},{6,10},{... | collective-permute-start | bytes 460808 | tf_op jit(solution)/shard_map/ppermute | solution.py:683
  249.5 9.7 %collective-permute-start.23 = (bf16[24,3200]{1,0:T(8,128)(2,1)S(1)}, bf16[24,3200]{1,0:T(8,128)(2,1)S(1)}, u32[]{:S(2)}, u32[]{:S(2)}) collective-permute-start(bf16[24,3200]{1,0:T(8,128)(2,1)S(1)} %get-tuple-element.163), channel_id=1, source_target_pairs={{0,8},{4,12},{8,0},{12,4},{1,9},{5,13},{9,1},{13,5},{2,10},{6,14},... | collective-permute-start | bytes 460808 | tf_op jit(solution)/shard_map/ppermute | solution.py:683
  249.5 9.7 %collective-permute-start.24 = (bf16[24,3200]{1,0:T(8,128)(2,1)S(1)}, bf16[24,3200]{1,0:T(8,128)(2,1)S(1)}, u32[]{:S(2)}, u32[]{:S(2)}) collective-permute-start(bf16[24,3200]{1,0:T(8,128)(2,1)S(1)} %get-tuple-element.162), channel_id=1, source_target_pairs={{0,12},{4,0},{8,4},{12,8},{1,13},{5,1},{9,5},{13,9},{2,14},{6,2},{... | collective-permute-start | bytes 460808 | tf_op jit(solution)/shard_map/ppermute | solution.py:683
  (16 other events, 175.6 us)
Sparse Core Ops, SparseCore 0:
  11.5 94.2 all-gather.1
  134.0 60.8 reduce-scatter.2
  206.1 26.8 reduce-scatter.4

commit v3 on v2

--- a/solution.py
+++ b/solution.py
@@ -691,7 +691,6 @@
         place = jnp.stack([self.dp, self.line, self.side, self.core]).astype(jnp.int32)
         pieces = here + there
 
-        wide = 5 * PAIR
 
         def kernel(place_ref, *refs):
             out_ref = refs[-1]
@@ -707,12 +706,11 @@
         count = dps * lines * sides * 2
         return pl.pallas_call(
             kernel,
-            grid=(columns // wide,),
             in_specs=[pl.BlockSpec(memory_space=pltpu.SMEM)]
-            + [pl.BlockSpec((lines, unit, wide), lambda i: (0, 0, i))] * len(pieces),
-            out_specs=pl.BlockSpec((count, unit, wide), lambda i: (0, 0, i)),
+            + [pl.BlockSpec(memory_space=pltpu.VMEM)] * len(pieces),
+            out_specs=pl.BlockSpec(memory_space=pltpu.VMEM),
             out_shape=like((count, unit, columns), mine.dtype),
-            compiler_params=pltpu.CompilerParams(vmem_limit_bytes=VMEM),
+            compiler_params=pltpu.CompilerParams(vmem_limit_bytes=8 * MIB),
             name="place",
         )(place, *pieces).reshape(-1, columns)
 

time: 268 us -> 266 us (level)
  waiting for transfers between devices: 57 us -> 66 us
  starting transfers between devices: 35 us -> 28.7 us
  Pallas kernels: 133 us -> 128 us
    ppermute x9, starting transfers between devices: 23.3 us -> 16.9 us  [to_line(): lax.ppermute(array, 'line', [(i, (i + shift) % count) for i in range(coun...]
    pallas_call x1, Pallas kernels: 6.54 us -> 1.8 us  [gather(): pl.pallas_call(kernel, in_specs=[pl.BlockSpec(memory_space=pltpu.SMEM)] +...]
    ppermute x10, waiting for transfers between devices: 35.9 us -> 39.2 us  [to_plane(): return lax.ppermute(array, ('dp', 'side'), pairs)]
  transfers between devices with their start and end apart: 28 -> 28, of which waited for: 9 -> 12; matrix products, arithmetic and copies ran while one was open for 9% -> 8% of each run, Pallas kernels for 38% -> 37%
where the time goes in v3:
time: 266 us; the launch traced here: 264 us
  Pallas kernels  128 us (48%)
  waiting for transfers between devices  66 us (25%)
  starting transfers between devices  28.7 us (11%)
  other arithmetic  21.2 us (8%)
  between operations  14 us (5%)
  local copies, waits for them, and re-layouts  6.25 us (2%)
    ppermute x10, waiting for transfers between devices, to_plane(): return lax.ppermute(array, ('dp', 'side'), pairs)  39.2 us
    pallas_call x1, Pallas kernels, attention_forward(): pl.pallas_call(attention_forward_kernel, grid=(seqs, GROUPS), in_specs=[r...  30.9 us
    pallas_call x1, Pallas kernels, ffn_forward(): pl.pallas_call(lambda *refs: ffn_forward_kernel(unit, *refs), grid=(2 * C...  27.8 us
    pallas_call x1, Pallas kernels, attention_backward(): pl.pallas_call(lambda *refs: attention_backward_kernel(unit, *refs), grid...  26.5 us
    ppermute x9, waiting for transfers between devices, to_line(): lax.ppermute(array, 'line', [(i, (i + shift) % count) for i in range(coun...  21.9 us
    pallas_call x1, Pallas kernels, ffn_backward(): pl.pallas_call(lambda *refs: ffn_backward_kernel(unit, *refs), grid=(CHUN...  21.6 us
    ppermute x9, starting transfers between devices, to_line(): lax.ppermute(array, 'line', [(i, (i + shift) % count) for i in range(coun...  16.9 us
    ppermute x10, starting transfers between devices, to_plane(): return lax.ppermute(array, ('dp', 'side'), pairs)  11.1 us
  transfers between devices with their start and end apart: 28, of which 12 were waited for; matrix products, arithmetic and copies ran while one was open for 8% of the time, Pallas kernels for 37%

profile of v3, /device:TPU:0, one launch (start us, length us, event | category | flops | bytes accessed | tf_op | source)
XLA Modules:
  0.0 264.3 jit_solution(9743451231848098825)
XLA Ops:
  9.2 3.1 %collective-permute-start = (bf16[24,3200]{1,0:T(8,128)(2,1)}, bf16[24,3200]{1,0:T(8,128)(2,1)S(1)}, u32[]{:S(2)}, u32[]{:S(2)}) collective-permute-start(bf16[24,3200]{1,0:T(8,128)(2,1)} %get-tuple-element.88.refs_0_), channel_id=1, source_target_pairs={{0,4},{4,8},{8,12},{12,0},{1,5},{5,9},{9,13},{13,1},{2,6},{6,10},{... | collective-permute-start | bytes 460808 | tf_op jit(solution)/shard_map/ppermute | solution.py:683
  12.3 2.6 collective-permute-start.1
  16.2 3.2 %collective-permute-done.refs_1_ = bf16[24,3200]{1,0:T(8,128)(2,1)S(1)} collective-permute-done((bf16[24,3200]{1,0:T(8,128)(2,1)}, bf16[24,3200]{1,0:T(8,128)(2,1)S(1)}, u32[]{:S(2)}, u32[]{:S(2)}) %collective-permute-start) | collective-permute-done | bytes 153632 | tf_op jit(solution)/shard_map/ppermute | solution.py:683
  19.4 5.7 %collective-permute-done.1.refs_2_ = bf16[24,3200]{1,0:T(8,128)(2,1)S(1)} collective-permute-done((bf16[24,3200]{1,0:T(8,128)(2,1)}, bf16[24,3200]{1,0:T(8,128)(2,1)S(1)}, u32[]{:S(2)}, u32[]{:S(2)}) %collective-permute-start.1) | collective-permute-done | bytes 153632 | tf_op jit(solution)/shard_map/ppermute | solution.py:683
  29.7 13.2 %collective-permute-done.3.refs_1_ = bf16[4,24,3200]{2,1,0:T(8,128)(2,1)S(1)} collective-permute-done((bf16[4,24,3200]{2,1,0:T(8,128)(2,1)S(1)}, bf16[4,24,3200]{2,1,0:T(8,128)(2,1)S(1)}, u32[]{:S(2)}, u32[]{:S(2)}) %collective-permute-start.3) | collective-permute-done | bytes 614432 | tf_op jit(solution)/shard_map/ppermute | solution.py:679
  43.0 6.9 %collective-permute-done.4.refs_2_ = bf16[4,24,3200]{2,1,0:T(8,128)(2,1)S(1)} collective-permute-done((bf16[4,24,3200]{2,1,0:T(8,128)(2,1)S(1)}, bf16[4,24,3200]{2,1,0:T(8,128)(2,1)S(1)}, u32[]{:S(2)}, u32[]{:S(2)}) %collective-permute-start.4) | collective-permute-done | bytes 614432 | tf_op jit(solution)/shard_map/ppermute | solution.py:679
  49.8 14.7 %collective-permute-done.5.refs_3_ = bf16[4,24,3200]{2,1,0:T(8,128)(2,1)S(1)} collective-permute-done((bf16[4,24,3200]{2,1,0:T(8,128)(2,1)S(1)}, bf16[4,24,3200]{2,1,0:T(8,128)(2,1)S(1)}, u32[]{:S(2)}, u32[]{:S(2)}) %collective-permute-start.5) | collective-permute-done | bytes 614432 | tf_op jit(solution)/shard_map/ppermute | solution.py:679
  68.5 2.1 copy-done
  72.1 30.9 %attention_forward.1 = (bf16[1024,2304]{1,0:T(8,128)(2,1)}, bf16[1024,768]{1,0:T(8,128)(2,1)}, bf16[2,3,4,512,512]{4,3,2,1,0:T(8,128)(2,1)}, bf16[2,768,512]{2,1...) custom-call(bf16[1024,768]{1,0:T(8,128)(2,1)} %bitcast.137, ...), custom_call_target="tpu_custom_call" | custom-call | flops 6442450944 | bytes 37748736 | tf_op jit(solution)/shard_map/attention_forward/pallas_call | solution.py:116
  103.1 2.7 %all-gather.2.cloned.1.call-done.refs_1_.refs_2_.refs_4_.refs_5_ = bf16[768,6144]{1,0:T(8,128)(2,1)} async-done(((bf16[24,6144]{1,0:T(8,128)(2,1)}), bf16[768,6144]{1,0:T(8,128)(2,1)}) %all-gather.2.cloned.1.call-update) | async-done | bytes 9437200 | tf_op jit(solution)/shard_map/all_gather | solution.py:848
  105.8 27.8 %ffn_forward.1 = (bf16[1024,3072]{1,0:T(8,128)(2,1)}, bf16[2,2,2,4,96,768]{5,4,3,2,1,0:T(8,128)(2,1)}, f32[8,768]{1,0:T(8,128)}, bf16[1024,768]{1,0:T(8,128)(2,1...) custom-call(bf16[1024,768]{1,0:T(8,128)(2,1)} %get-tuple-element.89.refs_0_, ...), custom_call_target="tpu_custom_call" | custom-call | flops 14495514624 | bytes 35651584 | tf_op jit(solution)/shard_map/ffn_forward/pallas_call | solution.py:404
  133.8 21.6 %ffn_backward.1 = (bf16[384,3072]{1,0:T(8,128)(2,1)}, bf16[384,3072]{1,0:T(8,128)(2,1)}, f32[1,3072]{1,0:T(1,128)}, f32[1024,768]{1,0:T(8,128)}) custom-call(s32[1]{0:T(128)} %bitcast.4.refs_0_, bf16[768,1024]{1,0:T(8,128)(2,1)} %get-tuple-element.95.refs_1_, bf16[1024,3072]{1,0:T(8,128)(2,1)} %get-tuple-element.96.refs_2_, ...), custom_call_target="tpu_custom_call" | custom-call | flops 14495514624 | bytes 31457280 | tf_op jit(solution)/shard_map/ffn_backward/pallas_call | solution.py:490
  155.7 8.7 %norm_backward.1 = (bf16[384,3200]{1,0:T(8,128)(2,1)}, bf16[384,3200]{1,0:T(8,128)(2,1)}, f32[8,768]{1,0:T(8,128)}, bf16[1024,768]{1,0:T(8,128)(2,1)}, bf16[1024,768]{1,0:T(8,128)(2,1)}) custom-call(s32[1]{0:T(128)} %bitcast.4.refs_0_, bf16[768,3200]{1,0:T(8,128)(2,1)} %bitcast.103, f32[8,768]{1,0:T(8,128)} %reshape.211.vec_ref.refs_4_.refs_2_, ...), custom_call_target="tpu_custom_call" | custom-call | flops 2415919104 | bytes 17825792 | tf_op jit(solution)/shard_map/norm_backward/pallas_call | solution.py:573
  164.4 2.2 add_convert_fusion.4
  168.3 2.2 add_convert_fusion.3
  171.5 26.5 %attention_backward.1 = (bf16[384,3200]{1,0:T(8,128)(2,1)}, bf16[384,3200]{1,0:T(8,128)(2,1)}, bf16[1024,2304]{1,0:T(8,128)(2,1)}, f32[8,768]{1,0:T(8,128)}) custom-call(s32[1]{0:T(128)} %bitcast.4.refs_0_, bf16[2,768,512]{2,1,0:T(8,128)(2,1)} %get-tuple-element.110.refs_1_, ...), custom_call_target="tpu_custom_call", output_to_operand_aliasing={{3}: (6, {}), {0}: (7, {}), {1}: (8, {})} | custom-call | flops 6845104128 | bytes 37748736 | tf_op jit(solution)/shard_map/attention_backward/pallas_call | solution.py:221
  205.9 3.9 %fusion.3 = (bf16[4,24,3200]{2,1,0:T(8,128)(2,1)}, bf16[4,24,3200]{2,1,0:T(8,128)(2,1)}, bf16[4,24,3200]{2,1,0:T(8,128)(2,1)}) fusion(bf16[2,4,2,24,3200]{4,3,2,1,0:T(8,128)(2,1)S(1)} %bitcast.110, s32[]{:T(128)S(6)} %select_n.89, s32[]{:T(128)S(6)} %select_n.88, bf16[2,4,2,24,3200]{4,3,2,1,0:T(8,128)(2,1)} %bitcast.107, s32[]{:T(128)S(6)} %select_n.90, ...), kind=kLoop, calls=%fused_computation.17 | loop fusion | flops 3686400 | bytes 5529616 | tf_op jit(solution)/shard_map/convert_element_type | solution.py:746
  218.4 3.0 %collective-permute-start.19 = (bf16[24,3072]{1,0:T(8,128)(2,1)S(1)}, bf16[24,3072]{1,0:T(8,128)(2,1)S(1)}, u32[]{:S(2)}, u32[]{:S(2)}) collective-permute-start(bf16[24,3072]{1,0:T(8,128)(2,1)S(1)} %get-tuple-element.168), channel_id=1, source_target_pairs={{0,4},{4,8},{8,12},{12,0},{1,5},{5,9},{9,13},{13,1},{2,6},{6,10},{... | collective-permute-start | bytes 442376 | tf_op jit(solution)/shard_map/ppermute | solution.py:683
  221.8 7.5 %collective-permute-done.19 = bf16[24,3072]{1,0:T(8,128)(2,1)S(1)} collective-permute-done((bf16[24,3072]{1,0:T(8,128)(2,1)S(1)}, bf16[24,3072]{1,0:T(8,128)(2,1)S(1)}, u32[]{:S(2)}, u32[]{:S(2)}) %collective-permute-start.19) | collective-permute-done | bytes 147488 | tf_op jit(solution)/shard_map/ppermute | solution.py:683
  230.1 8.2 %input_grad.1 = bf16[1024,768]{1,0:T(8,128)(2,1)} custom-call(bf16[1024,768]{1,0:T(8,128)(2,1)} %get-tuple-element.105.da_ref, bf16[1024,2304]{1,0:T(8,128)(2,1)} %get-tuple-element.129.dqkv_ref, bf16[768,3200]{1,0:T(8,128)(2,1)} %bitcast.104, bf16[768,3200]{1,0:T(8,128)(2,1)} %bitcast.105, bf16[768,3200]{1,0:T(8,128)(2,1)} %bitcast.106), custom_call_target="tpu_custom_call" | custom-call | flops 3623878656 | bytes 13631488 | tf_op jit(solution)/shard_map/input_grad/pallas_call | solution.py:259
  238.3 2.7 %collective-permute-done.18 = bf16[4,24,3200]{2,1,0:T(8,128)(2,1)} collective-permute-done((bf16[4,24,3200]{2,1,0:T(8,128)(2,1)}, bf16[4,24,3200]{2,1,0:T(8,128)(2,1)}, u32[]{:S(2)}, u32[]{:S(2)}) %collective-permute-start.18) | collective-permute-done | bytes 614432 | tf_op jit(solution)/shard_map/ppermute | solution.py:679
  243.2 3.4 %collective-permute-start.22 = (bf16[24,3200]{1,0:T(8,128)(2,1)S(1)}, bf16[24,3200]{1,0:T(8,128)(2,1)S(1)}, u32[]{:S(2)}, u32[]{:S(2)}) collective-permute-start(bf16[24,3200]{1,0:T(8,128)(2,1)S(1)} %get-tuple-element.164), channel_id=1, source_target_pairs={{0,4},{4,8},{8,12},{12,0},{1,5},{5,9},{9,13},{13,1},{2,6},{6,10},{... | collective-permute-start | bytes 460808 | tf_op jit(solution)/shard_map/ppermute | solution.py:683
  246.6 2.4 collective-permute-start.24
  251.8 5.2 %collective-permute-done.23.refs_2_ = bf16[24,3200]{1,0:T(8,128)(2,1)S(1)} collective-permute-done((bf16[24,3200]{1,0:T(8,128)(2,1)S(1)}, bf16[24,3200]{1,0:T(8,128)(2,1)S(1)}, u32[]{:S(2)}, u32[]{:S(2)}) %collective-permute-start.23) | collective-permute-done | bytes 153632 | tf_op jit(solution)/shard_map/ppermute | solution.py:683
  (90 shorter events, 39.7 us)
Async XLA Ops:
  7.2 98.6 %all-gather.2.cloned.1.call-start = ((), (), s32[]{:S(2)}) async-start(), calls=%async_computation.2 | async-start | bytes 9732096 | tf_op jit(solution)/shard_map/all_gather | solution.py:848
  9.2 190.0 %reduce-scatter.3.cloned.1.call-start = ((), (), s32[]{:S(2)}) async-start(), calls=%async_computation.3 | async-start | bytes 5308416 | tf_op jit(solution)/shard_map/reduce_scatter | solution.py:719
  9.2 10.2 %collective-permute-start = (bf16[24,3200]{1,0:T(8,128)(2,1)}, bf16[24,3200]{1,0:T(8,128)(2,1)S(1)}, u32[]{:S(2)}, u32[]{:S(2)}) collective-permute-start(bf16[24,3200]{1,0:T(8,128)(2,1)} %get-tuple-element.88.refs_0_), channel_id=1, source_target_pairs={{0,4},{4,8},{8,12},{12,0},{1,5},{5,9},{9,13},{13,1},{2,6},{6,10},{... | collective-permute-start | bytes 460808 | tf_op jit(solution)/shard_map/ppermute | solution.py:683
  12.3 12.9 %collective-permute-start.1 = (bf16[24,3200]{1,0:T(8,128)(2,1)}, bf16[24,3200]{1,0:T(8,128)(2,1)S(1)}, u32[]{:S(2)}, u32[]{:S(2)}) collective-permute-start(bf16[24,3200]{1,0:T(8,128)(2,1)} %get-tuple-element.88.refs_0_), channel_id=1, source_target_pairs={{0,8},{4,12},{8,0},{12,4},{1,9},{5,13},{9,1},{13,5},{2,10},{6,14},... | collective-permute-start | bytes 460808 | tf_op jit(solution)/shard_map/ppermute | solution.py:683
  14.9 10.3 %collective-permute-start.2 = (bf16[24,3200]{1,0:T(8,128)(2,1)}, bf16[24,3200]{1,0:T(8,128)(2,1)S(1)}, u32[]{:S(2)}, u32[]{:S(2)}) collective-permute-start(bf16[24,3200]{1,0:T(8,128)(2,1)} %get-tuple-element.88.refs_0_), channel_id=1, source_target_pairs={{0,12},{4,0},{8,4},{12,8},{1,13},{5,1},{9,5},{13,9},{2,14},{6,2},{... | collective-permute-start | bytes 460808 | tf_op jit(solution)/shard_map/ppermute | solution.py:683
  26.2 16.8 %collective-permute-start.3 = (bf16[4,24,3200]{2,1,0:T(8,128)(2,1)S(1)}, bf16[4,24,3200]{2,1,0:T(8,128)(2,1)S(1)}, u32[]{:S(2)}, u32[]{:S(2)}) collective-permute-start(bf16[4,24,3200]{2,1,0:T(8,128)(2,1)S(1)} %stack.21.refs_0_), channel_id=1, source_target_pairs={{0,2},{2,0},{16,18},{18,16},{1,3},{3,1},{17,19},{19,17},{4,6},{6,4... | collective-permute-start | bytes 1843208 | tf_op jit(solution)/shard_map/ppermute | solution.py:679
  27.7 22.1 %collective-permute-start.4 = (bf16[4,24,3200]{2,1,0:T(8,128)(2,1)S(1)}, bf16[4,24,3200]{2,1,0:T(8,128)(2,1)S(1)}, u32[]{:S(2)}, u32[]{:S(2)}) collective-permute-start(bf16[4,24,3200]{2,1,0:T(8,128)(2,1)S(1)} %stack.21.refs_0_), channel_id=1, source_target_pairs={{0,16},{2,18},{16,0},{18,2},{1,17},{3,19},{17,1},{19,3},{4,20},{6,... | collective-permute-start | bytes 1843208 | tf_op jit(solution)/shard_map/ppermute | solution.py:679
  29.2 35.3 %collective-permute-start.5 = (bf16[4,24,3200]{2,1,0:T(8,128)(2,1)S(1)}, bf16[4,24,3200]{2,1,0:T(8,128)(2,1)S(1)}, u32[]{:S(2)}, u32[]{:S(2)}) collective-permute-start(bf16[4,24,3200]{2,1,0:T(8,128)(2,1)S(1)} %stack.21.refs_0_), channel_id=1, source_target_pairs={{0,18},{2,16},{16,2},{18,0},{1,19},{3,17},{17,3},{19,1},{4,22},{6,... | collective-permute-start | bytes 1843208 | tf_op jit(solution)/shard_map/ppermute | solution.py:679
  29.7 34.9 %collective-permute-start.6 = (bf16[4,24,3200]{2,1,0:T(8,128)(2,1)S(1)}, bf16[4,24,3200]{2,1,0:T(8,128)(2,1)S(1)}, u32[]{:S(2)}, u32[]{:S(2)}) collective-permute-start(bf16[4,24,3200]{2,1,0:T(8,128)(2,1)S(1)} %stack.21.refs_0_), channel_id=1, source_target_pairs={{0,1},{1,0},{2,3},{3,2},{4,5},{5,4},{6,7},{7,6},{8,9},{9,8},{10,11... | collective-permute-start | bytes 1843208 | tf_op jit(solution)/shard_map/ppermute | solution.py:670
  43.0 21.6 %collective-permute-start.7 = (bf16[4,24,3200]{2,1,0:T(8,128)(2,1)S(1)}, bf16[4,24,3200]{2,1,0:T(8,128)(2,1)}, u32[]{:S(2)}, u32[]{:S(2)}) collective-permute-start(bf16[4,24,3200]{2,1,0:T(8,128)(2,1)S(1)} %collective-permute-done.3.refs_1_), channel_id=1, source_target_pairs={{0,1},{1,0},{2,3},{3,2},{4,5},{5,4},{6,7},{7,6},{8,9},{9,8},{10,11... | collective-permute-start | bytes 1843208 | tf_op jit(solution)/shard_map/ppermute | solution.py:670
  49.8 14.8 %collective-permute-start.8 = (bf16[4,24,3200]{2,1,0:T(8,128)(2,1)S(1)}, bf16[4,24,3200]{2,1,0:T(8,128)(2,1)}, u32[]{:S(2)}, u32[]{:S(2)}) collective-permute-start(bf16[4,24,3200]{2,1,0:T(8,128)(2,1)S(1)} %collective-permute-done.4.refs_2_), channel_id=1, source_target_pairs={{0,1},{1,0},{2,3},{3,2},{4,5},{5,4},{6,7},{7,6},{8,9},{9,8},{10,11... | collective-permute-start | bytes 1843208 | tf_op jit(solution)/shard_map/ppermute | solution.py:670
  133.6 104.7 %reduce-scatter.5.cloned.1.call-start = ((), (), s32[]{:S(2)}) async-start(), calls=%async_computation.4 | async-start | bytes 737280 | tf_op jit(solution)/shard_map/reduce_scatter | solution.py:722
  155.4 9.0 %collective-permute-start.10 = (bf16[384,3072]{1,0:T(8,128)(2,1)}, bf16[384,3072]{1,0:T(8,128)(2,1)}, u32[]{:S(2)}, u32[]{:S(2)}) collective-permute-start(bf16[384,3072]{1,0:T(8,128)(2,1)} %get-tuple-element.102), channel_id=1, source_target_pairs={{0,1},{1,0},{2,3},{3,2},{4,5},{5,4},{6,7},{7,6},{8,9},{9,8},{10,11... | collective-permute-start | bytes 7077896 | tf_op jit(solution)/shard_map/ppermute | solution.py:670
  166.7 32.5 %collective-permute-start.11 = (bf16[2,4,1,24,1536]{4,3,1,2,0:T(8,128)(2,1)}, bf16[2,4,1,24,1536]{4,3,1,2,0:T(8,128)(2,1)S(1)}, u32[]{:S(2)}, u32[]{:S(2)}) collective-permute-start(bf16[2,4,1,24,1536]{4,3,1,2,0:T(8,128)(2,1)} %add_convert_fusion.4), channel_id=1, source_target_pairs={{0,2},{2,0},{16,18},{18,16},{1,3},{3,1},{17,19},{19,17},{4,6},{6,4... | collective-permute-start | bytes 1769480 | tf_op jit(solution)/shard_map/ppermute | solution.py:679
  170.5 28.6 %collective-permute-start.12 = (bf16[1,4,2,24,1536]{4,3,2,1,0:T(8,128)(2,1)}, bf16[1,4,2,24,1536]{4,3,2,1,0:T(8,128)(2,1)}, u32[]{:S(2)}, u32[]{:S(2)}) collective-permute-start(bf16[1,4,2,24,1536]{4,3,2,1,0:T(8,128)(2,1)} %add_convert_fusion.3), channel_id=1, source_target_pairs={{0,16},{2,18},{16,0},{18,2},{1,17},{3,19},{17,1},{19,3},{4,20},{6,... | collective-permute-start | bytes 1769480 | tf_op jit(solution)/shard_map/ppermute | solution.py:679
  201.8 11.5 %collective-permute-start.13 = (bf16[1,4,1,24,1536]{4,3,1,2,0:T(8,128)(2,1)}, bf16[1,4,1,24,1536]{4,3,1,2,0:T(8,128)(2,1)S(1)}, u32[]{:S(2)}, u32[]{:S(2)}) collective-permute-start(bf16[1,4,1,24,1536]{4,3,1,2,0:T(8,128)(2,1)} %add_convert_fusion.8), channel_id=1, source_target_pairs={{0,16},{2,18},{16,0},{18,2},{1,17},{3,19},{17,1},{19,3},{4,20},{6,... | collective-permute-start | bytes 884744 | tf_op jit(solution)/shard_map/ppermute | solution.py:679
  204.8 10.2 %collective-permute-start.14 = (bf16[1,4,1,24,1536]{4,3,2,1,0:T(8,128)(2,1)}, bf16[1,4,1,24,1536]{4,3,2,1,0:T(8,128)(2,1)}, u32[]{:S(2)}, u32[]{:S(2)}) collective-permute-start(bf16[1,4,1,24,1536]{4,3,2,1,0:T(8,128)(2,1)} %add_convert_fusion.7), channel_id=1, source_target_pairs={{0,2},{2,0},{16,18},{18,16},{1,3},{3,1},{17,19},{19,17},{4,6},{6,4... | collective-permute-start | bytes 884744 | tf_op jit(solution)/shard_map/ppermute | solution.py:679
  209.8 28.5 %collective-permute-start.16 = (bf16[4,24,3200]{2,1,0:T(8,128)(2,1)}, bf16[4,24,3200]{2,1,0:T(8,128)(2,1)S(1)}, u32[]{:S(2)}, u32[]{:S(2)}) collective-permute-start(bf16[4,24,3200]{2,1,0:T(8,128)(2,1)} %get-tuple-element.161), channel_id=1, source_target_pairs={{0,2},{2,0},{16,18},{18,16},{1,3},{3,1},{17,19},{19,17},{4,6},{6,4... | collective-permute-start | bytes 1843208 | tf_op jit(solution)/shard_map/ppermute | solution.py:679
  211.4 26.9 %collective-permute-start.17 = (bf16[4,24,3200]{2,1,0:T(8,128)(2,1)}, bf16[4,24,3200]{2,1,0:T(8,128)(2,1)}, u32[]{:S(2)}, u32[]{:S(2)}) collective-permute-start(bf16[4,24,3200]{2,1,0:T(8,128)(2,1)} %get-tuple-element.160), channel_id=1, source_target_pairs={{0,16},{2,18},{16,0},{18,2},{1,17},{3,19},{17,1},{19,3},{4,20},{6,... | collective-permute-start | bytes 1843208 | tf_op jit(solution)/shard_map/ppermute | solution.py:679
  212.4 28.6 %collective-permute-start.18 = (bf16[4,24,3200]{2,1,0:T(8,128)(2,1)}, bf16[4,24,3200]{2,1,0:T(8,128)(2,1)}, u32[]{:S(2)}, u32[]{:S(2)}) collective-permute-start(bf16[4,24,3200]{2,1,0:T(8,128)(2,1)} %get-tuple-element.159), channel_id=1, source_target_pairs={{0,18},{2,16},{16,2},{18,0},{1,19},{3,17},{17,3},{19,1},{4,22},{6,... | collective-permute-start | bytes 1843208 | tf_op jit(solution)/shard_map/ppermute | solution.py:679
  218.4 10.8 %collective-permute-start.19 = (bf16[24,3072]{1,0:T(8,128)(2,1)S(1)}, bf16[24,3072]{1,0:T(8,128)(2,1)S(1)}, u32[]{:S(2)}, u32[]{:S(2)}) collective-permute-start(bf16[24,3072]{1,0:T(8,128)(2,1)S(1)} %get-tuple-element.168), channel_id=1, source_target_pairs={{0,4},{4,8},{8,12},{12,0},{1,5},{5,9},{9,13},{13,1},{2,6},{6,10},{... | collective-permute-start | bytes 442376 | tf_op jit(solution)/shard_map/ppermute | solution.py:683
  221.5 16.8 %collective-permute-start.20 = (bf16[24,3072]{1,0:T(8,128)(2,1)}, bf16[24,3072]{1,0:T(8,128)(2,1)}, u32[]{:S(2)}, u32[]{:S(2)}) collective-permute-start(bf16[24,3072]{1,0:T(8,128)(2,1)} %get-tuple-element.169), channel_id=1, source_target_pairs={{0,8},{4,12},{8,0},{12,4},{1,9},{5,13},{9,1},{13,5},{2,10},{6,14},... | collective-permute-start | bytes 442376 | tf_op jit(solution)/shard_map/ppermute | solution.py:683
  246.6 10.4 %collective-permute-start.23 = (bf16[24,3200]{1,0:T(8,128)(2,1)S(1)}, bf16[24,3200]{1,0:T(8,128)(2,1)S(1)}, u32[]{:S(2)}, u32[]{:S(2)}) collective-permute-start(bf16[24,3200]{1,0:T(8,128)(2,1)S(1)} %get-tuple-element.163), channel_id=1, source_target_pairs={{0,8},{4,12},{8,0},{12,4},{1,9},{5,13},{9,1},{13,5},{2,10},{6,14},... | collective-permute-start | bytes 460808 | tf_op jit(solution)/shard_map/ppermute | solution.py:683
  246.6 10.4 %collective-permute-start.24 = (bf16[24,3200]{1,0:T(8,128)(2,1)S(1)}, bf16[24,3200]{1,0:T(8,128)(2,1)S(1)}, u32[]{:S(2)}, u32[]{:S(2)}) collective-permute-start(bf16[24,3200]{1,0:T(8,128)(2,1)S(1)} %get-tuple-element.162), channel_id=1, source_target_pairs={{0,12},{4,0},{8,4},{12,8},{1,13},{5,1},{9,5},{13,9},{2,14},{6,2},{... | collective-permute-start | bytes 460808 | tf_op jit(solution)/shard_map/ppermute | solution.py:683
  (12 other events, 88.3 us)
Sparse Core Ops, SparseCore 0:
  11.5 94.2 all-gather.1
  133.7 59.6 reduce-scatter.2
  205.3 24.5 reduce-scatter.4
